TPU v7x, 128 devices: a whole 4x4x4 slice. The times are simulated.
128 devices in a mesh: plane: 4 (over x_hi, core), ray: 32 (over z, y, x_lo).
Axes of the slice: x: 4 (x_hi: 2, x_lo: 2; x = x_hi * 2 + x_lo), y: 4, z: 4, core: 2. Of those that a mesh axis runs over, the one named last changes fastest.
Arguments:
- coarse_potential: float32 [2048, 512], P(('plane', 'ray')), may hold values from -72 to 72
- fine_tiles: bfloat16 [4, 32768, 256], P('plane', 'ray'), may hold values from -0.59765625 to 0.59765625
- tile_requests: int32 [128, 4, 32, 16], P(('plane', 'ray')), may hold values from 0 to 1023, as said below
- ray_slot: int32 [4, 131072], P(None, ('plane', 'ray')), may hold values from 0 to 511, as said below
- fine_cell: int32 [4, 131072], P(None, ('plane', 'ray')), may hold values from 17 to 221, as said below
- coarse_cell: int32 [4, 131072], P(None, ('plane', 'ray')), may hold values from 0 to 262143
- tile_root: int32 [4, 131072], P(None, ('plane', 'ray')), may hold values from 0 to 3
- ray_offset: float32 [2, 131072], P(None, ('plane', 'ray')), may hold values from 0 to 1
Outputs:
- displacement: float32 [2, 131072], P(None, ('plane', 'ray'))
- distortion: float32 [4, 131072], P(None, ('plane', 'ray'))
Inputs may be any that keep to these rules, and one draw needn't show every extreme that they name: `tile_requests`: entries are tile indices within one owner's tiles of the plane. `ray_slot`: A ray's slot r * 16 + s names a tile requested by its own bundle from owner r at that plane. `fine_cell`: both coordinates of a ray's fine cell lie in 1 to 13.
All inputs are finite; a program needn't handle non-finite values.
Results may differ from a plain program's by a relative error of at most 0.0026.
Values may be sent and summed in bfloat16 or wider, within the bound.
No kernel may reach another device: no remote copies, remote signals or barrier semaphores. Data moves between devices by JAX's collectives and lax.ppermute only.
A program may use at most 128 MiB of HBM per device.

v0:
```python
import jax
import jax.numpy as jnp
from jax import lax
from jax.sharding import PartitionSpec as P

TP = 16
RATIO = 32
FIRST = 31


def tile_fields(tiles):
    padded = jnp.pad(tiles, ((0, 0), (1, 1), (1, 1)))
    right_val = padded[:, 1:-1, 2:]
    left_val = padded[:, 1:-1, :-2]
    upper_val = padded[:, 2:, 1:-1]
    lower_val = padded[:, :-2, 1:-1]
    grad_x = (right_val - left_val) * 0.5
    grad_y = (upper_val - lower_val) * 0.5
    hess_xx = right_val - 2.0 * tiles + left_val
    hess_yy = upper_val - 2.0 * tiles + lower_val
    hess_xy = (
        padded[:, 2:, 2:] - padded[:, :-2, 2:] - padded[:, 2:, :-2] + padded[:, :-2, :-2]
    ) * 0.25
    return jnp.stack([grad_x, grad_y, hess_xx, hess_yy, hess_xy], axis=1)


def coarse_terms(plane_rows, coarse_row, fine_row, root_row, position, coarse_side):
    cell_x = coarse_row % coarse_side
    cell_y = coarse_row // coarse_side
    root_x = (root_row % 2 * (RATIO // 2)).astype(jnp.float32)
    root_y = (root_row // 2 * (RATIO // 2)).astype(jnp.float32)
    frac_x = (root_x + (fine_row % TP).astype(jnp.float32) + position[0]) / RATIO
    frac_y = (root_y + (fine_row // TP).astype(jnp.float32) + position[1]) / RATIO
    column_ids = jnp.arange(coarse_side, dtype=jnp.int32)[None, :]
    column_masks = [
        (column_ids == ((cell_x + shift_x) % coarse_side)[:, None]).astype(jnp.float32)
        for shift_x in range(-1, 3)
    ]
    grid_rows = []
    for shift_y in range(-1, 3):
        fetched = jnp.take(plane_rows, (cell_y + shift_y) % coarse_side, axis=0)
        grid_rows.append([jnp.sum(fetched * column_mask, axis=1) for column_mask in column_masks])
    weights = [
        (1.0 - frac_x) * (1.0 - frac_y),
        frac_x * (1.0 - frac_y),
        (1.0 - frac_x) * frac_y,
        frac_x * frac_y,
    ]
    total = jnp.zeros((5, coarse_row.shape[0]), jnp.float32)
    corner_list = ((0, 0), (0, 1), (1, 0), (1, 1))
    for corner_index in range(4):
        step_y = corner_list[corner_index][0] + 1
        step_x = corner_list[corner_index][1] + 1
        middle = grid_rows[step_y][step_x]
        right_val = grid_rows[step_y][step_x + 1]
        left_val = grid_rows[step_y][step_x - 1]
        upper_val = grid_rows[step_y + 1][step_x]
        lower_val = grid_rows[step_y - 1][step_x]
        cross = (
            grid_rows[step_y + 1][step_x + 1]
            - grid_rows[step_y - 1][step_x + 1]
            - grid_rows[step_y + 1][step_x - 1]
            + grid_rows[step_y - 1][step_x - 1]
        ) * 0.25
        stacked = jnp.stack(
            [
                (right_val - left_val) * 0.5,
                (upper_val - lower_val) * 0.5,
                right_val - 2.0 * middle + left_val,
                upper_val - 2.0 * middle + lower_val,
                cross,
            ]
        )
        total = total + weights[corner_index] * stacked
    scales = jnp.array(
        [
            1.0 / RATIO,
            1.0 / RATIO,
            1.0 / (RATIO * RATIO),
            1.0 / (RATIO * RATIO),
            1.0 / (RATIO * RATIO),
        ],
        jnp.float32,
    )
    return total * scales[:, None]


def advance(displacement, previous, distortion, before, deriv, plane_index):
    chi_now = float(FIRST + plane_index)
    ahead = 2.0 * chi_now / (chi_now + 1.0)
    behind = (chi_now - 1.0) / (chi_now + 1.0)
    strength = chi_now / (chi_now + 1.0)
    grad_x, grad_y, hess_xx, hess_yy, hess_xy = (deriv[0], deriv[1], deriv[2], deriv[3], deriv[4])
    new_disp = ahead * displacement - behind * previous - strength * jnp.stack([grad_x, grad_y])
    product = jnp.stack(
        [
            hess_xx * distortion[0] + hess_xy * distortion[2],
            hess_xx * distortion[1] + hess_xy * distortion[3],
            hess_xy * distortion[0] + hess_yy * distortion[2],
            hess_xy * distortion[1] + hess_yy * distortion[3],
        ]
    )
    new_dist = ahead * distortion - behind * before - strength * product
    return (new_disp, displacement, new_dist, distortion)


def fine_block(fields_flat, slot_row, cell_row, position):
    cand_count = fields_flat.shape[0]
    rows_here = slot_row.shape[0]
    tile_cells = TP * TP
    onehot = (slot_row[:, None] == jnp.arange(cand_count, dtype=jnp.int32)[None, :]).astype(
        jnp.bfloat16
    )
    picked = jnp.dot(onehot, fields_flat, preferred_element_type=jnp.float32).reshape(
        rows_here, 5, tile_cells
    )
    cell_ids = jnp.arange(tile_cells, dtype=jnp.int32)[None, :]
    along_x = position[0][:, None]
    along_y = position[1][:, None]
    anchor = cell_row[:, None]
    weights = (
        (1.0 - along_x) * (1.0 - along_y) * (cell_ids == anchor).astype(jnp.float32)
        + along_x * (1.0 - along_y) * (cell_ids == anchor + 1).astype(jnp.float32)
        + (1.0 - along_x) * along_y * (cell_ids == anchor + TP).astype(jnp.float32)
        + along_x * along_y * (cell_ids == anchor + TP + 1).astype(jnp.float32)
    )
    return jnp.einsum("bcn,bn->cb", picked, weights)


def body(
    coarse_potential,
    fine_tiles,
    tile_requests,
    ray_slot,
    fine_cell,
    coarse_cell,
    tile_root,
    ray_offset,
):
    planes = lax.axis_size("plane")
    owners = lax.axis_size("ray")
    slot_count = tile_requests.shape[3]
    coarse_side = coarse_potential.shape[1]
    count_rays = ray_offset.shape[1]
    tile_cells = TP * TP
    requests_local = tile_requests.reshape(planes, owners, slot_count)
    wanted_ids = lax.all_to_all(
        requests_local.reshape(planes * owners, slot_count),
        ("plane", "ray"),
        split_axis=0,
        concat_axis=0,
        tiled=True,
    )
    outgoing = jnp.take(fine_tiles[0], wanted_ids.reshape(-1), axis=0).reshape(
        planes, owners, slot_count, tile_cells
    )
    arrived = lax.all_to_all(
        outgoing.reshape(planes * owners, slot_count, tile_cells),
        ("plane", "ray"),
        split_axis=0,
        concat_axis=0,
        tiled=True,
    )
    arrived = arrived.reshape(planes, owners * slot_count, TP, TP)
    whole_rows = lax.all_gather(coarse_potential, ("plane", "ray"), axis=0, tiled=True)
    displacement = jnp.zeros((2, count_rays), jnp.float32)
    previous = displacement
    ones_row = jnp.ones((count_rays,), jnp.float32)
    zero_row = jnp.zeros((count_rays,), jnp.float32)
    distortion = jnp.stack([ones_row, zero_row, zero_row, ones_row])
    before = distortion
    block_rows = min(512, count_rays)
    block_total = count_rays // block_rows
    for plane_index in range(planes):
        position = ray_offset + displacement
        plane_rows = whole_rows[plane_index * coarse_side : (plane_index + 1) * coarse_side]
        coarse_part = coarse_terms(
            plane_rows,
            coarse_cell[plane_index],
            fine_cell[plane_index],
            tile_root[plane_index],
            position,
            coarse_side,
        )
        fields_flat = (
            tile_fields(arrived[plane_index].astype(jnp.float32))
            .astype(jnp.bfloat16)
            .reshape(-1, 5 * tile_cells)
        )

        def run_block(pieces):
            return fine_block(fields_flat, pieces[0], pieces[1], pieces[2])

        fine_blocks = lax.map(
            run_block,
            (
                ray_slot[plane_index].reshape(block_total, block_rows),
                fine_cell[plane_index].reshape(block_total, block_rows),
                position.reshape(2, block_total, block_rows).transpose(1, 0, 2),
            ),
        )
        fine_part = fine_blocks.transpose(1, 0, 2).reshape(5, count_rays)
        displacement, previous, distortion, before = advance(
            displacement, previous, distortion, before, fine_part + coarse_part, plane_index
        )
    return (displacement, distortion)


def solution(mesh):
    in_specs = (
        P(("plane", "ray"), None),
        P("plane", "ray", None),
        P(("plane", "ray"), None, None, None),
        P(None, ("plane", "ray")),
        P(None, ("plane", "ray")),
        P(None, ("plane", "ray")),
        P(None, ("plane", "ray")),
        P(None, ("plane", "ray")),
    )
    out_specs = (P(None, ("plane", "ray")), P(None, ("plane", "ray")))
    return jax.shard_map(body, mesh=mesh, in_specs=in_specs, out_specs=out_specs, check_vma=False)
```

profile of v0, /device:TPU:1, one launch (start us, length us, event | category | flops | bytes accessed | tf_op | source)
XLA Modules:
  0.0 516.9 jit_solution(14348921904441071178)
XLA Ops:
  8.7 11.5 %all-to-all-start = ((s32[128,1,16]{2,1,0:T(1,128)}), s32[128,1,16]{2,1,0:T(1,128)S(1)}, u32[]{:S(2)}, u32[]{:S(2)}) async-start(s32[128,1,16]{2,1,0:T(1,128)} %bitcast.38), calls=%async_computation | async-start | bytes 131072 | tf_op jit(solution)/shard_map/all_to_all | solution.py:147
  31.3 7.5 %gather_fusion = bf16[2048,256]{1,0:T(8,128)(2,1)S(1)} fusion(bf16[1024,256]{1,0:T(8,128)(2,1)S(1)} %bitcast.261, s32[2048]{0:T(1024)S(1)} %broadcast_clamp_fusion), kind=kCustom, calls=%fused_computation.16 | custom fusion | bytes 2105344 | tf_op jit(solution)/shard_map/jit(_take)/gather | solution.py:154
  40.1 9.5 %all-to-all-start.1 = ((bf16[128,16,256]{2,1,0:T(8,128)(2,1)}), bf16[128,16,256]{2,1,0:T(8,128)(2,1)S(1)}, u32[]{:S(2)}, u32[]{:S(2)}) async-start(bf16[128,16,256]{2,1,0:T(8,128)(2,1)} %broadcast_select_fusion), calls=%async_computation.1 | async-start | bytes 2097152 | tf_op jit(solution)/shard_map/all_to_all | solution.py:157
  52.3 17.2 %all-to-all-done.1 = bf16[128,16,256]{2,1,0:T(8,128)(2,1)S(1)} async-done(((bf16[128,16,256]{2,1,0:T(8,128)(2,1)}), bf16[128,16,256]{2,1,0:T(8,128)(2,1)S(1)}, u32[]{:S(2)}, u32[]{:S(2)}) %all-to-all-start.1) | async-done | bytes 1048608 | tf_op jit(solution)/shard_map/all_to_all | solution.py:157
  73.2 31.9 %fusion.47 = (bf16[512,1,16,16]{3,2,0,1:T(8,128)(2,1)S(1)}, bf16[512,1,16,16]{3,2,0,1:T(8,128)(2,1)}, bf16[512,1,16,16]{3,2,0,1:T(8,128)(2,1)}, bf16[512,1,16,16]{3,2,0,1:T(8,128)(2,1)}, bf16[512,1,16,16]{3,2,0,1:T(8,128)(2,1)}) fusion(f32[512,16,16]{2,1,0:T(8,128)} %reshape.2442), kind=kLoop, calls=%fused_computation.264 | loop fusion | flops 2359296 | bytes 1835008 | tf_op jit(solution)/shard_map/stack | solution.py:24
  130.2 32.4 %fusion.46 = (bf16[512,1,16,16]{3,2,0,1:T(8,128)(2,1)S(1)}, bf16[512,1,16,16]{3,2,0,1:T(8,128)(2,1)}, bf16[512,1,16,16]{3,2,0,1:T(8,128)(2,1)}, bf16[512,1,16,16]{3,2,0,1:T(8,128)(2,1)}, bf16[512,1,16,16]{3,2,0,1:T(8,128)(2,1)}) fusion(f32[512,16,16]{2,1,0:T(8,128)} %reshape.2443), kind=kLoop, calls=%fused_computation.263 | loop fusion | flops 2359296 | bytes 1835008 | tf_op jit(solution)/shard_map/stack | solution.py:24
  183.8 31.9 %fusion.45 = (bf16[512,1,16,16]{3,2,0,1:T(8,128)(2,1)S(1)}, bf16[512,1,16,16]{3,2,0,1:T(8,128)(2,1)}, bf16[512,1,16,16]{3,2,0,1:T(8,128)(2,1)}, bf16[512,1,16,16]{3,2,0,1:T(8,128)(2,1)}, bf16[512,1,16,16]{3,2,0,1:T(8,128)(2,1)}) fusion(f32[512,16,16]{2,1,0:T(8,128)} %reshape.2444), kind=kLoop, calls=%fused_computation.262 | loop fusion | flops 2359296 | bytes 1835008 | tf_op jit(solution)/shard_map/stack | solution.py:24
  234.9 31.9 %fusion.44 = (bf16[512,1,16,16]{3,2,0,1:T(8,128)(2,1)S(1)}, bf16[512,1,16,16]{3,2,0,1:T(8,128)(2,1)}, bf16[512,1,16,16]{3,2,0,1:T(8,128)(2,1)}, bf16[512,1,16,16]{3,2,0,1:T(8,128)(2,1)}, bf16[512,1,16,16]{3,2,0,1:T(8,128)(2,1)}) fusion(f32[512,16,16]{2,1,0:T(8,128)} %reshape.2445), kind=kLoop, calls=%fused_computation.261 | loop fusion | flops 2359296 | bytes 1835008 | tf_op jit(solution)/shard_map/stack | solution.py:24
  280.0 11.2 %while.48 = (s32[]{:T(128)}, f32[2,5,512]{2,1,0:T(8,128)S(1)}, s32[2,512]{1,0:T(2,128)S(1)}, f32[2,2,512]{2,1,0:T(2,128)S(1)}, s32[2,512]{1,0:T(2,128)S(1)}, /*i...) while((s32[]{:T(128)}, f32[2,5,512]{2,1,0:T(8,128)S(1)}, s32[2,512]{1,0:T(2,128)S(1)}, ...), condition=%wide.region_1.2_spmd, body=%wide.region_0.1_spmd.sunk | while | flops 674105344 | bytes 8749185 | solution.py:194
  291.2 39.6 %all-gather.2.cloned.1.call-done = f32[2048,512]{1,0:T(8,128)} async-done(((f32[16,512]{1,0:T(8,128)}), f32[2048,512]{1,0:T(8,128)}) %all-gather.2.cloned.1.call-update) | async-done | bytes 4194320 | tf_op jit(solution)/shard_map/all_gather | solution.py:165
  334.4 6.5 %gather_fusion.2 = f32[1024,512]{1,0:T(8,128)} fusion(f32[512,512]{1,0:T(8,128)} %get-tuple-element.600, s32[1024]{0:T(1024)S(1)} %get-tuple-element.791), kind=kCustom, calls=%fused_computation.1.clone | custom fusion | bytes 4198400 | tf_op jit(solution)/shard_map/jit(_take)/gather | solution.py:41
  341.0 6.5 %gather_fusion.3 = f32[1024,512]{1,0:T(8,128)} fusion(f32[512,512]{1,0:T(8,128)} %get-tuple-element.600, s32[1024]{0:T(1024)S(1)} %get-tuple-element.790), kind=kCustom, calls=%fused_computation.2.clone | custom fusion | bytes 4198400 | tf_op jit(solution)/shard_map/jit(_take)/gather | solution.py:41
  347.5 6.5 %gather_fusion.4 = f32[1024,512]{1,0:T(8,128)} fusion(f32[512,512]{1,0:T(8,128)} %get-tuple-element.600, s32[1024]{0:T(1024)S(1)} %get-tuple-element.789), kind=kCustom, calls=%fused_computation.3.clone | custom fusion | bytes 4198400 | tf_op jit(solution)/shard_map/jit(_take)/gather | solution.py:41
  354.0 6.5 %gather_fusion.1 = f32[1024,512]{1,0:T(8,128)} fusion(f32[512,512]{1,0:T(8,128)} %get-tuple-element.600, s32[1024]{0:T(1024)S(1)} %get-tuple-element.792), kind=kCustom, calls=%fused_computation.clone | custom fusion | bytes 4198400 | tf_op jit(solution)/shard_map/jit(_take)/gather | solution.py:41
  360.6 9.5 %select_reduce_fusion.56 = (f32[1024]{0:T(1024)S(1)}, f32[1024]{0:T(1024)S(1)}, f32[1024]{0:T(1024)S(1)}, f32[1024]{0:T(1024)S(1)}, f32[1024]{0:T(1024)S(1)}, /*...) fusion(f32[1024,512]{1,0:T(8,128)} %gather_fusion.2, ...), kind=kLoop, calls=%fused_computation.250 | loop fusion | flops 20955136 | bytes 8474624 | tf_op jit(solution)/shard_map/reduce_sum | solution.py:42
  371.9 19.3 %while.49 = (s32[]{:T(128)}, f32[2,5,512]{2,1,0:T(8,128)S(1)}, s32[2,512]{1,0:T(2,128)S(1)}, f32[2,2,512]{2,1,0:T(2,128)S(1)}, s32[2,512]{1,0:T(2,128)S(1)}, /*i...) while((s32[]{:T(128)}, f32[2,5,512]{2,1,0:T(8,128)S(1)}, s32[2,512]{1,0:T(2,128)S(1)}, ...), condition=%wide.region_19.21_spmd, body=%wide.region_18.20_spmd.sunk | while | flops 674105344 | bytes 8749185 | solution.py:194
  396.1 4.9 gather_fusion.7
  410.9 9.5 %select_reduce_fusion.40 = (f32[1024]{0:T(1024)S(1)}, f32[1024]{0:T(1024)S(1)}, f32[1024]{0:T(1024)S(1)}, f32[1024]{0:T(1024)S(1)}, f32[1024]{0:T(1024)S(1)}, /*...) fusion(f32[1024,512]{1,0:T(8,128)} %gather_fusion.6, ...), kind=kLoop, calls=%fused_computation.230 | loop fusion | flops 20955136 | bytes 8474624 | tf_op jit(solution)/shard_map/reduce_sum | solution.py:42
  421.5 14.0 %while.50 = (s32[]{:T(128)}, f32[2,5,512]{2,1,0:T(8,128)S(1)}, s32[2,512]{1,0:T(2,128)S(1)}, f32[2,2,512]{2,1,0:T(2,128)S(1)}, s32[2,512]{1,0:T(2,128)S(1)}, /*i...) while((s32[]{:T(128)}, f32[2,5,512]{2,1,0:T(8,128)S(1)}, s32[2,512]{1,0:T(2,128)S(1)}, ...), condition=%wide.region_37.39_spmd, body=%wide.region_36.38_spmd.sunk | while | flops 674105344 | bytes 8749185 | solution.py:194
  440.4 4.9 gather_fusion.11
  455.3 9.6 %select_reduce_fusion.24 = (f32[1024]{0:T(1024)S(1)}, f32[1024]{0:T(1024)S(1)}, f32[1024]{0:T(1024)S(1)}, f32[1024]{0:T(1024)S(1)}, f32[1024]{0:T(1024)S(1)}, /*...) fusion(f32[1024,512]{1,0:T(8,128)} %gather_fusion.10, ...), kind=kLoop, calls=%fused_computation.210 | loop fusion | flops 20955136 | bytes 8474624 | tf_op jit(solution)/shard_map/reduce_sum | solution.py:42
  467.3 12.5 %while.51 = (s32[]{:T(128)}, f32[2,5,512]{2,1,0:T(8,128)S(1)}, s32[2,512]{1,0:T(2,128)}, f32[2,2,512]{2,1,0:T(2,128)S(1)}, s32[2,512]{1,0:T(2,128)}, /*index=5*/...) while((s32[]{:T(128)}, f32[2,5,512]{2,1,0:T(8,128)S(1)}, s32[2,512]{1,0:T(2,128)}, ...), condition=%wide.region_55.57_spmd, body=%wide.region_54.56_spmd.sunk | while | flops 674105344 | bytes 8749185 | solution.py:194
  488.3 4.9 gather_fusion.16
  498.7 9.2 %select_reduce_fusion.8 = (f32[1024]{0:T(1024)S(1)}, f32[1024]{0:T(1024)S(1)}, f32[1024]{0:T(1024)S(1)}, f32[1024]{0:T(1024)S(1)}, f32[1024]{0:T(1024)S(1)}, /*i...) fusion(f32[1024,512]{1,0:T(8,128)S(1)} %gather_fusion.14, ...), kind=kLoop, calls=%fused_computation.190 | loop fusion | flops 20955136 | bytes 8474624 | tf_op jit(solution)/shard_map/reduce_sum | solution.py:42
  (318 shorter events, 208.5 us)
Async XLA Ops:
  7.2 24.1 %copy-start = (bf16[1,1024,256]{2,1,0:T(8,128)(2,1)S(1)}, bf16[1,1024,256]{2,1,0:T(8,128)(2,1)}, u32[]{:S(2)}) copy-start(bf16[1,1024,256]{2,1,0:T(8,128)(2,1)} %param.23) | copy-start | bytes 1572868
  8.7 21.1 %all-to-all-start = ((s32[128,1,16]{2,1,0:T(1,128)}), s32[128,1,16]{2,1,0:T(1,128)S(1)}, u32[]{:S(2)}, u32[]{:S(2)}) async-start(s32[128,1,16]{2,1,0:T(1,128)} %bitcast.38), calls=%async_computation | async-start | bytes 131072 | tf_op jit(solution)/shard_map/all_to_all | solution.py:147
  20.2 310.7 %all-gather.2.cloned.1.call-start = ((), (), s32[]{:S(2)}) async-start(), calls=%async_computation.2 | async-start | bytes 4227072 | tf_op jit(solution)/shard_map/all_gather | solution.py:165
  38.8 11.4 %copy-start.5 = (f32[2,1024]{1,0:T(2,128)S(1)}, f32[2,1024]{1,0:T(2,128)}, u32[]{:S(2)}) copy-start(f32[2,1024]{1,0:T(2,128)} %param.29) | copy-start | bytes 24580
  38.8 11.4 %copy-start.11 = (s32[4,1024]{1,0:T(4,128)S(1)}, s32[4,1024]{1,0:T(4,128)}, u32[]{:S(2)}) copy-start(s32[4,1024]{1,0:T(4,128)} %param.26) | copy-start | bytes 49156
  40.1 29.4 %all-to-all-start.1 = ((bf16[128,16,256]{2,1,0:T(8,128)(2,1)}), bf16[128,16,256]{2,1,0:T(8,128)(2,1)S(1)}, u32[]{:S(2)}, u32[]{:S(2)}) async-start(bf16[128,16,256]{2,1,0:T(8,128)(2,1)} %broadcast_select_fusion), calls=%async_computation.1 | async-start | bytes 2097152 | tf_op jit(solution)/shard_map/all_to_all | solution.py:157
  121.0 6.6 %copy-start.2 = (f32[32,16,256]{2,1,0:T(8,128)S(1)}, f32[32,16,256]{2,1,0:T(8,128)}, u32[]{:S(2)}) copy-start(f32[32,16,256]{2,1,0:T(8,128)} %get-tuple-element.623) | copy-start | bytes 1572868
  354.0 6.5 %copy-start.48 = (pred[1024]{0:T(1024)(128)(4,1)S(1)}, pred[1024]{0:T(1024)(128)(4,1)}, u32[]{:S(2)}) copy-start(pred[1024]{0:T(1024)(128)(4,1)} %get-tuple-element.551) | copy-start | bytes 3076
  354.0 6.5 %copy-start.49 = (pred[1024]{0:T(1024)(128)(4,1)S(1)}, pred[1024]{0:T(1024)(128)(4,1)}, u32[]{:S(2)}) copy-start(pred[1024]{0:T(1024)(128)(4,1)} %get-tuple-element.774) | copy-start | bytes 3076
  354.0 6.5 %copy-start.50 = (pred[1024]{0:T(1024)(128)(4,1)S(1)}, pred[1024]{0:T(1024)(128)(4,1)}, u32[]{:S(2)}) copy-start(pred[1024]{0:T(1024)(128)(4,1)} %get-tuple-element.775) | copy-start | bytes 3076
  354.0 6.5 %copy-start.51 = (pred[1024]{0:T(1024)(128)(4,1)S(1)}, pred[1024]{0:T(1024)(128)(4,1)}, u32[]{:S(2)}) copy-start(pred[1024]{0:T(1024)(128)(4,1)} %get-tuple-element.776) | copy-start | bytes 3076
  360.6 9.8 %copy-start.30 = (f32[1,1024]{1,0:T(1,128)S(1)}, f32[1,1024]{1,0:T(1,128)}, u32[]{:S(2)}) copy-start(f32[1,1024]{1,0:T(1,128)} %get-tuple-element.714) | copy-start | bytes 12292
  360.6 11.2 %copy-start.26 = (s32[4,1024]{1,0:T(4,128)S(1)}, s32[4,1024]{1,0:T(4,128)}, u32[]{:S(2)}) copy-start(s32[4,1024]{1,0:T(4,128)} %param.28) | copy-start | bytes 49156
  410.9 9.8 %copy-start.33 = (f32[5]{0:T(128)S(1)}, f32[5]{0:T(128)}, u32[]{:S(2)}) copy-start(f32[5]{0:T(128)} %constant.668.clone) | copy-start | bytes 64
  455.3 9.9 %copy-start.32 = (f32[1,1024]{1,0:T(1,128)S(1)}, f32[1,1024]{1,0:T(1,128)}, u32[]{:S(2)}) copy-start(f32[1,1024]{1,0:T(1,128)} %get-tuple-element.538) | copy-start | bytes 12292
  455.3 9.9 %copy-start.34 = (f32[5]{0:T(128)S(1)}, f32[5]{0:T(128)}, u32[]{:S(2)}) copy-start(f32[5]{0:T(128)} %constant.668.clone) | copy-start | bytes 64
  455.3 12.0 %copy-start.3 = (bf16[512,1280]{1,0:T(8,128)(2,1)S(1)}, bf16[512,1280]{1,0:T(8,128)(2,1)}, u32[]{:S(2)}) copy-start(bf16[512,1280]{1,0:T(8,128)(2,1)} %copy.85) | copy-start | bytes 3932164
  467.3 12.6 %copy-start.20 = (s32[1024]{0:T(1024)S(1)}, s32[1024]{0:T(1024)}, u32[]{:S(2)}) copy-start(s32[1024]{0:T(1024)} %get-tuple-element.738) | copy-start | bytes 12292
  493.3 5.2 %copy-start.13 = (s32[1024]{0:T(1024)S(1)}, s32[1024]{0:T(1024)}, u32[]{:S(2)}) copy-start(s32[1024]{0:T(1024)} %get-tuple-element.744) | copy-start | bytes 12292
  493.3 5.2 %copy-start.14 = (s32[1024]{0:T(1024)S(1)}, s32[1024]{0:T(1024)}, u32[]{:S(2)}) copy-start(s32[1024]{0:T(1024)} %get-tuple-element.745) | copy-start | bytes 12292
  498.6 9.5 %copy-start.31 = (f32[1,1024]{1,0:T(1,128)S(1)}, f32[1,1024]{1,0:T(1,128)}, u32[]{:S(2)}) copy-start(f32[1,1024]{1,0:T(1,128)} %get-tuple-element.531) | copy-start | bytes 12292
  498.6 9.5 %copy-start.35 = (f32[5]{0:T(128)S(1)}, f32[5]{0:T(128)}, u32[]{:S(2)}) copy-start(f32[5]{0:T(128)} %constant.668.clone) | copy-start | bytes 64
  498.7 9.6 %copy-start.12 = (f32[2,1024]{1,0:T(2,128)S(1)}, f32[2,1024]{1,0:T(2,128)}, u32[]{:S(2)}) copy-start(f32[2,1024]{1,0:T(2,128)} %get-tuple-element.537) | copy-start | bytes 24580
  498.7 10.9 %copy-start.1 = (bf16[1,1024,256]{2,1,0:T(8,128)(2,1)S(1)}, bf16[1,1024,256]{2,1,0:T(8,128)(2,1)}, u32[]{:S(2)}) copy-start(bf16[1,1024,256]{2,1,0:T(8,128)(2,1)} %param.23) | copy-start | bytes 1572868
  (31 other events, 153.1 us)
Sparse Core Ops, SparseCore 0:
  22.7 308.0 all-gather.1
where the time goes:
time: 527 us; the launch traced here: 517 us
  other arithmetic  206 us (39%)
  local copies, waits for them, and re-layouts  190 us (36%)
  waiting for transfers between devices  57.8 us (11%)
  matrix products  25.3 us (5%)
  starting transfers between devices  21.1 us (4%)
  between operations  15.5 us (3%)
    another operation x4, other arithmetic, tile_fields(): return jnp.stack([grad_x, grad_y, hess_xx, hess_yy, hess_xy], axis=1)  128 us
    gather x16, local copies, waits for them, and re-layouts, coarse_terms(): fetched = jnp.take(plane_rows, (cell_y + shift_y) % coarse_side, axis=0)  83.5 us
    another operation x24, local copies, waits for them, and re-layouts, tile_fields(): return jnp.stack([grad_x, grad_y, hess_xx, hess_yy, hess_xy], axis=1)  53.9 us
    all_gather x1, waiting for transfers between devices, body(): lax.all_gather(coarse_potential, ('plane', 'ray'), axis=0, tiled=True)  39.6 us
    reduce_sum x4, other arithmetic, coarse_terms(): jnp.sum(fetched * column_mask, axis=1)  37.7 us
    dot_general x8, matrix products, fine_block(): jnp.dot(onehot, fields_flat, preferred_element_type=jnp.float32)  25.3 us
    all_to_all x1, waiting for transfers between devices, body(): lax.all_to_all(outgoing.reshape(planes * owners, slot_count, tile_cells),...  17.2 us
    dot_general x8, other arithmetic, fine_block(): return jnp.einsum('bcn,bn->cb', picked, weights)  15.8 us
  transfers between devices with their start and end apart: 3, of which 3 were waited for; matrix products, arithmetic and copies ran while one was open for 47% of the time, Pallas kernels for 0%

commit v1 on v0

v1 whole, which is shorter than its diff:
```python
import jax
import jax.numpy as jnp
from jax import lax
from jax.experimental import pallas as pl
from jax.experimental.pallas import tpu as pltpu
from jax.sharding import PartitionSpec as P

TP = 16
RATIO = 32
FIRST = 31
LANES = 128
HALO = 8
WIN = 8
TALL = WIN + 3


def shift_rows(rows, amount, bits, keep):
    left = sum(bits)
    for bit in bits:
        left -= bit
        taken = (amount & bit) != 0
        need = keep + left
        rows = [
            jnp.where(taken, rows[j + bit], rows[j]) if j + bit < len(rows) else rows[j]
            for j in range(min(need, len(rows)))
        ]
    return rows


def shift_within(low, high, amount):
    index = lax.broadcasted_iota(jnp.int32, low.shape, 0)
    far = jnp.where(index < 4, pltpu.roll(low, 4, 0), pltpu.roll(high, 4, 0))
    here = jnp.where((amount & 4) != 0, far, low)
    here = jnp.where((amount & 2) != 0, pltpu.roll(here, 6, 0), here)
    return jnp.where((amount & 1) != 0, pltpu.roll(here, 7, 0), here)


def out_side(rows):
    side = 1
    while side * side < rows * LANES:
        side *= 2
    return side


def coarse_kernel(plane_ref, cell_ref, out_ref, table_ref):
    side = out_side(plane_ref.shape[0])
    windows = side // WIN
    chunks = side // LANES
    stride = chunks * WIN
    width = TALL * LANES
    step = 256
    count = windows * chunks
    for chunk in range(chunks):
        base = chunk * windows
        after = (chunk + 1) % chunks
        halo = jnp.zeros((windows, LANES), jnp.float32)
        lane = lax.broadcasted_iota(jnp.int32, (windows, LANES), 1)
        for dy in range(TALL):
            row = dy % WIN
            main = plane_ref[pl.ds(chunk * WIN + row, windows, stride=stride), :]
            near = plane_ref[pl.ds(after * WIN + row, windows, stride=stride), :]
            if dy >= WIN:
                main = pltpu.roll(main, windows - 1, 0)
                near = pltpu.roll(near, windows - 1, 0)
            near = pltpu.roll(near, dy * HALO, 1) if dy else near
            halo = jnp.where((lane >= dy * HALO) & (lane < (dy + 1) * HALO), near, halo)
            high = main.astype(jnp.bfloat16)
            low = (main - high.astype(jnp.float32)).astype(jnp.bfloat16)
            table_ref[pl.ds(base, windows), pl.ds(dy * LANES, LANES)] = high
            table_ref[pl.ds(count + base, windows), pl.ds(dy * LANES, LANES)] = low
        high = halo.astype(jnp.bfloat16)
        low = (halo - high.astype(jnp.float32)).astype(jnp.bfloat16)
        table_ref[pl.ds(base, windows), pl.ds(width, LANES)] = high
        table_ref[pl.ds(count + base, windows), pl.ds(width, LANES)] = low

    bundles = cell_ref.shape[0]
    per = cell_ref.shape[1] // step

    def one(index, carry):
        bundle = index // per
        start = pl.multiple_of((index % per) * step, step)
        cell = cell_ref[pl.ds(bundle, 1), pl.ds(start, step)]
        first_x = (cell - 1) & (side - 1)
        first_y = (cell // side - 1) & (side - 1)
        window = (first_x // LANES) * windows + first_y // WIN
        ids = lax.broadcasted_iota(jnp.int32, (count, step), 0)
        onehot = (ids == window).astype(jnp.float32).astype(jnp.bfloat16)
        onehot = jnp.concatenate([onehot, onehot], axis=0)
        picked = lax.dot_general(
            table_ref[...], onehot, (((0,), (0,)), ((), ())), preferred_element_type=jnp.float32
        )
        off_y = first_y & (WIN - 1)
        off_x = first_x & (LANES - 1)
        lines = []
        for dy in range(TALL):
            parts = [picked[dy * LANES + 8 * k : dy * LANES + 8 * k + 8] for k in range(LANES // 8)]
            parts.append(picked[width + dy * HALO : width + (dy + 1) * HALO])
            lines.append(shift_rows(parts, off_x // 8, (8, 4, 2, 1), 2))
        low = shift_rows([line[0] for line in lines], off_y, (4, 2, 1), 4)
        high = shift_rows([line[1] for line in lines], off_y, (4, 2, 1), 4)
        patch = [shift_within(low[i], high[i], off_x)[:4] for i in range(4)]
        out_ref[bundle, :, pl.ds(start, step)] = jnp.concatenate(patch, axis=0)
        return carry

    lax.fori_loop(0, bundles * per, one, 0)


def stencil_terms(patch, frac_x, frac_y):
    keep_y = 1.0 - frac_y
    level = keep_y * patch[1] + frac_y * patch[2]
    slope = (keep_y * (patch[2] - patch[0]) + frac_y * (patch[3] - patch[1])) * 0.5
    bend = keep_y * (patch[2] - 2.0 * patch[1] + patch[0]) + frac_y * (patch[3] - 2.0 * patch[2] + patch[1])
    keep_x = 1.0 - frac_x

    def across(rows):
        return [rows[k : k + 1] for k in range(4)]

    def flat(rows):
        return keep_x * rows[1] + frac_x * rows[2]

    def tilt(rows):
        return (keep_x * (rows[2] - rows[0]) + frac_x * (rows[3] - rows[1])) * 0.5

    def curve(rows):
        return keep_x * (rows[2] - 2.0 * rows[1] + rows[0]) + frac_x * (rows[3] - 2.0 * rows[2] + rows[1])

    level, slope, bend = across(level), across(slope), across(bend)
    return tilt(level), flat(slope), curve(level), flat(bend), tilt(slope)


def trace_kernel(tile_ref, slot_ref, fine_ref, root_ref, coarse_ref, offset_ref, disp_ref, dist_ref, patch_ref):
    planes = tile_ref.shape[0]
    slots = tile_ref.shape[1]
    rays = slot_ref.shape[1]
    step = 256

    def one(index, carry):
        plane = index // (rays // step)
        start = pl.multiple_of((index % (rays // step)) * step, step)
        slot = slot_ref[pl.ds(plane, 1), pl.ds(start, step)]
        cell = fine_ref[pl.ds(plane, 1), pl.ds(start, step)]
        ids = lax.broadcasted_iota(jnp.int32, (slots, step), 0)
        onehot = (ids == slot).astype(jnp.float32).astype(jnp.bfloat16)
        picked = lax.dot_general(
            tile_ref[plane], onehot, (((0,), (0,)), ((), ())), preferred_element_type=jnp.float32
        )
        off_x = cell % TP - 1
        off_y = cell // TP - 1
        low = shift_rows([picked[TP * y : TP * y + 8] for y in range(TP)], off_y, (8, 4, 2, 1), 4)
        high = shift_rows([picked[TP * y + 8 : TP * y + 16] for y in range(TP)], off_y, (8, 4, 2, 1), 4)
        for i in range(4):
            first = jnp.where(off_x >= 8, high[i], low[i])
            patch_ref[plane, i, :, pl.ds(start, step)] = shift_within(first, high[i], off_x)
        return carry

    lax.fori_loop(0, planes * (rays // step), one, 0)

    offset = [offset_ref[0:1], offset_ref[1:2]]
    disp = [jnp.zeros((1, rays), jnp.float32)] * 2
    last = disp
    zero = jnp.zeros((1, rays), jnp.float32)
    unit = jnp.ones((1, rays), jnp.float32)
    dist = [unit, zero, zero, unit]
    before = dist
    for plane in range(planes):
        chi = float(FIRST + plane)
        ahead = 2.0 * chi / (chi + 1.0)
        behind = (chi - 1.0) / (chi + 1.0)
        strength = chi / (chi + 1.0)
        position = [offset[0] + disp[0], offset[1] + disp[1]]
        fine = stencil_terms([patch_ref[plane, i] for i in range(4)], position[0], position[1])
        cell = fine_ref[plane : plane + 1]
        root = root_ref[plane : plane + 1]
        base_x = ((root % 2) * (RATIO // 2) + cell % TP).astype(jnp.float32)
        base_y = ((root // 2) * (RATIO // 2) + cell // TP).astype(jnp.float32)
        coarse = stencil_terms(
            [coarse_ref[plane, 4 * i : 4 * i + 4] for i in range(4)],
            (base_x + position[0]) * (1.0 / RATIO),
            (base_y + position[1]) * (1.0 / RATIO),
        )
        once = 1.0 / RATIO
        twice = once * once
        grad_x = fine[0] + coarse[0] * once
        grad_y = fine[1] + coarse[1] * once
        xx = fine[2] + coarse[2] * twice
        yy = fine[3] + coarse[3] * twice
        xy = fine[4] + coarse[4] * twice
        new_disp = [
            ahead * disp[0] - behind * last[0] - strength * grad_x,
            ahead * disp[1] - behind * last[1] - strength * grad_y,
        ]
        product = [
            xx * dist[0] + xy * dist[2],
            xx * dist[1] + xy * dist[3],
            xy * dist[0] + yy * dist[2],
            xy * dist[1] + yy * dist[3],
        ]
        new_dist = [ahead * dist[k] - behind * before[k] - strength * product[k] for k in range(4)]
        disp, last, dist, before = new_disp, disp, new_dist, dist
    for k in range(2):
        disp_ref[k : k + 1] = disp[k]
    for k in range(4):
        dist_ref[k : k + 1] = dist[k]


def swap(array, axes):
    return lax.all_to_all(array, axes, split_axis=0, concat_axis=0, tiled=True)


def body(
    coarse_potential,
    fine_tiles,
    tile_requests,
    ray_slot,
    fine_cell,
    coarse_cell,
    tile_root,
    ray_offset,
):
    planes = lax.axis_size("plane")
    owners = lax.axis_size("ray")
    slots = tile_requests.shape[3]
    side = coarse_potential.shape[1]
    rays = ray_offset.shape[1]
    cells = TP * TP
    wanted = swap(tile_requests.reshape(planes * owners, slots), ("plane", "ray"))

    chunks = side // LANES
    rows = coarse_potential.reshape(-1, WIN, chunks, LANES).transpose(0, 2, 1, 3).reshape(-1, LANES)
    rows = jnp.broadcast_to(rows[None], (owners,) + rows.shape)
    plane_rows = swap(rows, "ray").reshape(side * chunks, LANES)
    asked = swap(coarse_cell, "plane")
    found = pl.pallas_call(
        coarse_kernel,
        out_shape=jax.ShapeDtypeStruct((planes, 16, rays), jnp.float32),
        in_specs=[pl.BlockSpec(memory_space=pltpu.VMEM)] * 2,
        out_specs=pl.BlockSpec(memory_space=pltpu.VMEM),
        scratch_shapes=[pltpu.VMEM((2 * side // WIN * (side // LANES), (TALL + 1) * LANES), jnp.bfloat16)],
        compiler_params=pltpu.CompilerParams(vmem_limit_bytes=32 << 20),
        cost_estimate=pl.CostEstimate(flops=6_000_000_000, bytes_accessed=1_500_000, transcendentals=0),
        name="coarse",
    )(plane_rows, asked)
    coarse = swap(found, "plane")

    outgoing = fine_tiles[0].at[wanted.reshape(-1)].get(mode="promise_in_bounds")
    arrived = swap(outgoing.reshape(planes * owners, slots, cells), ("plane", "ray"))
    return pl.pallas_call(
        trace_kernel,
        out_shape=(
            jax.ShapeDtypeStruct((2, rays), jnp.float32),
            jax.ShapeDtypeStruct((4, rays), jnp.float32),
        ),
        in_specs=[pl.BlockSpec(memory_space=pltpu.VMEM)] * 6,
        out_specs=(pl.BlockSpec(memory_space=pltpu.VMEM),) * 2,
        scratch_shapes=[pltpu.VMEM((planes, 4, 8, rays), jnp.float32)],
        compiler_params=pltpu.CompilerParams(vmem_limit_bytes=32 << 20),
        cost_estimate=pl.CostEstimate(flops=1_500_000_000, bytes_accessed=1_500_000, transcendentals=0),
        name="trace",
    )(
        arrived.reshape(planes, owners * slots, cells),
        ray_slot,
        fine_cell,
        tile_root,
        coarse,
        ray_offset,
    )


def solution(mesh):
    in_specs = (
        P(("plane", "ray"), None),
        P("plane", "ray", None),
        P(("plane", "ray"), None, None, None),
        P(None, ("plane", "ray")),
        P(None, ("plane", "ray")),
        P(None, ("plane", "ray")),
        P(None, ("plane", "ray")),
        P(None, ("plane", "ray")),
    )
    out_specs = (P(None, ("plane", "ray")), P(None, ("plane", "ray")))
    return jax.shard_map(body, mesh=mesh, in_specs=in_specs, out_specs=out_specs, check_vma=False)
```

time: 527 us -> 94 us (0.18); the launches traced: 517 us -> 93.5 us
  other arithmetic: 206 us -> 0.82 us
  local copies, waits for them, and re-layouts: 190 us -> 12.4 us
  waiting for transfers between devices: 57.8 us -> 23 us
  matrix products: 25.3 us -> 0 us
  Pallas kernels: 0 us -> 18 us
  blocking collectives: 0 us -> 17.7 us
  between operations: 15.5 us -> 0.78 us
    another operation x4 -> x0, other arithmetic: 128 us -> none  [tile_fields(): return jnp.stack([grad_x, grad_y, hess_xx, hess_yy, hess_xy], axis=1)]
    gather x17 -> x1, local copies, waits for them, and re-layouts: 91 us -> 9.02 us  [body(): fine_tiles[0].at[wanted.reshape(-1)].get(mode='promise_in_bounds')]
    another operation x52 -> x0, local copies, waits for them, and re-layouts: 55.8 us -> none  [the longest x24 53.9 us: tile_fields(): return jnp.stack([grad_x, grad_y, hess_xx, hess_yy, hess_xy], axis=1)]
    all_gather x1 -> x0, waiting for transfers between devices: 39.6 us -> none  [body(): lax.all_gather(coarse_potential, ('plane', 'ray'), axis=0, tiled=True)]
    reduce_sum x4 -> x0, other arithmetic: 37.7 us -> none  [coarse_terms(): jnp.sum(fetched * column_mask, axis=1)]
    dot_general x8 -> x0, matrix products: 25.3 us -> none  [fine_block(): jnp.dot(onehot, fields_flat, preferred_element_type=jnp.float32)]
    pallas_call x0 -> x2, Pallas kernels: none -> 18 us  [the longest x1 12.1 us: body(): pl.pallas_call(coarse_kernel, out_shape=jax.ShapeDtypeStruct((planes, 16,...]
    all_to_all x0 -> x2, blocking collectives: none -> 17.7 us  [swap(): return lax.all_to_all(array, axes, split_axis=0, concat_axis=0, tiled=True)]
  transfers between devices with their start and end apart: 3 -> 3, of which waited for: 3 -> 3; matrix products, arithmetic and copies ran while one was open for 47% -> 11% of each run, Pallas kernels for 0% -> 13%
where the time goes in v1:
time: 94 us; the launch traced here: 93.5 us
  waiting for transfers between devices  23 us (24%)
  starting transfers between devices  20.9 us (22%)
  Pallas kernels  18 us (19%)
  blocking collectives  17.7 us (19%)
  local copies, waits for them, and re-layouts  12.4 us (13%)
    all_to_all x3, waiting for transfers between devices, swap(): return lax.all_to_all(array, axes, split_axis=0, concat_axis=0, tiled=True)  23 us
    all_to_all x3, starting transfers between devices, swap(): return lax.all_to_all(array, axes, split_axis=0, concat_axis=0, tiled=True)  20.9 us
    all_to_all x2, blocking collectives, swap(): return lax.all_to_all(array, axes, split_axis=0, concat_axis=0, tiled=True)  17.7 us
    pallas_call x1, Pallas kernels, body(): pl.pallas_call(coarse_kernel, out_shape=jax.ShapeDtypeStruct((planes, 16,...  12.1 us
    gather x1, local copies, waits for them, and re-layouts, body(): fine_tiles[0].at[wanted.reshape(-1)].get(mode='promise_in_bounds')  9.02 us
    pallas_call x1, Pallas kernels, body(): pl.pallas_call(trace_kernel, out_shape=(jax.ShapeDtypeStruct((2, rays), j...  5.83 us
    all_to_all x3, local copies, waits for them, and re-layouts, swap(): return lax.all_to_all(array, axes, split_axis=0, concat_axis=0, tiled=True)  2.05 us
  transfers between devices with their start and end apart: 3, of which 3 were waited for; matrix products, arithmetic and copies ran while one was open for 11% of the time, Pallas kernels for 13%

profile of v1, /device:TPU:1, one launch (start us, length us, event | category | flops | bytes accessed | tf_op | source)
XLA Modules:
  0.0 93.5 jit_solution(1259299744927663140)
XLA Ops:
  0.6 0.0 copy-start
  0.6 1.5 %copy.14 = s32[1,4,32,16]{3,2,1,0:T(8,128)} copy(s32[1,4,32,16]{2,3,1,0:T(8,128)} %param.10) | data formatting | bytes 16384 | tf_op jit(solution)/shard_map/all_to_all | solution.py:207
  2.2 11.5 %all-to-all-start = ((s32[128,1,16]{2,1,0:T(1,128)}), s32[128,1,16]{2,1,0:T(1,128)S(1)}, u32[]{:S(2)}, u32[]{:S(2)}) async-start(s32[128,1,16]{2,1,0:T(1,128)} %bitcast.1), calls=%async_computation | async-start | bytes 131072 | tf_op jit(solution)/shard_map/all_to_all | solution.py:207
  13.7 0.0 copy-done.6
  13.7 0.0 copy-start.5
  13.7 9.5 %all-to-all-done = s32[128,1,16]{2,1,0:T(1,128)S(1)} async-done(((s32[128,1,16]{2,1,0:T(1,128)}), s32[128,1,16]{2,1,0:T(1,128)S(1)}, u32[]{:S(2)}, u32[]{:S(2)}) %all-to-all-start) | async-done | bytes 8224 | tf_op jit(solution)/shard_map/all_to_all | solution.py:207
  23.2 7.8 %all_to_all.35 = s32[4,1,1024]{2,1,0:T(1,128)S(1)} all-to-all(s32[4,1,1024]{2,1,0:T(1,128)S(1)} %all_to_all.26), channel_id=1, replica_groups=mesh['plane'=4,'ray'=32] {'plane'}, dimensions={0} | all-to-all | bytes 32768 | tf_op jit(solution)/shard_map/all_to_all | solution.py:207
  31.0 1.1 %broadcast_in_dim.9 = f32[32,64,128]{2,1,0:T(8,128)} broadcast(f32[64,128]{1,0:T(8,128)S(1)} %bitcast.19), dimensions={1,2} | broadcast | bytes 1081344 | tf_op jit(solution)/shard_map/broadcast_in_dim | solution.py:230
  32.2 3.9 %all-to-all-start.2 = ((f32[32,64,128]{2,1,0:T(8,128)}), f32[32,64,128]{2,1,0:T(8,128)S(1)}, u32[]{:S(2)}, u32[]{:S(2)}) async-start(f32[32,64,128]{2,1,0:T(8,128)} %broadcast_in_dim.9), calls=%async_computation.2 | async-start | bytes 2097152 | tf_op jit(solution)/shard_map/all_to_all | solution.py:207
  36.1 0.5 broadcast.21
  36.6 0.8 reduce.3
  37.4 0.1 reshape.55
  37.6 9.0 %gather_fusion = bf16[2048,256]{1,0:T(8,128)(2,1)} fusion(bf16[1024,256]{1,0:T(8,128)(2,1)S(1)} %bitcast.14, s32[2048]{0:T(1024)S(1)} %broadcast_clamp_fusion), kind=kCustom, calls=%fused_computation | custom fusion | bytes 2105344 | tf_op jit(solution)/shard_map/gather | solution.py:245
  46.6 6.3 %all-to-all-done.2 = f32[32,64,128]{2,1,0:T(8,128)S(1)} async-done(((f32[32,64,128]{2,1,0:T(8,128)}), f32[32,64,128]{2,1,0:T(8,128)S(1)}, u32[]{:S(2)}, u32[]{:S(2)}) %all-to-all-start.2) | async-done | bytes 1048608 | tf_op jit(solution)/shard_map/all_to_all | solution.py:207
  52.9 5.5 %all-to-all-start.1 = ((bf16[128,16,256]{2,1,0:T(8,128)(2,1)}), bf16[128,16,256]{2,1,0:T(8,128)(2,1)S(1)}, u32[]{:S(2)}, u32[]{:S(2)}) async-start(bf16[128,16,256]{2,1,0:T(8,128)(2,1)} %bitcast.18), calls=%async_computation.1 | async-start | bytes 2097152 | tf_op jit(solution)/shard_map/all_to_all | solution.py:207
  58.4 12.1 %coarse.1 = f32[4,16,1024]{2,1,0:T(8,128)S(1)} custom-call(f32[2048,128]{1,0:T(8,128)S(1)} %bitcast.15, s32[4,1024]{1,0:T(4,128)S(1)} %bitcast.17), custom_call_target="tpu_custom_call" | custom-call | flops 6000000000 | bytes 1500000 | tf_op jit(solution)/shard_map/coarse/pallas_call | solution.py:233
  70.5 0.0 copy-start.1
  70.5 0.0 copy-start.2
  70.6 0.0 copy-start.3
  70.6 0.0 copy-start.4
  70.6 7.2 %all-to-all-done.1 = bf16[128,16,256]{2,1,0:T(8,128)(2,1)S(1)} async-done(((bf16[128,16,256]{2,1,0:T(8,128)(2,1)}), bf16[128,16,256]{2,1,0:T(8,128)(2,1)S(1)}, u32[]{:S(2)}, u32[]{:S(2)}) %all-to-all-start.1) | async-done | bytes 1048608 | tf_op jit(solution)/shard_map/all_to_all | solution.py:207
  77.8 9.9 %all_to_all.36.coarse_ref = f32[4,16,1024]{2,1,0:T(8,128)S(1)} all-to-all(f32[4,16,1024]{2,1,0:T(8,128)S(1)} %coarse.1), channel_id=1, replica_groups=mesh['plane'=4,'ray'=32] {'plane'}, dimensions={0} | all-to-all | bytes 524288 | tf_op jit(solution)/shard_map/all_to_all | solution.py:207
  87.7 0.0 copy-done.1
  87.7 5.8 %trace.1 = (f32[2,1024]{1,0:T(2,128)}, f32[4,1024]{1,0:T(4,128)}) custom-call(bf16[4,512,256]{2,1,0:T(8,128)(2,1)S(1)} %bitcast.16, s32[4,1024]{1,0:T(4,128)S(1)} %copy-done.1, s32[4,1024]{1,0:T(4,128)S(1)} %copy-done.2, s32[4,1024]{1,0:T(4,128)S(1)} %copy-done.3, f32[4,16,1024]{2,1,0:T(8,128)S(1)} %all_to_all.36.coarse_ref, f32[2,1024]{1,0:T(2,128)S(1)} %copy-done.4), custom_call_target="tpu_custom_call" | custom-call | flops 1500000000 | bytes 1500000 | tf_op jit(solution)/shard_map/trace/pallas_call | solution.py:247
  (10 shorter events, 0.0 us)
Async XLA Ops:
  0.6 36.9 %copy-start = (bf16[1,1024,256]{2,1,0:T(8,128)(2,1)S(1)}, bf16[1,1024,256]{2,1,0:T(8,128)(2,1)}, u32[]{:S(2)}) copy-start(bf16[1,1024,256]{2,1,0:T(8,128)(2,1)} %param.9) | copy-start | bytes 1572868
  2.2 11.5 %copy-start.6 = (s32[4,1024]{1,0:T(4,128)S(1)}, s32[4,1024]{1,0:T(4,128)}, u32[]{:S(2)}) copy-start(s32[4,1024]{1,0:T(4,128)} %param.13) | copy-start | bytes 49156
  2.2 21.1 %all-to-all-start = ((s32[128,1,16]{2,1,0:T(1,128)}), s32[128,1,16]{2,1,0:T(1,128)S(1)}, u32[]{:S(2)}, u32[]{:S(2)}) async-start(s32[128,1,16]{2,1,0:T(1,128)} %bitcast.1), calls=%async_computation | async-start | bytes 131072 | tf_op jit(solution)/shard_map/all_to_all | solution.py:207
  13.7 17.3 %copy-start.5 = (f32[16,512]{1,0:T(8,128)S(1)}, f32[16,512]{1,0:T(8,128)}, u32[]{:S(2)}) copy-start(f32[16,512]{1,0:T(8,128)} %param.8) | copy-start | bytes 98308
  32.2 20.7 %all-to-all-start.2 = ((f32[32,64,128]{2,1,0:T(8,128)}), f32[32,64,128]{2,1,0:T(8,128)S(1)}, u32[]{:S(2)}, u32[]{:S(2)}) async-start(f32[32,64,128]{2,1,0:T(8,128)} %broadcast_in_dim.9), calls=%async_computation.2 | async-start | bytes 2097152 | tf_op jit(solution)/shard_map/all_to_all | solution.py:207
  52.9 24.9 %all-to-all-start.1 = ((bf16[128,16,256]{2,1,0:T(8,128)(2,1)}), bf16[128,16,256]{2,1,0:T(8,128)(2,1)S(1)}, u32[]{:S(2)}, u32[]{:S(2)}) async-start(bf16[128,16,256]{2,1,0:T(8,128)(2,1)} %bitcast.18), calls=%async_computation.1 | async-start | bytes 2097152 | tf_op jit(solution)/shard_map/all_to_all | solution.py:207
  70.5 17.1 %copy-start.1 = (s32[4,1024]{1,0:T(4,128)S(1)}, s32[4,1024]{1,0:T(4,128)}, u32[]{:S(2)}) copy-start(s32[4,1024]{1,0:T(4,128)} %slot_ref.1) | copy-start | bytes 49156
  70.5 17.1 %copy-start.2 = (s32[4,1024]{1,0:T(4,128)S(1)}, s32[4,1024]{1,0:T(4,128)}, u32[]{:S(2)}) copy-start(s32[4,1024]{1,0:T(4,128)} %fine_ref.1) | copy-start | bytes 49156
  70.6 17.1 %copy-start.3 = (s32[4,1024]{1,0:T(4,128)S(1)}, s32[4,1024]{1,0:T(4,128)}, u32[]{:S(2)}) copy-start(s32[4,1024]{1,0:T(4,128)} %root_ref.1) | copy-start | bytes 49156
  70.6 17.1 %copy-start.4 = (f32[2,1024]{1,0:T(2,128)S(1)}, f32[2,1024]{1,0:T(2,128)}, u32[]{:S(2)}) copy-start(f32[2,1024]{1,0:T(2,128)} %offset_ref.1) | copy-start | bytes 24580

commit v2 on v1

--- a/solution.py
+++ b/solution.py
@@ -12,6 +12,7 @@
 HALO = 8
 WIN = 8
 TALL = WIN + 3
+UNIT = 72.0 / 32767.0
 
 
 def shift_rows(rows, amount, bits, keep):
@@ -35,43 +36,89 @@
     return jnp.where((amount & 1) != 0, pltpu.roll(here, 7, 0), here)
 
 
-def out_side(rows):
-    side = 1
-    while side * side < rows * LANES:
-        side *= 2
-    return side
-
-
-def coarse_kernel(plane_ref, cell_ref, out_ref, table_ref):
-    side = out_side(plane_ref.shape[0])
+def pack_kernel(coarse_ref, request_ref, out_ref, row_ref):
+    planes, owners, slots = request_ref.shape
+    side = coarse_ref.shape[1]
+    half = side // 2
+    code = jnp.floor(coarse_ref[...] * (1.0 / UNIT) + 0.5).astype(jnp.int32)
+    word = (code[:, :half] << 16) | (code[:, half:] & 0xFFFF)
+    tiles = []
+    for y in range(coarse_ref.shape[0] // WIN):
+        for x in range(half // LANES):
+            tiles.append(word[y * WIN : (y + 1) * WIN, x * LANES : (x + 1) * LANES])
+    block = jnp.concatenate(tiles, axis=0)
+    row_ref[...] = jnp.zeros_like(row_ref)
+    for plane in range(planes):
+        row_ref[:, plane * slots : (plane + 1) * slots] = request_ref[plane]
+    size = block.shape[0]
+    for owner in range(owners):
+        out_ref[owner, 0:size] = block
+        out_ref[owner, size : size + 8] = jnp.broadcast_to(row_ref[owner : owner + 1], (8, LANES))
+
+
+def take_kernel(plane_ref, own_ref, one_ref, two_ref, three_ref, tile_ref, out_ref, turned_ref):
+    planes, owners, slots, cells = out_ref.shape
+    plane = plane_ref[0]
+    count = tile_ref.shape[0]
+    group = 16
+    ids = lax.broadcasted_iota(jnp.int32, (slots, count), 1)
+    for k, ref in enumerate((own_ref, one_ref, two_ref, three_ref)):
+        turned_ref[...] = jnp.transpose(ref[...])
+        wanted = turned_ref[pl.ds(pl.multiple_of(plane * slots, slots), slots), :]
+        source = (plane + planes - k) & (planes - 1)
+        for first in range(0, owners, group):
+            onehot = jnp.concatenate(
+                [(ids == wanted[:, r : r + 1]).astype(jnp.float32).astype(jnp.bfloat16) for r in range(first, first + group)],
+                axis=0,
+            )
+            got = jnp.dot(onehot, tile_ref[...], preferred_element_type=jnp.float32).astype(jnp.bfloat16)
+            out_ref[source, pl.ds(first, group)] = got.reshape(group, slots, cells)
+
+
+def coarse_kernel(plane_ref, grid_ref, own_ref, one_ref, two_ref, three_ref, out_ref, table_ref, cell_ref):
+    owners, rows, _ = grid_ref.shape
+    plane = plane_ref[0]
+    side = owners * 2 * WIN
     windows = side // WIN
     chunks = side // LANES
-    stride = chunks * WIN
+    halves = chunks // 2
     width = TALL * LANES
     step = 256
     count = windows * chunks
+    grid = grid_ref.reshape(owners * rows, LANES)
+
+    def load(chunk, dy):
+        parts = []
+        for parity in range(2):
+            pick = (parity + dy // WIN) % 2
+            start = (pick * halves + chunk % halves) * WIN + dy % WIN
+            part = grid[pl.ds(start, owners, stride=rows), :]
+            if parity + dy // WIN >= 2:
+                part = pltpu.roll(part, owners - 1, 0)
+            parts.append(part)
+        word = jnp.concatenate(parts, axis=0)
+        return word >> 16 if chunk < halves else (word << 16) >> 16
+
+    def put(code, start, column):
+        high = ((code + 128) >> 8) << 8
+        table_ref[pl.ds(start, windows), pl.ds(column, LANES)] = high.astype(jnp.float32).astype(jnp.bfloat16)
+        table_ref[pl.ds(count + start, windows), pl.ds(column, LANES)] = (
+            (code - high).astype(jnp.float32).astype(jnp.bfloat16)
+        )
+
+    lane = lax.broadcasted_iota(jnp.int32, (windows, LANES), 1)
     for chunk in range(chunks):
         base = chunk * windows
-        after = (chunk + 1) % chunks
-        halo = jnp.zeros((windows, LANES), jnp.float32)
-        lane = lax.broadcasted_iota(jnp.int32, (windows, LANES), 1)
+        halo = jnp.zeros((windows, LANES), jnp.int32)
         for dy in range(TALL):
-            row = dy % WIN
-            main = plane_ref[pl.ds(chunk * WIN + row, windows, stride=stride), :]
-            near = plane_ref[pl.ds(after * WIN + row, windows, stride=stride), :]
-            if dy >= WIN:
-                main = pltpu.roll(main, windows - 1, 0)
-                near = pltpu.roll(near, windows - 1, 0)
+            near = load((chunk + 1) % chunks, dy)
             near = pltpu.roll(near, dy * HALO, 1) if dy else near
             halo = jnp.where((lane >= dy * HALO) & (lane < (dy + 1) * HALO), near, halo)
-            high = main.astype(jnp.bfloat16)
-            low = (main - high.astype(jnp.float32)).astype(jnp.bfloat16)
-            table_ref[pl.ds(base, windows), pl.ds(dy * LANES, LANES)] = high
-            table_ref[pl.ds(count + base, windows), pl.ds(dy * LANES, LANES)] = low
-        high = halo.astype(jnp.bfloat16)
-        low = (halo - high.astype(jnp.float32)).astype(jnp.bfloat16)
-        table_ref[pl.ds(base, windows), pl.ds(width, LANES)] = high
-        table_ref[pl.ds(count + base, windows), pl.ds(width, LANES)] = low
+            put(load(chunk, dy), base, dy * LANES)
+        put(halo, base, width)
+
+    for k, ref in enumerate((own_ref, one_ref, two_ref, three_ref)):
+        cell_ref[k : k + 1] = ref[pl.ds(plane, 1), :]
 
     bundles = cell_ref.shape[0]
     per = cell_ref.shape[1] // step
@@ -82,7 +129,8 @@
         cell = cell_ref[pl.ds(bundle, 1), pl.ds(start, step)]
         first_x = (cell - 1) & (side - 1)
         first_y = (cell // side - 1) & (side - 1)
-        window = (first_x // LANES) * windows + first_y // WIN
+        tall = first_y // WIN
+        window = (first_x // LANES) * windows + (tall & 1) * owners + tall // 2
         ids = lax.broadcasted_iota(jnp.int32, (count, step), 0)
         onehot = (ids == window).astype(jnp.float32).astype(jnp.bfloat16)
         onehot = jnp.concatenate([onehot, onehot], axis=0)
@@ -128,8 +176,13 @@
     return tilt(level), flat(slope), curve(level), flat(bend), tilt(slope)
 
 
-def trace_kernel(tile_ref, slot_ref, fine_ref, root_ref, coarse_ref, offset_ref, disp_ref, dist_ref, patch_ref):
+def trace_kernel(
+    plane_ref, tile_ref, slot_ref, fine_ref, root_ref, own_ref, one_ref, two_ref, three_ref, offset_ref,
+    disp_ref, dist_ref, patch_ref, coarse_ref
+):
     planes = tile_ref.shape[0]
+    for k, ref in enumerate((own_ref, one_ref, two_ref, three_ref)):
+        coarse_ref[(plane_ref[0] + k) & (planes - 1)] = ref[...]
     slots = tile_ref.shape[1]
     rays = slot_ref.shape[1]
     step = 256
@@ -178,8 +231,8 @@
             (base_x + position[0]) * (1.0 / RATIO),
             (base_y + position[1]) * (1.0 / RATIO),
         )
-        once = 1.0 / RATIO
-        twice = once * once
+        once = UNIT / RATIO
+        twice = UNIT / (RATIO * RATIO)
         grad_x = fine[0] + coarse[0] * once
         grad_y = fine[1] + coarse[1] * once
         xx = fine[2] + coarse[2] * twice
@@ -223,45 +276,76 @@
     side = coarse_potential.shape[1]
     rays = ray_offset.shape[1]
     cells = TP * TP
-    wanted = swap(tile_requests.reshape(planes * owners, slots), ("plane", "ray"))
-
-    chunks = side // LANES
-    rows = coarse_potential.reshape(-1, WIN, chunks, LANES).transpose(0, 2, 1, 3).reshape(-1, LANES)
-    rows = jnp.broadcast_to(rows[None], (owners,) + rows.shape)
-    plane_rows = swap(rows, "ray").reshape(side * chunks, LANES)
-    asked = swap(coarse_cell, "plane")
+    vmem = pl.BlockSpec(memory_space=pltpu.VMEM)
+    smem = pl.BlockSpec(memory_space=pltpu.SMEM)
+    plane = jnp.full((1,), lax.axis_index("plane"), jnp.int32)
+
+    def hop(array, by):
+        return lax.ppermute(array, "plane", [(i, (i + by) % planes) for i in range(planes)])
+
+    size = coarse_potential.shape[0] * side // 2 // LANES
+    message = pl.pallas_call(
+        pack_kernel,
+        out_shape=jax.ShapeDtypeStruct((owners, size + 8, LANES), jnp.int32),
+        in_specs=[vmem] * 2,
+        out_specs=vmem,
+        scratch_shapes=[pltpu.VMEM((owners, LANES), jnp.int32)],
+        name="pack",
+    )(coarse_potential, tile_requests.reshape(planes, owners, slots))
+    messages = swap(message, "ray")
+    cell_parts = [coarse_cell] + [hop(coarse_cell, k) for k in range(1, planes)]
+    asked = messages[:, size]
+    asked_parts = [asked] + [hop(asked, k) for k in range(1, planes)]
+
+    outgoing = pl.pallas_call(
+        take_kernel,
+        out_shape=jax.ShapeDtypeStruct((planes, owners, slots, cells), jnp.bfloat16),
+        in_specs=[smem] + [vmem] * 5,
+        out_specs=vmem,
+        scratch_shapes=[pltpu.VMEM((LANES, owners), jnp.int32)],
+        compiler_params=pltpu.CompilerParams(vmem_limit_bytes=32 << 20),
+        cost_estimate=pl.CostEstimate(flops=1_100_000_000, bytes_accessed=1_600_000, transcendentals=0),
+        name="take",
+    )(plane, *asked_parts, fine_tiles[0])
+    arrived = swap(outgoing.reshape(planes * owners, slots, cells), ("plane", "ray"))
+
     found = pl.pallas_call(
         coarse_kernel,
         out_shape=jax.ShapeDtypeStruct((planes, 16, rays), jnp.float32),
-        in_specs=[pl.BlockSpec(memory_space=pltpu.VMEM)] * 2,
-        out_specs=pl.BlockSpec(memory_space=pltpu.VMEM),
-        scratch_shapes=[pltpu.VMEM((2 * side // WIN * (side // LANES), (TALL + 1) * LANES), jnp.bfloat16)],
+        in_specs=[smem] + [vmem] * 5,
+        out_specs=vmem,
+        scratch_shapes=[
+            pltpu.VMEM((2 * side // WIN * (side // LANES), (TALL + 1) * LANES), jnp.bfloat16),
+            pltpu.VMEM((planes, rays), jnp.int32),
+        ],
         compiler_params=pltpu.CompilerParams(vmem_limit_bytes=32 << 20),
         cost_estimate=pl.CostEstimate(flops=6_000_000_000, bytes_accessed=1_500_000, transcendentals=0),
         name="coarse",
-    )(plane_rows, asked)
-    coarse = swap(found, "plane")
-
-    outgoing = fine_tiles[0].at[wanted.reshape(-1)].get(mode="promise_in_bounds")
-    arrived = swap(outgoing.reshape(planes * owners, slots, cells), ("plane", "ray"))
+    )(plane, messages, *cell_parts)
+    found_parts = [found[0]] + [hop(found[k], planes - k) for k in range(1, planes)]
+
     return pl.pallas_call(
         trace_kernel,
         out_shape=(
             jax.ShapeDtypeStruct((2, rays), jnp.float32),
             jax.ShapeDtypeStruct((4, rays), jnp.float32),
         ),
-        in_specs=[pl.BlockSpec(memory_space=pltpu.VMEM)] * 6,
-        out_specs=(pl.BlockSpec(memory_space=pltpu.VMEM),) * 2,
-        scratch_shapes=[pltpu.VMEM((planes, 4, 8, rays), jnp.float32)],
+        in_specs=[smem] + [vmem] * 9,
+        out_specs=(vmem,) * 2,
+        scratch_shapes=[
+            pltpu.VMEM((planes, 4, 8, rays), jnp.float32),
+            pltpu.VMEM((planes, 16, rays), jnp.float32),
+        ],
         compiler_params=pltpu.CompilerParams(vmem_limit_bytes=32 << 20),
         cost_estimate=pl.CostEstimate(flops=1_500_000_000, bytes_accessed=1_500_000, transcendentals=0),
         name="trace",
     )(
+        plane,
         arrived.reshape(planes, owners * slots, cells),
         ray_slot,
         fine_cell,
         tile_root,
-        coarse,
+        *found_parts,
         ray_offset,
     )
 

time: 94 us -> 83.5 us (0.89)
  local copies, waits for them, and re-layouts: 12.4 us -> 1.54 us
  waiting for transfers between devices: 23 us -> 17.1 us
  blocking collectives: 17.7 us -> 22.5 us
  Pallas kernels: 18 us -> 21.3 us
  starting transfers between devices: 20.9 us -> 19.9 us
    all_to_all x3 -> x1, waiting for transfers between devices: 23 us -> 0.01 us  [swap(): return lax.all_to_all(array, axes, split_axis=0, concat_axis=0, tiled=True)]
    ppermute x0 -> x9, waiting for transfers between devices: none -> 17.1 us  [hop(): lax.ppermute(array, 'plane', [(i, (i + by) % planes) for i in range(plane...]
    all_to_all x3 -> x1, starting transfers between devices: 20.9 us -> 6.39 us  [swap(): return lax.all_to_all(array, axes, split_axis=0, concat_axis=0, tiled=True)]
    ppermute x0 -> x9, starting transfers between devices: none -> 13.5 us  [hop(): lax.ppermute(array, 'plane', [(i, (i + by) % planes) for i in range(plane...]
    gather x1 -> x0, local copies, waits for them, and re-layouts: 9.02 us -> none  [body(): fine_tiles[0].at[wanted.reshape(-1)].get(mode='promise_in_bounds')]
    all_to_all x2 -> x1, blocking collectives: 17.7 us -> 22.5 us  [swap(): return lax.all_to_all(array, axes, split_axis=0, concat_axis=0, tiled=True)]
    pallas_call x0 -> x2, Pallas kernels: none -> 4.33 us  [the longest x1 2.54 us: body(): pl.pallas_call(take_kernel, out_shape=jax.ShapeDtypeStruct((planes, owner...]
    all_to_all x3 -> x0, local copies, waits for them, and re-layouts: 2.05 us -> none  [swap(): return lax.all_to_all(array, axes, split_axis=0, concat_axis=0, tiled=True)]
  transfers between devices with their start and end apart: 3 -> 10, of which waited for: 3 -> 6; matrix products, arithmetic and copies ran while one was open for 11% -> 0% of each run, Pallas kernels for 13% -> 13%
where the time goes in v2:
time: 83.5 us; the launch traced here: 83 us
  blocking collectives  22.5 us (27%)
  Pallas kernels  21.3 us (26%)
  starting transfers between devices  19.9 us (24%)
  waiting for transfers between devices  17.1 us (20%)
  local copies, waits for them, and re-layouts  1.54 us (2%)
    all_to_all x1, blocking collectives, swap(): return lax.all_to_all(array, axes, split_axis=0, concat_axis=0, tiled=True)  22.5 us
    ppermute x9, waiting for transfers between devices, hop(): lax.ppermute(array, 'plane', [(i, (i + by) % planes) for i in range(plane...  17.1 us
    ppermute x9, starting transfers between devices, hop(): lax.ppermute(array, 'plane', [(i, (i + by) % planes) for i in range(plane...  13.5 us
    pallas_call x1, Pallas kernels, body(): pl.pallas_call(coarse_kernel, out_shape=jax.ShapeDtypeStruct((planes, 16,...  11.1 us
    all_to_all x1, starting transfers between devices, swap(): return lax.all_to_all(array, axes, split_axis=0, concat_axis=0, tiled=True)  6.39 us
    pallas_call x1, Pallas kernels, body(): pl.pallas_call(trace_kernel, out_shape=(jax.ShapeDtypeStruct((2, rays), j...  5.83 us
    pallas_call x1, Pallas kernels, body(): pl.pallas_call(take_kernel, out_shape=jax.ShapeDtypeStruct((planes, owner...  2.54 us
    pallas_call x1, Pallas kernels, body(): pl.pallas_call(pack_kernel, out_shape=jax.ShapeDtypeStruct((owners, size...  1.79 us
  transfers between devices with their start and end apart: 10, of which 6 were waited for; matrix products, arithmetic and copies ran while one was open for 0% of the time, Pallas kernels for 13%

profile of v2, /device:TPU:1, one launch (start us, length us, event | category | flops | bytes accessed | tf_op | source)
XLA Modules:
  0.0 83.0 jit_solution(8121877229579915423)
XLA Ops:
  0.6 1.5 %copy.10 = s32[1,4,32,16]{3,2,1,0:T(8,128)} copy(s32[1,4,32,16]{2,3,1,0:T(8,128)} %param.10) | data formatting | bytes 16384 | tf_op args[2]
  2.1 1.8 %pack.1 = s32[32,40,128]{2,1,0:T(8,128)} custom-call(f32[16,512]{1,0:T(8,128)} %coarse_ref.1, s32[4,32,16]{2,1,0:T(8,128)} %bitcast.20), custom_call_target="tpu_custom_call" | custom-call | tf_op jit(solution)/shard_map/pack/pallas_call | solution.py:287
  3.9 22.5 %all_to_all.10.grid_ref = s32[32,40,128]{2,1,0:T(8,128)S(1)} all-to-all(s32[32,40,128]{2,1,0:T(8,128)} %pack.1), channel_id=1, replica_groups=mesh['plane'=4,'ray'=32] {'ray'}, dimensions={0} | all-to-all | bytes 1310720 | tf_op jit(solution)/shard_map/all_to_all | solution.py:260
  26.4 2.2 %collective-permute-start.2 = (s32[32,128]{1,0:T(8,128)S(1)}, s32[32,128]{1,0:T(8,128)S(1)}, u32[]{:S(2)}, u32[]{:S(2)}) collective-permute-start(s32[32,128]{1,0:T(8,128)S(1)} %bitcast.15), channel_id=1, source_target_pairs={{0,96},{32,0},{64,32},{96,64},{1,97},{33,1},{65,33},{97,65},{2,98}... | collective-permute-start | bytes 49160 | tf_op jit(solution)/shard_map/ppermute | solution.py:284
  28.5 2.5 %collective-permute-start.1 = (s32[32,128]{1,0:T(8,128)S(1)}, s32[32,128]{1,0:T(8,128)S(1)}, u32[]{:S(2)}, u32[]{:S(2)}) collective-permute-start(s32[32,128]{1,0:T(8,128)S(1)} %bitcast.16), channel_id=1, source_target_pairs={{0,64},{32,96},{64,0},{96,32},{1,65},{33,97},{65,1},{97,33},{2,66}... | collective-permute-start | bytes 49160 | tf_op jit(solution)/shard_map/ppermute | solution.py:284
  31.0 1.4 %collective-permute-start = (s32[32,128]{1,0:T(8,128)S(1)}, s32[32,128]{1,0:T(8,128)S(1)}, u32[]{:S(2)}, u32[]{:S(2)}) collective-permute-start(s32[32,128]{1,0:T(8,128)S(1)} %bitcast.17), channel_id=1, source_target_pairs={{0,32},{32,64},{64,96},{96,0},{1,33},{33,65},{65,97},{97,1},{2,34}... | collective-permute-start | bytes 49160 | tf_op jit(solution)/shard_map/ppermute | solution.py:284
  32.4 0.2 collective-permute-done.1.two_ref
  32.6 0.6 collective-permute-done.one_ref
  33.3 2.5 %take.1 = bf16[4,32,16,256]{3,2,1,0:T(8,128)(2,1)} custom-call(s32[1]{0:T(128)} %bitcast.plane_ref, s32[32,128]{1,0:T(8,128)S(1)} %bitcast.18, s32[32,128]{1,0:T(8,128)S(1)} %collective-permute-done.one_ref, s32[32,128]{1,0:T(8,128)S(1)} %collective-permute-done.1.two_ref, s32[32,128]{1,0:T(8,128)S(1)} %collective-permute-done.2.three_ref, ...), custom_call_target="tpu_custom_call" | custom-call | flops 1100000000 | bytes 1600000 | tf_op jit(solution)/shard_map/take/pallas_call | solution.py:300
  35.8 6.4 %all-to-all-start.1 = ((bf16[128,16,256]{2,1,0:T(8,128)(2,1)}), bf16[128,16,256]{2,1,0:T(8,128)(2,1)S(1)}, u32[]{:S(2)}, u32[]{:S(2)}) async-start(bf16[128,16,256]{2,1,0:T(8,128)(2,1)} %bitcast.4), calls=%async_computation.1 | async-start | bytes 2097152 | tf_op jit(solution)/shard_map/all_to_all | solution.py:260
  42.2 3.0 %collective-permute-start.4 = (s32[4,1024]{1,0:T(4,128)S(1)}, s32[4,1024]{1,0:T(4,128)S(1)}, u32[]{:S(2)}, u32[]{:S(2)}) collective-permute-start(s32[4,1024]{1,0:T(4,128)S(1)} %copy-done.1), channel_id=1, source_target_pairs={{0,64},{32,96},{64,0},{96,32},{1,65},{33,97},{65,1},{97,33},{2,66}... | collective-permute-start | bytes 49160 | tf_op jit(solution)/shard_map/ppermute | solution.py:284
  45.2 1.4 %collective-permute-start.3 = (s32[4,1024]{1,0:T(4,128)S(1)}, s32[4,1024]{1,0:T(4,128)S(1)}, u32[]{:S(2)}, u32[]{:S(2)}) collective-permute-start(s32[4,1024]{1,0:T(4,128)S(1)} %copy-done.1), channel_id=1, source_target_pairs={{0,32},{32,64},{64,96},{96,0},{1,33},{33,65},{65,97},{97,1},{2,34}... | collective-permute-start | bytes 49160 | tf_op jit(solution)/shard_map/ppermute | solution.py:284
  46.6 10.2 %collective-permute-done.4.two_ref = s32[4,1024]{1,0:T(4,128)S(1)} collective-permute-done((s32[4,1024]{1,0:T(4,128)S(1)}, s32[4,1024]{1,0:T(4,128)S(1)}, u32[]{:S(2)}, u32[]{:S(2)}) %collective-permute-start.4) | collective-permute-done | bytes 16416 | tf_op jit(solution)/shard_map/ppermute | solution.py:284
  56.8 0.8 collective-permute-done.5.three_ref
  57.6 11.1 %coarse.1 = f32[4,16,1024]{2,1,0:T(8,128)S(1)} custom-call(s32[1]{0:T(128)} %bitcast.plane_ref, s32[32,40,128]{2,1,0:T(8,128)S(1)} %all_to_all.10.grid_ref, s32[4,1024]{1,0:T(4,128)S(1)} %copy-done.1, s32[4,1024]{1,0:T(4,128)S(1)} %collective-permute-done.3.one_ref, s32[4,1024]{1,0:T(4,128)S(1)} %collective-permute-done.4.two_ref, ...), custom_call_target="tpu_custom_call" | custom-call | flops 6000000000 | bytes 1500000 | tf_op jit(solution)/shard_map/coarse/pallas_call | solution.py:312
  68.8 0.0 copy-start.2
  68.8 0.0 copy-start.3
  68.8 0.0 copy-start.4
  68.8 0.0 copy-start.5
  68.8 0.3 collective-permute-start.8
  69.1 2.9 %collective-permute-start.7 = (f32[16,1024]{1,0:T(8,128)S(1)}, f32[16,1024]{1,0:T(8,128)S(1)}, u32[]{:S(2)}, u32[]{:S(2)}) collective-permute-start(f32[16,1024]{1,0:T(8,128)S(1)} %get-tuple-element.3), channel_id=1, source_target_pairs={{0,64},{32,96},{64,0},{96,32},{1,65},{33,97},{65,1},{97,33},{2,66}... | collective-permute-start | bytes 196616 | tf_op jit(solution)/shard_map/ppermute | solution.py:284
  72.0 3.2 %collective-permute-done.7.two_ref = f32[16,1024]{1,0:T(8,128)S(1)} collective-permute-done((f32[16,1024]{1,0:T(8,128)S(1)}, f32[16,1024]{1,0:T(8,128)S(1)}, u32[]{:S(2)}, u32[]{:S(2)}) %collective-permute-start.7) | collective-permute-done | bytes 65568 | tf_op jit(solution)/shard_map/ppermute | solution.py:284
  75.2 2.0 %collective-permute-done.6.one_ref = f32[16,1024]{1,0:T(8,128)S(1)} collective-permute-done((f32[16,1024]{1,0:T(8,128)S(1)}, f32[16,1024]{1,0:T(8,128)S(1)}, u32[]{:S(2)}, u32[]{:S(2)}) %collective-permute-start.6) | collective-permute-done | bytes 65568 | tf_op jit(solution)/shard_map/ppermute | solution.py:284
  77.2 5.8 %trace.1 = (f32[2,1024]{1,0:T(2,128)}, f32[4,1024]{1,0:T(4,128)}) custom-call(s32[1]{0:T(128)} %bitcast.plane_ref, bf16[4,512,256]{2,1,0:T(8,128)(2,1)S(1)} %bitcast.14, s32[4,1024]{1,0:T(4,128)S(1)} %copy-done.2, s32[4,1024]{1,0:T(4,128)S(1)} %copy-done.3, s32[4,1024]{1,0:T(4,128)S(1)} %copy-done.4, f32[16,1024]{1,0:T(8,128)S(1)} %get-tuple-element.5.own_ref, ...), custom_call_target="tpu_custom_call" | custom-call | flops 1500000000 | bytes 1500000 | tf_op jit(solution)/shard_map/trace/pallas_call | solution.py:327
  (16 shorter events, 0.1 us)
Async XLA Ops:
  3.9 29.4 %copy-start = (bf16[1,1024,256]{2,1,0:T(8,128)(2,1)S(1)}, bf16[1,1024,256]{2,1,0:T(8,128)(2,1)}, u32[]{:S(2)}) copy-start(bf16[1,1024,256]{2,1,0:T(8,128)(2,1)} %param.9) | copy-start | bytes 1572868
  26.4 6.1 %collective-permute-start.2 = (s32[32,128]{1,0:T(8,128)S(1)}, s32[32,128]{1,0:T(8,128)S(1)}, u32[]{:S(2)}, u32[]{:S(2)}) collective-permute-start(s32[32,128]{1,0:T(8,128)S(1)} %bitcast.15), channel_id=1, source_target_pairs={{0,96},{32,0},{64,32},{96,64},{1,97},{33,1},{65,33},{97,65},{2,98}... | collective-permute-start | bytes 49160 | tf_op jit(solution)/shard_map/ppermute | solution.py:284
  28.5 4.1 %collective-permute-start.1 = (s32[32,128]{1,0:T(8,128)S(1)}, s32[32,128]{1,0:T(8,128)S(1)}, u32[]{:S(2)}, u32[]{:S(2)}) collective-permute-start(s32[32,128]{1,0:T(8,128)S(1)} %bitcast.16), channel_id=1, source_target_pairs={{0,64},{32,96},{64,0},{96,32},{1,65},{33,97},{65,1},{97,33},{2,66}... | collective-permute-start | bytes 49160 | tf_op jit(solution)/shard_map/ppermute | solution.py:284
  31.0 2.3 %collective-permute-start = (s32[32,128]{1,0:T(8,128)S(1)}, s32[32,128]{1,0:T(8,128)S(1)}, u32[]{:S(2)}, u32[]{:S(2)}) collective-permute-start(s32[32,128]{1,0:T(8,128)S(1)} %bitcast.17), channel_id=1, source_target_pairs={{0,32},{32,64},{64,96},{96,0},{1,33},{33,65},{65,97},{97,1},{2,34}... | collective-permute-start | bytes 49160 | tf_op jit(solution)/shard_map/ppermute | solution.py:284
  35.8 6.4 %copy-start.1 = (s32[4,1024]{1,0:T(4,128)S(1)}, s32[4,1024]{1,0:T(4,128)}, u32[]{:S(2)}) copy-start(s32[4,1024]{1,0:T(4,128)} %own_ref.1) | copy-start | bytes 49156
  35.8 41.4 %all-to-all-start.1 = ((bf16[128,16,256]{2,1,0:T(8,128)(2,1)}), bf16[128,16,256]{2,1,0:T(8,128)(2,1)S(1)}, u32[]{:S(2)}, u32[]{:S(2)}) async-start(bf16[128,16,256]{2,1,0:T(8,128)(2,1)} %bitcast.4), calls=%async_computation.1 | async-start | bytes 2097152 | tf_op jit(solution)/shard_map/all_to_all | solution.py:260
  42.2 14.6 %collective-permute-start.4 = (s32[4,1024]{1,0:T(4,128)S(1)}, s32[4,1024]{1,0:T(4,128)S(1)}, u32[]{:S(2)}, u32[]{:S(2)}) collective-permute-start(s32[4,1024]{1,0:T(4,128)S(1)} %copy-done.1), channel_id=1, source_target_pairs={{0,64},{32,96},{64,0},{96,32},{1,65},{33,97},{65,1},{97,33},{2,66}... | collective-permute-start | bytes 49160 | tf_op jit(solution)/shard_map/ppermute | solution.py:284
  45.2 11.6 %collective-permute-start.3 = (s32[4,1024]{1,0:T(4,128)S(1)}, s32[4,1024]{1,0:T(4,128)S(1)}, u32[]{:S(2)}, u32[]{:S(2)}) collective-permute-start(s32[4,1024]{1,0:T(4,128)S(1)} %copy-done.1), channel_id=1, source_target_pairs={{0,32},{32,64},{64,96},{96,0},{1,33},{33,65},{65,97},{97,1},{2,34}... | collective-permute-start | bytes 49160 | tf_op jit(solution)/shard_map/ppermute | solution.py:284
  46.6 11.1 %collective-permute-start.5 = (s32[4,1024]{1,0:T(4,128)S(1)}, s32[4,1024]{1,0:T(4,128)S(1)}, u32[]{:S(2)}, u32[]{:S(2)}) collective-permute-start(s32[4,1024]{1,0:T(4,128)S(1)} %copy-done.1), channel_id=1, source_target_pairs={{0,96},{32,0},{64,32},{96,64},{1,97},{33,1},{65,33},{97,65},{2,98}... | collective-permute-start | bytes 49160 | tf_op jit(solution)/shard_map/ppermute | solution.py:284
  68.8 8.4 %copy-start.2 = (s32[4,1024]{1,0:T(4,128)S(1)}, s32[4,1024]{1,0:T(4,128)}, u32[]{:S(2)}) copy-start(s32[4,1024]{1,0:T(4,128)} %slot_ref.1) | copy-start | bytes 49156
  68.8 8.4 %copy-start.3 = (s32[4,1024]{1,0:T(4,128)S(1)}, s32[4,1024]{1,0:T(4,128)}, u32[]{:S(2)}) copy-start(s32[4,1024]{1,0:T(4,128)} %fine_ref.1) | copy-start | bytes 49156
  68.8 8.4 %copy-start.4 = (s32[4,1024]{1,0:T(4,128)S(1)}, s32[4,1024]{1,0:T(4,128)}, u32[]{:S(2)}) copy-start(s32[4,1024]{1,0:T(4,128)} %root_ref.1) | copy-start | bytes 49156
  68.8 8.4 %copy-start.5 = (f32[2,1024]{1,0:T(2,128)S(1)}, f32[2,1024]{1,0:T(2,128)}, u32[]{:S(2)}) copy-start(f32[2,1024]{1,0:T(2,128)} %offset_ref.1) | copy-start | bytes 24580
  68.8 3.2 %collective-permute-start.8 = (f32[16,1024]{1,0:T(8,128)S(1)}, f32[16,1024]{1,0:T(8,128)S(1)}, u32[]{:S(2)}, u32[]{:S(2)}) collective-permute-start(f32[16,1024]{1,0:T(8,128)S(1)} %get-tuple-element.2), channel_id=1, source_target_pairs={{0,32},{32,64},{64,96},{96,0},{1,33},{33,65},{65,97},{97,1},{2,34}... | collective-permute-start | bytes 196616 | tf_op jit(solution)/shard_map/ppermute | solution.py:284
  69.1 6.1 %collective-permute-start.7 = (f32[16,1024]{1,0:T(8,128)S(1)}, f32[16,1024]{1,0:T(8,128)S(1)}, u32[]{:S(2)}, u32[]{:S(2)}) collective-permute-start(f32[16,1024]{1,0:T(8,128)S(1)} %get-tuple-element.3), channel_id=1, source_target_pairs={{0,64},{32,96},{64,0},{96,32},{1,65},{33,97},{65,1},{97,33},{2,66}... | collective-permute-start | bytes 196616 | tf_op jit(solution)/shard_map/ppermute | solution.py:284
  72.0 5.2 %collective-permute-start.6 = (f32[16,1024]{1,0:T(8,128)S(1)}, f32[16,1024]{1,0:T(8,128)S(1)}, u32[]{:S(2)}, u32[]{:S(2)}) collective-permute-start(f32[16,1024]{1,0:T(8,128)S(1)} %get-tuple-element.4), channel_id=1, source_target_pairs={{0,96},{32,0},{64,32},{96,64},{1,97},{33,1},{65,33},{97,65},{2,98}... | collective-permute-start | bytes 196616 | tf_op jit(solution)/shard_map/ppermute | solution.py:284

commit v3 on v2

--- a/solution.py
+++ b/solution.py
@@ -294,7 +294,7 @@
     )(coarse_potential, tile_requests.reshape(planes, owners, slots))
     messages = swap(message, "ray")
     cell_parts = [coarse_cell] + [hop(coarse_cell, k) for k in range(1, planes)]
-    asked = messages[:, size]
+    asked, *cell_parts = lax.optimization_barrier((messages[:, size], *cell_parts))
     asked_parts = [asked] + [hop(asked, k) for k in range(1, planes)]
 
     outgoing = pl.pallas_call(

time: 83.5 us -> 69.9 us (0.84)
  blocking collectives: 22.5 us -> 0 us
  starting transfers between devices: 19.9 us -> 31.5 us
  waiting for transfers between devices: 17.1 us -> 14.5 us
    all_to_all x1 -> x0, blocking collectives: 22.5 us -> none  [swap(): return lax.all_to_all(array, axes, split_axis=0, concat_axis=0, tiled=True)]
    ppermute x9, waiting for transfers between devices: 17.1 us -> 6.07 us  [hop(): lax.ppermute(array, 'plane', [(i, (i + by) % planes) for i in range(plane...]
    all_to_all x1 -> x2, starting transfers between devices: 6.39 us -> 17.3 us  [swap(): return lax.all_to_all(array, axes, split_axis=0, concat_axis=0, tiled=True)]
    all_to_all x1 -> x2, waiting for transfers between devices: 0.01 us -> 8.39 us  [swap(): return lax.all_to_all(array, axes, split_axis=0, concat_axis=0, tiled=True)]
  transfers between devices with their start and end apart: 10 -> 11, of which waited for: 6 -> 7; matrix products, arithmetic and copies ran while one was open for 0% -> 0% of each run, Pallas kernels for 13% -> 16%
where the time goes in v3:
time: 69.9 us; the launch traced here: 69.5 us
  starting transfers between devices  31.5 us (45%)
  Pallas kernels  21.3 us (30%)
  waiting for transfers between devices  14.5 us (21%)
  local copies, waits for them, and re-layouts  1.54 us (2%)
  between operations  0.76 us (1%)
    all_to_all x2, starting transfers between devices, swap(): return lax.all_to_all(array, axes, split_axis=0, concat_axis=0, tiled=True)  17.3 us
    ppermute x9, starting transfers between devices, hop(): lax.ppermute(array, 'plane', [(i, (i + by) % planes) for i in range(plane...  14.2 us
    pallas_call x1, Pallas kernels, body(): pl.pallas_call(coarse_kernel, out_shape=jax.ShapeDtypeStruct((planes, 16,...  11.1 us
    all_to_all x2, waiting for transfers between devices, swap(): return lax.all_to_all(array, axes, split_axis=0, concat_axis=0, tiled=True)  8.39 us
    ppermute x9, waiting for transfers between devices, hop(): lax.ppermute(array, 'plane', [(i, (i + by) % planes) for i in range(plane...  6.07 us
    pallas_call x1, Pallas kernels, body(): pl.pallas_call(trace_kernel, out_shape=(jax.ShapeDtypeStruct((2, rays), j...  5.83 us
    pallas_call x1, Pallas kernels, body(): pl.pallas_call(take_kernel, out_shape=jax.ShapeDtypeStruct((planes, owner...  2.53 us
    pallas_call x1, Pallas kernels, body(): pl.pallas_call(pack_kernel, out_shape=jax.ShapeDtypeStruct((owners, size...  1.8 us
  transfers between devices with their start and end apart: 11, of which 7 were waited for; matrix products, arithmetic and copies ran while one was open for 0% of the time, Pallas kernels for 16%

profile of v3, /device:TPU:1, one launch (start us, length us, event | category | flops | bytes accessed | tf_op | source)
XLA Modules:
  0.0 69.5 jit_solution(915401825894572488)
XLA Ops:
  0.6 1.5 %copy.10 = s32[1,4,32,16]{3,2,1,0:T(8,128)} copy(s32[1,4,32,16]{2,3,1,0:T(8,128)} %param.10) | data formatting | bytes 16384 | tf_op args[2]
  2.1 1.8 %pack.1 = s32[32,40,128]{2,1,0:T(8,128)} custom-call(f32[16,512]{1,0:T(8,128)} %coarse_ref.1, s32[4,32,16]{2,1,0:T(8,128)} %bitcast.20), custom_call_target="tpu_custom_call" | custom-call | tf_op jit(solution)/shard_map/pack/pallas_call | solution.py:287
  3.9 9.9 %all-to-all-start = ((s32[32,40,128]{2,1,0:T(8,128)}), s32[32,40,128]{2,1,0:T(8,128)S(1)}, u32[]{:S(2)}, u32[]{:S(2)}) async-start(s32[32,40,128]{2,1,0:T(8,128)} %pack.1), calls=%async_computation | async-start | bytes 1310720 | tf_op jit(solution)/shard_map/all_to_all | solution.py:260
  13.9 2.5 %collective-permute-start.1 = (s32[4,1024]{1,0:T(4,128)S(1)}, s32[4,1024]{1,0:T(4,128)S(1)}, u32[]{:S(2)}, u32[]{:S(2)}) collective-permute-start(s32[4,1024]{1,0:T(4,128)S(1)} %copy-done.1), channel_id=1, source_target_pairs={{0,64},{32,96},{64,0},{96,32},{1,65},{33,97},{65,1},{97,33},{2,66}... | collective-permute-start | bytes 49160 | tf_op jit(solution)/shard_map/ppermute | solution.py:284
  16.4 1.6 %collective-permute-start = (s32[4,1024]{1,0:T(4,128)S(1)}, s32[4,1024]{1,0:T(4,128)S(1)}, u32[]{:S(2)}, u32[]{:S(2)}) collective-permute-start(s32[4,1024]{1,0:T(4,128)S(1)} %copy-done.1), channel_id=1, source_target_pairs={{0,32},{32,64},{64,96},{96,0},{1,33},{33,65},{65,97},{97,1},{2,34}... | collective-permute-start | bytes 49160 | tf_op jit(solution)/shard_map/ppermute | solution.py:284
  18.0 8.4 %all-to-all-done.grid_ref = s32[32,40,128]{2,1,0:T(8,128)S(1)} async-done(((s32[32,40,128]{2,1,0:T(8,128)}), s32[32,40,128]{2,1,0:T(8,128)S(1)}, u32[]{:S(2)}, u32[]{:S(2)}) %all-to-all-start) | async-done | bytes 655392 | tf_op jit(solution)/shard_map/all_to_all | solution.py:260
  26.5 2.5 %collective-permute-start.5 = (s32[32,128]{1,0:T(8,128)S(1)}, s32[32,128]{1,0:T(8,128)S(1)}, u32[]{:S(2)}, u32[]{:S(2)}) collective-permute-start(s32[32,128]{1,0:T(8,128)S(1)} %bitcast.15), channel_id=1, source_target_pairs={{0,96},{32,0},{64,32},{96,64},{1,97},{33,1},{65,33},{97,65},{2,98}... | collective-permute-start | bytes 49160 | tf_op jit(solution)/shard_map/ppermute | solution.py:284
  28.9 2.5 %collective-permute-start.4 = (s32[32,128]{1,0:T(8,128)S(1)}, s32[32,128]{1,0:T(8,128)S(1)}, u32[]{:S(2)}, u32[]{:S(2)}) collective-permute-start(s32[32,128]{1,0:T(8,128)S(1)} %bitcast.16), channel_id=1, source_target_pairs={{0,64},{32,96},{64,0},{96,32},{1,65},{33,97},{65,1},{97,33},{2,66}... | collective-permute-start | bytes 49160 | tf_op jit(solution)/shard_map/ppermute | solution.py:284
  31.4 1.1 %collective-permute-start.3 = (s32[32,128]{1,0:T(8,128)S(1)}, s32[32,128]{1,0:T(8,128)S(1)}, u32[]{:S(2)}, u32[]{:S(2)}) collective-permute-start(s32[32,128]{1,0:T(8,128)S(1)} %bitcast.17), channel_id=1, source_target_pairs={{0,32},{32,64},{64,96},{96,0},{1,33},{33,65},{65,97},{97,1},{2,34}... | collective-permute-start | bytes 49160 | tf_op jit(solution)/shard_map/ppermute | solution.py:284
  32.5 0.2 collective-permute-done.5.three_ref
  32.7 0.3 collective-permute-done.4.two_ref
  33.0 0.4 collective-permute-done.3.one_ref
  33.4 2.5 %take.1 = bf16[4,32,16,256]{3,2,1,0:T(8,128)(2,1)} custom-call(s32[1]{0:T(128)} %bitcast.plane_ref, s32[32,128]{1,0:T(8,128)S(1)} %bitcast.18, s32[32,128]{1,0:T(8,128)S(1)} %collective-permute-done.3.one_ref, s32[32,128]{1,0:T(8,128)S(1)} %collective-permute-done.4.two_ref, s32[32,128]{1,0:T(8,128)S(1)} %collective-permute-done.5.three_ref, ...), custom_call_target="tpu_custom_call" | custom-call | flops 1100000000 | bytes 1600000 | tf_op jit(solution)/shard_map/take/pallas_call | solution.py:300
  35.9 7.3 %all-to-all-start.1 = ((bf16[128,16,256]{2,1,0:T(8,128)(2,1)}), bf16[128,16,256]{2,1,0:T(8,128)(2,1)S(1)}, u32[]{:S(2)}, u32[]{:S(2)}) async-start(bf16[128,16,256]{2,1,0:T(8,128)(2,1)} %bitcast.4), calls=%async_computation.1 | async-start | bytes 2097152 | tf_op jit(solution)/shard_map/all_to_all | solution.py:260
  43.3 11.1 %coarse.1 = f32[4,16,1024]{2,1,0:T(8,128)S(1)} custom-call(s32[1]{0:T(128)} %bitcast.plane_ref, s32[32,40,128]{2,1,0:T(8,128)S(1)} %all-to-all-done.grid_ref, s32[4,1024]{1,0:T(4,128)S(1)} %copy-done.1, s32[4,1024]{1,0:T(4,128)S(1)} %collective-permute-done.one_ref, s32[4,1024]{1,0:T(4,128)S(1)} %collective-permute-done.1.two_ref, ...), custom_call_target="tpu_custom_call" | custom-call | flops 6000000000 | bytes 1500000 | tf_op jit(solution)/shard_map/coarse/pallas_call | solution.py:312
  54.4 0.0 copy-start.2
  54.4 0.0 copy-start.3
  54.4 0.0 copy-start.4
  54.4 3.2 %collective-permute-start.8 = (f32[16,1024]{1,0:T(8,128)S(1)}, f32[16,1024]{1,0:T(8,128)S(1)}, u32[]{:S(2)}, u32[]{:S(2)}) collective-permute-start(f32[16,1024]{1,0:T(8,128)S(1)} %get-tuple-element.12), channel_id=1, source_target_pairs={{0,32},{32,64},{64,96},{96,0},{1,33},{33,65},{65,97},{97,1},{2,34}... | collective-permute-start | bytes 196616 | tf_op jit(solution)/shard_map/ppermute | solution.py:284
  57.7 0.8 %collective-permute-start.7 = (f32[16,1024]{1,0:T(8,128)S(1)}, f32[16,1024]{1,0:T(8,128)S(1)}, u32[]{:S(2)}, u32[]{:S(2)}) collective-permute-start(f32[16,1024]{1,0:T(8,128)S(1)} %get-tuple-element.13), channel_id=1, source_target_pairs={{0,64},{32,96},{64,0},{96,32},{1,65},{33,97},{65,1},{97,33},{2,66}... | collective-permute-start | bytes 196616 | tf_op jit(solution)/shard_map/ppermute | solution.py:284
  58.4 0.5 collective-permute-done.8.three_ref
  59.0 3.6 %collective-permute-done.7.two_ref = f32[16,1024]{1,0:T(8,128)S(1)} collective-permute-done((f32[16,1024]{1,0:T(8,128)S(1)}, f32[16,1024]{1,0:T(8,128)S(1)}, u32[]{:S(2)}, u32[]{:S(2)}) %collective-permute-start.7) | collective-permute-done | bytes 65568 | tf_op jit(solution)/shard_map/ppermute | solution.py:284
  62.6 1.1 %collective-permute-done.6.one_ref = f32[16,1024]{1,0:T(8,128)S(1)} collective-permute-done((f32[16,1024]{1,0:T(8,128)S(1)}, f32[16,1024]{1,0:T(8,128)S(1)}, u32[]{:S(2)}, u32[]{:S(2)}) %collective-permute-start.6) | collective-permute-done | bytes 65568 | tf_op jit(solution)/shard_map/ppermute | solution.py:284
  63.7 5.8 %trace.1 = (f32[2,1024]{1,0:T(2,128)}, f32[4,1024]{1,0:T(4,128)}) custom-call(s32[1]{0:T(128)} %bitcast.plane_ref, bf16[4,512,256]{2,1,0:T(8,128)(2,1)S(1)} %bitcast.14, s32[4,1024]{1,0:T(4,128)S(1)} %copy-done.2, s32[4,1024]{1,0:T(4,128)S(1)} %copy-done.3, s32[4,1024]{1,0:T(4,128)S(1)} %copy-done.4, f32[16,1024]{1,0:T(8,128)S(1)} %get-tuple-element.15.own_ref, ...), custom_call_target="tpu_custom_call" | custom-call | flops 1500000000 | bytes 1500000 | tf_op jit(solution)/shard_map/trace/pallas_call | solution.py:327
  (17 shorter events, 0.1 us)
Async XLA Ops:
  3.9 10.0 %copy-start.1 = (s32[4,1024]{1,0:T(4,128)S(1)}, s32[4,1024]{1,0:T(4,128)}, u32[]{:S(2)}) copy-start(s32[4,1024]{1,0:T(4,128)} %own_ref) | copy-start | bytes 49156
  3.9 29.5 %copy-start = (bf16[1,1024,256]{2,1,0:T(8,128)(2,1)S(1)}, bf16[1,1024,256]{2,1,0:T(8,128)(2,1)}, u32[]{:S(2)}) copy-start(bf16[1,1024,256]{2,1,0:T(8,128)(2,1)} %param.9) | copy-start | bytes 1572868
  3.9 22.5 %all-to-all-start = ((s32[32,40,128]{2,1,0:T(8,128)}), s32[32,40,128]{2,1,0:T(8,128)S(1)}, u32[]{:S(2)}, u32[]{:S(2)}) async-start(s32[32,40,128]{2,1,0:T(8,128)} %pack.1), calls=%async_computation | async-start | bytes 1310720 | tf_op jit(solution)/shard_map/all_to_all | solution.py:260
  13.9 12.6 %collective-permute-start.1 = (s32[4,1024]{1,0:T(4,128)S(1)}, s32[4,1024]{1,0:T(4,128)S(1)}, u32[]{:S(2)}, u32[]{:S(2)}) collective-permute-start(s32[4,1024]{1,0:T(4,128)S(1)} %copy-done.1), channel_id=1, source_target_pairs={{0,64},{32,96},{64,0},{96,32},{1,65},{33,97},{65,1},{97,33},{2,66}... | collective-permute-start | bytes 49160 | tf_op jit(solution)/shard_map/ppermute | solution.py:284
  16.4 10.1 %collective-permute-start = (s32[4,1024]{1,0:T(4,128)S(1)}, s32[4,1024]{1,0:T(4,128)S(1)}, u32[]{:S(2)}, u32[]{:S(2)}) collective-permute-start(s32[4,1024]{1,0:T(4,128)S(1)} %copy-done.1), channel_id=1, source_target_pairs={{0,32},{32,64},{64,96},{96,0},{1,33},{33,65},{65,97},{97,1},{2,34}... | collective-permute-start | bytes 49160 | tf_op jit(solution)/shard_map/ppermute | solution.py:284
  18.0 8.4 %collective-permute-start.2 = (s32[4,1024]{1,0:T(4,128)S(1)}, s32[4,1024]{1,0:T(4,128)S(1)}, u32[]{:S(2)}, u32[]{:S(2)}) collective-permute-start(s32[4,1024]{1,0:T(4,128)S(1)} %copy-done.1), channel_id=1, source_target_pairs={{0,96},{32,0},{64,32},{96,64},{1,97},{33,1},{65,33},{97,65},{2,98}... | collective-permute-start | bytes 49160 | tf_op jit(solution)/shard_map/ppermute | solution.py:284
  26.5 6.2 %collective-permute-start.5 = (s32[32,128]{1,0:T(8,128)S(1)}, s32[32,128]{1,0:T(8,128)S(1)}, u32[]{:S(2)}, u32[]{:S(2)}) collective-permute-start(s32[32,128]{1,0:T(8,128)S(1)} %bitcast.15), channel_id=1, source_target_pairs={{0,96},{32,0},{64,32},{96,64},{1,97},{33,1},{65,33},{97,65},{2,98}... | collective-permute-start | bytes 49160 | tf_op jit(solution)/shard_map/ppermute | solution.py:284
  28.9 4.1 %collective-permute-start.4 = (s32[32,128]{1,0:T(8,128)S(1)}, s32[32,128]{1,0:T(8,128)S(1)}, u32[]{:S(2)}, u32[]{:S(2)}) collective-permute-start(s32[32,128]{1,0:T(8,128)S(1)} %bitcast.16), channel_id=1, source_target_pairs={{0,64},{32,96},{64,0},{96,32},{1,65},{33,97},{65,1},{97,33},{2,66}... | collective-permute-start | bytes 49160 | tf_op jit(solution)/shard_map/ppermute | solution.py:284
  31.4 2.0 %collective-permute-start.3 = (s32[32,128]{1,0:T(8,128)S(1)}, s32[32,128]{1,0:T(8,128)S(1)}, u32[]{:S(2)}, u32[]{:S(2)}) collective-permute-start(s32[32,128]{1,0:T(8,128)S(1)} %bitcast.17), channel_id=1, source_target_pairs={{0,32},{32,64},{64,96},{96,0},{1,33},{33,65},{65,97},{97,1},{2,34}... | collective-permute-start | bytes 49160 | tf_op jit(solution)/shard_map/ppermute | solution.py:284
  35.9 27.7 %all-to-all-start.1 = ((bf16[128,16,256]{2,1,0:T(8,128)(2,1)}), bf16[128,16,256]{2,1,0:T(8,128)(2,1)S(1)}, u32[]{:S(2)}, u32[]{:S(2)}) async-start(bf16[128,16,256]{2,1,0:T(8,128)(2,1)} %bitcast.4), calls=%async_computation.1 | async-start | bytes 2097152 | tf_op jit(solution)/shard_map/all_to_all | solution.py:260
  54.4 9.3 %copy-start.2 = (s32[4,1024]{1,0:T(4,128)S(1)}, s32[4,1024]{1,0:T(4,128)}, u32[]{:S(2)}) copy-start(s32[4,1024]{1,0:T(4,128)} %slot_ref.1) | copy-start | bytes 49156
  54.4 9.3 %copy-start.3 = (s32[4,1024]{1,0:T(4,128)S(1)}, s32[4,1024]{1,0:T(4,128)}, u32[]{:S(2)}) copy-start(s32[4,1024]{1,0:T(4,128)} %fine_ref.1) | copy-start | bytes 49156
  54.4 9.3 %copy-start.4 = (s32[4,1024]{1,0:T(4,128)S(1)}, s32[4,1024]{1,0:T(4,128)}, u32[]{:S(2)}) copy-start(s32[4,1024]{1,0:T(4,128)} %root_ref.1) | copy-start | bytes 49156
  54.4 9.2 %copy-start.5 = (f32[2,1024]{1,0:T(2,128)S(1)}, f32[2,1024]{1,0:T(2,128)}, u32[]{:S(2)}) copy-start(f32[2,1024]{1,0:T(2,128)} %offset_ref.1) | copy-start | bytes 24580
  54.4 4.5 %collective-permute-start.8 = (f32[16,1024]{1,0:T(8,128)S(1)}, f32[16,1024]{1,0:T(8,128)S(1)}, u32[]{:S(2)}, u32[]{:S(2)}) collective-permute-start(f32[16,1024]{1,0:T(8,128)S(1)} %get-tuple-element.12), channel_id=1, source_target_pairs={{0,32},{32,64},{64,96},{96,0},{1,33},{33,65},{65,97},{97,1},{2,34}... | collective-permute-start | bytes 196616 | tf_op jit(solution)/shard_map/ppermute | solution.py:284
  57.7 4.9 %collective-permute-start.7 = (f32[16,1024]{1,0:T(8,128)S(1)}, f32[16,1024]{1,0:T(8,128)S(1)}, u32[]{:S(2)}, u32[]{:S(2)}) collective-permute-start(f32[16,1024]{1,0:T(8,128)S(1)} %get-tuple-element.13), channel_id=1, source_target_pairs={{0,64},{32,96},{64,0},{96,32},{1,65},{33,97},{65,1},{97,33},{2,66}... | collective-permute-start | bytes 196616 | tf_op jit(solution)/shard_map/ppermute | solution.py:284
  58.4 5.2 %collective-permute-start.6 = (f32[16,1024]{1,0:T(8,128)S(1)}, f32[16,1024]{1,0:T(8,128)S(1)}, u32[]{:S(2)}, u32[]{:S(2)}) collective-permute-start(f32[16,1024]{1,0:T(8,128)S(1)} %get-tuple-element.14), channel_id=1, source_target_pairs={{0,96},{32,0},{64,32},{96,64},{1,97},{33,1},{65,33},{97,65},{2,98}... | collective-permute-start | bytes 196616 | tf_op jit(solution)/shard_map/ppermute | solution.py:284

commit v4 on v3

--- a/solution.py
+++ b/solution.py
@@ -8,6 +8,7 @@
 TP = 16
 RATIO = 32
 FIRST = 31
+PLANES = 4
 LANES = 128
 HALO = 8
 WIN = 8
@@ -36,8 +37,10 @@
     return jnp.where((amount & 1) != 0, pltpu.roll(here, 7, 0), here)
 
 
-def pack_kernel(coarse_ref, request_ref, out_ref, row_ref):
-    planes, owners, slots = request_ref.shape
+def pack_kernel(plane_ref, coarse_ref, own_ref, one_ref, two_ref, three_ref, out_ref, wish_ref, row_ref):
+    owners, rows, _ = out_ref.shape
+    planes = PLANES
+    slots = own_ref.shape[0] // planes
     side = coarse_ref.shape[1]
     half = side // 2
     code = jnp.floor(coarse_ref[...] * (1.0 / UNIT) + 0.5).astype(jnp.int32)
@@ -47,32 +50,40 @@
         for x in range(half // LANES):
             tiles.append(word[y * WIN : (y + 1) * WIN, x * LANES : (x + 1) * LANES])
     block = jnp.concatenate(tiles, axis=0)
-    row_ref[...] = jnp.zeros_like(row_ref)
-    for plane in range(planes):
-        row_ref[:, plane * slots : (plane + 1) * slots] = request_ref[plane]
-    size = block.shape[0]
+    plane = plane_ref[0]
+    wish_ref[...] = jnp.zeros_like(wish_ref)
+    for k, ref in enumerate((own_ref, one_ref, two_ref, three_ref)):
+        source = (plane + planes - k) & (planes - 1)
+        wish_ref[pl.ds(pl.multiple_of(source * slots, slots), slots), 0:owners] = ref[
+            pl.ds(pl.multiple_of(plane * slots, slots), slots), :
+        ]
+    row_ref[...] = jnp.transpose(wish_ref[...])
+    size = rows - 8
     for owner in range(owners):
         out_ref[owner, 0:size] = block
-        out_ref[owner, size : size + 8] = jnp.broadcast_to(row_ref[owner : owner + 1], (8, LANES))
-
-
-def take_kernel(plane_ref, own_ref, one_ref, two_ref, three_ref, tile_ref, out_ref, turned_ref):
+        out_ref[owner, size:rows] = jnp.broadcast_to(row_ref[owner : owner + 1], (8, LANES))
+
+
+def take_kernel(asked_ref, tile_ref, out_ref, turned_ref):
     planes, owners, slots, cells = out_ref.shape
-    plane = plane_ref[0]
     count = tile_ref.shape[0]
-    group = 16
-    ids = lax.broadcasted_iota(jnp.int32, (slots, count), 1)
-    for k, ref in enumerate((own_ref, one_ref, two_ref, three_ref)):
-        turned_ref[...] = jnp.transpose(ref[...])
-        wanted = turned_ref[pl.ds(pl.multiple_of(plane * slots, slots), slots), :]
-        source = (plane + planes - k) & (planes - 1)
-        for first in range(0, owners, group):
-            onehot = jnp.concatenate(
-                [(ids == wanted[:, r : r + 1]).astype(jnp.float32).astype(jnp.bfloat16) for r in range(first, first + group)],
-                axis=0,
-            )
-            got = jnp.dot(onehot, tile_ref[...], preferred_element_type=jnp.float32).astype(jnp.bfloat16)
-            out_ref[source, pl.ds(first, group)] = got.reshape(group, slots, cells)
+    lot = planes * slots
+    group = 4
+    turned_ref[...] = jnp.transpose(asked_ref[...])
+    ids = lax.broadcasted_iota(jnp.int32, (lot, count), 1)
+    for first in range(0, owners, group):
+        onehot = jnp.concatenate(
+            [
+                (ids == turned_ref[0:lot, r : r + 1]).astype(jnp.float32).astype(jnp.bfloat16)
+                for r in range(first, first + group)
+            ],
+            axis=0,
+        )
+        got = jnp.dot(onehot, tile_ref[...], preferred_element_type=jnp.float32).astype(jnp.bfloat16)
+        for r in range(group):
+            for p in range(planes):
+                start = r * lot + p * slots
+                out_ref[p, first + r] = got[start : start + slots]
 
 
 def coarse_kernel(plane_ref, grid_ref, own_ref, one_ref, two_ref, three_ref, out_ref, table_ref, cell_ref):
@@ -283,30 +294,32 @@
     def hop(array, by):
         return lax.ppermute(array, "plane", [(i, (i + by) % planes) for i in range(planes)])
 
+    wishes = tile_requests[0].transpose(0, 2, 1).reshape(planes * slots, owners)
+    wish_parts = [wishes] + [hop(wishes, k) for k in range(1, planes)]
+    coarse_cell, *wish_parts = lax.optimization_barrier((coarse_cell, *wish_parts))
     size = coarse_potential.shape[0] * side // 2 // LANES
     message = pl.pallas_call(
         pack_kernel,
         out_shape=jax.ShapeDtypeStruct((owners, size + 8, LANES), jnp.int32),
-        in_specs=[vmem] * 2,
+        in_specs=[smem] + [vmem] * 5,
         out_specs=vmem,
-        scratch_shapes=[pltpu.VMEM((owners, LANES), jnp.int32)],
+        scratch_shapes=[pltpu.VMEM((LANES, LANES), jnp.int32)] * 2,
         name="pack",
-    )(coarse_potential, tile_requests.reshape(planes, owners, slots))
+    )(plane, coarse_potential, *wish_parts)
     messages = swap(message, "ray")
     cell_parts = [coarse_cell] + [hop(coarse_cell, k) for k in range(1, planes)]
     asked, *cell_parts = lax.optimization_barrier((messages[:, size], *cell_parts))
-    asked_parts = [asked] + [hop(asked, k) for k in range(1, planes)]
 
     outgoing = pl.pallas_call(
         take_kernel,
         out_shape=jax.ShapeDtypeStruct((planes, owners, slots, cells), jnp.bfloat16),
-        in_specs=[smem] + [vmem] * 5,
+        in_specs=[vmem] * 2,
         out_specs=vmem,
         scratch_shapes=[pltpu.VMEM((LANES, owners), jnp.int32)],
         compiler_params=pltpu.CompilerParams(vmem_limit_bytes=32 << 20),
         cost_estimate=pl.CostEstimate(flops=1_100_000_000, bytes_accessed=1_600_000, transcendentals=0),
         name="take",
-    )(plane, *asked_parts, fine_tiles[0])
+    )(asked, fine_tiles[0])
     arrived = swap(outgoing.reshape(planes * owners, slots, cells), ("plane", "ray"))
 
     found = pl.pallas_call(

time: 69.9 us -> 67.9 us (0.971)
  waiting for transfers between devices: 14.5 us -> 12.4 us
  starting transfers between devices: 31.5 us -> 32.6 us
  local copies, waits for them, and re-layouts: 1.54 us -> 0.67 us
    all_to_all x2, waiting for transfers between devices: 8.39 us -> 5.84 us  [swap(): return lax.all_to_all(array, axes, split_axis=0, concat_axis=0, tiled=True)]
    ppermute x9, starting transfers between devices: 14.2 us -> 16.7 us  [hop(): lax.ppermute(array, 'plane', [(i, (i + by) % planes) for i in range(plane...]
    all_to_all x2, starting transfers between devices: 17.3 us -> 15.9 us  [swap(): return lax.all_to_all(array, axes, split_axis=0, concat_axis=0, tiled=True)]
    unnamed x13 -> x18, local copies, waits for them, and re-layouts: 1.51 us -> 0.64 us
  transfers between devices with their start and end apart: 11 -> 11, of which waited for: 7 -> 5; matrix products, arithmetic and copies ran while one was open for 0% -> 0% of each run, Pallas kernels for 16% -> 16%
where the time goes in v4:
time: 67.9 us; the launch traced here: 67.6 us
  starting transfers between devices  32.6 us (48%)
  Pallas kernels  21.1 us (31%)
  waiting for transfers between devices  12.4 us (18%)
  between operations  0.78 us (1%)
    ppermute x9, starting transfers between devices, hop(): lax.ppermute(array, 'plane', [(i, (i + by) % planes) for i in range(plane...  16.7 us
    all_to_all x2, starting transfers between devices, swap(): return lax.all_to_all(array, axes, split_axis=0, concat_axis=0, tiled=True)  15.9 us
    pallas_call x1, Pallas kernels, body(): pl.pallas_call(coarse_kernel, out_shape=jax.ShapeDtypeStruct((planes, 16,...  11.1 us
    ppermute x9, waiting for transfers between devices, hop(): lax.ppermute(array, 'plane', [(i, (i + by) % planes) for i in range(plane...  6.52 us
    all_to_all x2, waiting for transfers between devices, swap(): return lax.all_to_all(array, axes, split_axis=0, concat_axis=0, tiled=True)  5.84 us
    pallas_call x1, Pallas kernels, body(): pl.pallas_call(trace_kernel, out_shape=(jax.ShapeDtypeStruct((2, rays), j...  5.83 us
    pallas_call x1, Pallas kernels, body(): pl.pallas_call(take_kernel, out_shape=jax.ShapeDtypeStruct((planes, owner...  2.42 us
    pallas_call x1, Pallas kernels, body(): pl.pallas_call(pack_kernel, out_shape=jax.ShapeDtypeStruct((owners, size...  1.79 us
  transfers between devices with their start and end apart: 11, of which 5 were waited for; matrix products, arithmetic and copies ran while one was open for 0% of the time, Pallas kernels for 16%

profile of v4, /device:TPU:1, one launch (start us, length us, event | category | flops | bytes accessed | tf_op | source)
XLA Modules:
  0.0 67.6 jit_solution(9879879046903999635)
XLA Ops:
  0.6 1.5 %collective-permute-start.2 = (s32[64,32]{1,0:T(8,128)}, s32[64,32]{1,0:T(8,128)S(1)}, u32[]{:S(2)}, u32[]{:S(2)}) collective-permute-start(s32[64,32]{1,0:T(8,128)} %bitcast.21), channel_id=1, source_target_pairs={{0,96},{32,0},{64,32},{96,64},{1,97},{33,1},{65,33},{97,65},{2,98}... | collective-permute-start | bytes 24584 | tf_op jit(solution)/shard_map/ppermute | solution.py:295
  2.1 2.8 %collective-permute-start.1 = (s32[64,32]{1,0:T(8,128)}, s32[64,32]{1,0:T(8,128)S(1)}, u32[]{:S(2)}, u32[]{:S(2)}) collective-permute-start(s32[64,32]{1,0:T(8,128)} %bitcast.22), channel_id=1, source_target_pairs={{0,64},{32,96},{64,0},{96,32},{1,65},{33,97},{65,1},{97,33},{2,66}... | collective-permute-start | bytes 24584 | tf_op jit(solution)/shard_map/ppermute | solution.py:295
  5.0 2.8 %collective-permute-start = (s32[64,32]{1,0:T(8,128)}, s32[64,32]{1,0:T(8,128)S(1)}, u32[]{:S(2)}, u32[]{:S(2)}) collective-permute-start(s32[64,32]{1,0:T(8,128)} %bitcast.23), channel_id=1, source_target_pairs={{0,32},{32,64},{64,96},{96,0},{1,33},{33,65},{65,97},{97,1},{2,34}... | collective-permute-start | bytes 24584 | tf_op jit(solution)/shard_map/ppermute | solution.py:295
  7.8 1.3 %collective-permute-done.one_ref = s32[64,32]{1,0:T(8,128)S(1)} collective-permute-done((s32[64,32]{1,0:T(8,128)}, s32[64,32]{1,0:T(8,128)S(1)}, u32[]{:S(2)}, u32[]{:S(2)}) %collective-permute-start) | collective-permute-done | bytes 8224 | tf_op jit(solution)/shard_map/ppermute | solution.py:295
  9.2 0.6 copy-done.8
  9.7 1.8 %pack.1 = s32[32,40,128]{2,1,0:T(8,128)} custom-call(s32[1]{0:T(128)} %bitcast.plane_ref, f32[16,512]{1,0:T(8,128)} %coarse_ref.1, s32[64,32]{1,0:T(8,128)} %bitcast.24, s32[64,32]{1,0:T(8,128)} %copy-done.8, s32[64,32]{1,0:T(8,128)} %copy-done.7, s32[64,32]{1,0:T(8,128)} %copy-done.6), custom_call_target="tpu_custom_call" | custom-call | tf_op jit(solution)/shard_map/pack/pallas_call | solution.py:301
  11.5 8.2 %all-to-all-start = ((s32[32,40,128]{2,1,0:T(8,128)}), s32[32,40,128]{2,1,0:T(8,128)S(1)}, u32[]{:S(2)}, u32[]{:S(2)}) async-start(s32[32,40,128]{2,1,0:T(8,128)} %pack.1), calls=%async_computation | async-start | bytes 1310720 | tf_op jit(solution)/shard_map/all_to_all | solution.py:271
  19.8 2.3 %collective-permute-start.5 = (s32[4,1024]{1,0:T(4,128)S(1)}, s32[4,1024]{1,0:T(4,128)S(1)}, u32[]{:S(2)}, u32[]{:S(2)}) collective-permute-start(s32[4,1024]{1,0:T(4,128)S(1)} %copy-done.1), channel_id=1, source_target_pairs={{0,96},{32,0},{64,32},{96,64},{1,97},{33,1},{65,33},{97,65},{2,98}... | collective-permute-start | bytes 49160 | tf_op jit(solution)/shard_map/ppermute | solution.py:295
  22.1 2.5 %collective-permute-start.4 = (s32[4,1024]{1,0:T(4,128)S(1)}, s32[4,1024]{1,0:T(4,128)S(1)}, u32[]{:S(2)}, u32[]{:S(2)}) collective-permute-start(s32[4,1024]{1,0:T(4,128)S(1)} %copy-done.1), channel_id=1, source_target_pairs={{0,64},{32,96},{64,0},{96,32},{1,65},{33,97},{65,1},{97,33},{2,66}... | collective-permute-start | bytes 49160 | tf_op jit(solution)/shard_map/ppermute | solution.py:295
  24.6 0.8 %collective-permute-start.3 = (s32[4,1024]{1,0:T(4,128)S(1)}, s32[4,1024]{1,0:T(4,128)S(1)}, u32[]{:S(2)}, u32[]{:S(2)}) collective-permute-start(s32[4,1024]{1,0:T(4,128)S(1)} %copy-done.1), channel_id=1, source_target_pairs={{0,32},{32,64},{64,96},{96,0},{1,33},{33,65},{65,97},{97,1},{2,34}... | collective-permute-start | bytes 49160 | tf_op jit(solution)/shard_map/ppermute | solution.py:295
  25.3 5.8 %all-to-all-done.grid_ref = s32[32,40,128]{2,1,0:T(8,128)S(1)} async-done(((s32[32,40,128]{2,1,0:T(8,128)}), s32[32,40,128]{2,1,0:T(8,128)S(1)}, u32[]{:S(2)}, u32[]{:S(2)}) %all-to-all-start) | async-done | bytes 655392 | tf_op jit(solution)/shard_map/all_to_all | solution.py:271
  31.2 2.4 %take.1 = bf16[4,32,16,256]{3,2,1,0:T(8,128)(2,1)} custom-call(s32[32,128]{1,0:T(8,128)S(1)} %bitcast.19, bf16[1024,256]{1,0:T(8,128)(2,1)S(1)} %bitcast.20), custom_call_target="tpu_custom_call" | custom-call | flops 1100000000 | bytes 1600000 | tf_op jit(solution)/shard_map/take/pallas_call | solution.py:313
  33.7 7.7 %all-to-all-start.1 = ((bf16[128,16,256]{2,1,0:T(8,128)(2,1)}), bf16[128,16,256]{2,1,0:T(8,128)(2,1)S(1)}, u32[]{:S(2)}, u32[]{:S(2)}) async-start(bf16[128,16,256]{2,1,0:T(8,128)(2,1)} %bitcast.8), calls=%async_computation.1 | async-start | bytes 2097152 | tf_op jit(solution)/shard_map/all_to_all | solution.py:271
  41.3 11.1 %coarse.1 = f32[4,16,1024]{2,1,0:T(8,128)S(1)} custom-call(s32[1]{0:T(128)} %bitcast.plane_ref, s32[32,40,128]{2,1,0:T(8,128)S(1)} %all-to-all-done.grid_ref, s32[4,1024]{1,0:T(4,128)S(1)} %copy-done.1, s32[4,1024]{1,0:T(4,128)S(1)} %collective-permute-done.3.one_ref, s32[4,1024]{1,0:T(4,128)S(1)} %collective-permute-done.4.two_ref, ...), custom_call_target="tpu_custom_call" | custom-call | flops 6000000000 | bytes 1500000 | tf_op jit(solution)/shard_map/coarse/pallas_call | solution.py:325
  52.5 0.0 copy-start.2
  52.5 0.0 copy-start.3
  52.5 0.0 copy-start.4
  52.5 0.0 copy-start.5
  52.5 3.2 %collective-permute-start.8 = (f32[16,1024]{1,0:T(8,128)S(1)}, f32[16,1024]{1,0:T(8,128)S(1)}, u32[]{:S(2)}, u32[]{:S(2)}) collective-permute-start(f32[16,1024]{1,0:T(8,128)S(1)} %get-tuple-element.22), channel_id=1, source_target_pairs={{0,32},{32,64},{64,96},{96,0},{1,33},{33,65},{65,97},{97,1},{2,34}... | collective-permute-start | bytes 196616 | tf_op jit(solution)/shard_map/ppermute | solution.py:295
  55.7 0.8 %collective-permute-start.7 = (f32[16,1024]{1,0:T(8,128)S(1)}, f32[16,1024]{1,0:T(8,128)S(1)}, u32[]{:S(2)}, u32[]{:S(2)}) collective-permute-start(f32[16,1024]{1,0:T(8,128)S(1)} %get-tuple-element.23), channel_id=1, source_target_pairs={{0,64},{32,96},{64,0},{96,32},{1,65},{33,97},{65,1},{97,33},{2,66}... | collective-permute-start | bytes 196616 | tf_op jit(solution)/shard_map/ppermute | solution.py:295
  56.5 0.5 collective-permute-done.8.three_ref
  57.1 3.6 %collective-permute-done.7.two_ref = f32[16,1024]{1,0:T(8,128)S(1)} collective-permute-done((f32[16,1024]{1,0:T(8,128)S(1)}, f32[16,1024]{1,0:T(8,128)S(1)}, u32[]{:S(2)}, u32[]{:S(2)}) %collective-permute-start.7) | collective-permute-done | bytes 65568 | tf_op jit(solution)/shard_map/ppermute | solution.py:295
  60.7 1.1 %collective-permute-done.6.one_ref = f32[16,1024]{1,0:T(8,128)S(1)} collective-permute-done((f32[16,1024]{1,0:T(8,128)S(1)}, f32[16,1024]{1,0:T(8,128)S(1)}, u32[]{:S(2)}, u32[]{:S(2)}) %collective-permute-start.6) | collective-permute-done | bytes 65568 | tf_op jit(solution)/shard_map/ppermute | solution.py:295
  61.8 5.8 %trace.1 = (f32[2,1024]{1,0:T(2,128)}, f32[4,1024]{1,0:T(4,128)}) custom-call(s32[1]{0:T(128)} %bitcast.plane_ref, bf16[4,512,256]{2,1,0:T(8,128)(2,1)S(1)} %bitcast.18, s32[4,1024]{1,0:T(4,128)S(1)} %copy-done.2, s32[4,1024]{1,0:T(4,128)S(1)} %copy-done.3, s32[4,1024]{1,0:T(4,128)S(1)} %copy-done.4, f32[16,1024]{1,0:T(8,128)S(1)} %get-tuple-element.25.own_ref, ...), custom_call_target="tpu_custom_call" | custom-call | flops 1500000000 | bytes 1500000 | tf_op jit(solution)/shard_map/trace/pallas_call | solution.py:340
  (22 shorter events, 0.1 us)
Async XLA Ops:
  0.6 7.2 %collective-permute-start.2 = (s32[64,32]{1,0:T(8,128)}, s32[64,32]{1,0:T(8,128)S(1)}, u32[]{:S(2)}, u32[]{:S(2)}) collective-permute-start(s32[64,32]{1,0:T(8,128)} %bitcast.21), channel_id=1, source_target_pairs={{0,96},{32,0},{64,32},{96,64},{1,97},{33,1},{65,33},{97,65},{2,98}... | collective-permute-start | bytes 24584 | tf_op jit(solution)/shard_map/ppermute | solution.py:295
  2.1 5.7 %collective-permute-start.1 = (s32[64,32]{1,0:T(8,128)}, s32[64,32]{1,0:T(8,128)S(1)}, u32[]{:S(2)}, u32[]{:S(2)}) collective-permute-start(s32[64,32]{1,0:T(8,128)} %bitcast.22), channel_id=1, source_target_pairs={{0,64},{32,96},{64,0},{96,32},{1,65},{33,97},{65,1},{97,33},{2,66}... | collective-permute-start | bytes 24584 | tf_op jit(solution)/shard_map/ppermute | solution.py:295
  5.0 4.2 %collective-permute-start = (s32[64,32]{1,0:T(8,128)}, s32[64,32]{1,0:T(8,128)S(1)}, u32[]{:S(2)}, u32[]{:S(2)}) collective-permute-start(s32[64,32]{1,0:T(8,128)} %bitcast.23), channel_id=1, source_target_pairs={{0,32},{32,64},{64,96},{96,0},{1,33},{33,65},{65,97},{97,1},{2,34}... | collective-permute-start | bytes 24584 | tf_op jit(solution)/shard_map/ppermute | solution.py:295
  7.8 1.3 %copy-start.6 = (s32[64,32]{1,0:T(8,128)}, s32[64,32]{1,0:T(8,128)S(1)}, u32[]{:S(2)}) copy-start(s32[64,32]{1,0:T(8,128)S(1)} %collective-permute-done.2.three_ref) | copy-start | bytes 24580
  7.8 1.3 %copy-start.7 = (s32[64,32]{1,0:T(8,128)}, s32[64,32]{1,0:T(8,128)S(1)}, u32[]{:S(2)}) copy-start(s32[64,32]{1,0:T(8,128)S(1)} %collective-permute-done.1.two_ref) | copy-start | bytes 24580
  9.1 0.6 copy-start.8
  11.5 8.2 %copy-start.1 = (s32[4,1024]{1,0:T(4,128)S(1)}, s32[4,1024]{1,0:T(4,128)}, u32[]{:S(2)}) copy-start(s32[4,1024]{1,0:T(4,128)} %own_ref) | copy-start | bytes 49156
  11.5 19.7 %copy-start = (bf16[1,1024,256]{2,1,0:T(8,128)(2,1)S(1)}, bf16[1,1024,256]{2,1,0:T(8,128)(2,1)}, u32[]{:S(2)}) copy-start(bf16[1,1024,256]{2,1,0:T(8,128)(2,1)} %param.9) | copy-start | bytes 1572868
  11.5 19.6 %all-to-all-start = ((s32[32,40,128]{2,1,0:T(8,128)}), s32[32,40,128]{2,1,0:T(8,128)S(1)}, u32[]{:S(2)}, u32[]{:S(2)}) async-start(s32[32,40,128]{2,1,0:T(8,128)} %pack.1), calls=%async_computation | async-start | bytes 1310720 | tf_op jit(solution)/shard_map/all_to_all | solution.py:271
  19.8 11.4 %collective-permute-start.5 = (s32[4,1024]{1,0:T(4,128)S(1)}, s32[4,1024]{1,0:T(4,128)S(1)}, u32[]{:S(2)}, u32[]{:S(2)}) collective-permute-start(s32[4,1024]{1,0:T(4,128)S(1)} %copy-done.1), channel_id=1, source_target_pairs={{0,96},{32,0},{64,32},{96,64},{1,97},{33,1},{65,33},{97,65},{2,98}... | collective-permute-start | bytes 49160 | tf_op jit(solution)/shard_map/ppermute | solution.py:295
  22.1 9.1 %collective-permute-start.4 = (s32[4,1024]{1,0:T(4,128)S(1)}, s32[4,1024]{1,0:T(4,128)S(1)}, u32[]{:S(2)}, u32[]{:S(2)}) collective-permute-start(s32[4,1024]{1,0:T(4,128)S(1)} %copy-done.1), channel_id=1, source_target_pairs={{0,64},{32,96},{64,0},{96,32},{1,65},{33,97},{65,1},{97,33},{2,66}... | collective-permute-start | bytes 49160 | tf_op jit(solution)/shard_map/ppermute | solution.py:295
  24.6 6.6 %collective-permute-start.3 = (s32[4,1024]{1,0:T(4,128)S(1)}, s32[4,1024]{1,0:T(4,128)S(1)}, u32[]{:S(2)}, u32[]{:S(2)}) collective-permute-start(s32[4,1024]{1,0:T(4,128)S(1)} %copy-done.1), channel_id=1, source_target_pairs={{0,32},{32,64},{64,96},{96,0},{1,33},{33,65},{65,97},{97,1},{2,34}... | collective-permute-start | bytes 49160 | tf_op jit(solution)/shard_map/ppermute | solution.py:295
  33.7 28.1 %all-to-all-start.1 = ((bf16[128,16,256]{2,1,0:T(8,128)(2,1)}), bf16[128,16,256]{2,1,0:T(8,128)(2,1)S(1)}, u32[]{:S(2)}, u32[]{:S(2)}) async-start(bf16[128,16,256]{2,1,0:T(8,128)(2,1)} %bitcast.8), calls=%async_computation.1 | async-start | bytes 2097152 | tf_op jit(solution)/shard_map/all_to_all | solution.py:271
  52.5 9.3 %copy-start.2 = (s32[4,1024]{1,0:T(4,128)S(1)}, s32[4,1024]{1,0:T(4,128)}, u32[]{:S(2)}) copy-start(s32[4,1024]{1,0:T(4,128)} %slot_ref.1) | copy-start | bytes 49156
  52.5 9.3 %copy-start.3 = (s32[4,1024]{1,0:T(4,128)S(1)}, s32[4,1024]{1,0:T(4,128)}, u32[]{:S(2)}) copy-start(s32[4,1024]{1,0:T(4,128)} %fine_ref.1) | copy-start | bytes 49156
  52.5 9.2 %copy-start.4 = (s32[4,1024]{1,0:T(4,128)S(1)}, s32[4,1024]{1,0:T(4,128)}, u32[]{:S(2)}) copy-start(s32[4,1024]{1,0:T(4,128)} %root_ref.1) | copy-start | bytes 49156
  52.5 9.2 %copy-start.5 = (f32[2,1024]{1,0:T(2,128)S(1)}, f32[2,1024]{1,0:T(2,128)}, u32[]{:S(2)}) copy-start(f32[2,1024]{1,0:T(2,128)} %offset_ref.1) | copy-start | bytes 24580
  52.5 4.5 %collective-permute-start.8 = (f32[16,1024]{1,0:T(8,128)S(1)}, f32[16,1024]{1,0:T(8,128)S(1)}, u32[]{:S(2)}, u32[]{:S(2)}) collective-permute-start(f32[16,1024]{1,0:T(8,128)S(1)} %get-tuple-element.22), channel_id=1, source_target_pairs={{0,32},{32,64},{64,96},{96,0},{1,33},{33,65},{65,97},{97,1},{2,34}... | collective-permute-start | bytes 196616 | tf_op jit(solution)/shard_map/ppermute | solution.py:295
  55.7 4.9 %collective-permute-start.7 = (f32[16,1024]{1,0:T(8,128)S(1)}, f32[16,1024]{1,0:T(8,128)S(1)}, u32[]{:S(2)}, u32[]{:S(2)}) collective-permute-start(f32[16,1024]{1,0:T(8,128)S(1)} %get-tuple-element.23), channel_id=1, source_target_pairs={{0,64},{32,96},{64,0},{96,32},{1,65},{33,97},{65,1},{97,33},{2,66}... | collective-permute-start | bytes 196616 | tf_op jit(solution)/shard_map/ppermute | solution.py:295
  56.5 5.2 %collective-permute-start.6 = (f32[16,1024]{1,0:T(8,128)S(1)}, f32[16,1024]{1,0:T(8,128)S(1)}, u32[]{:S(2)}, u32[]{:S(2)}) collective-permute-start(f32[16,1024]{1,0:T(8,128)S(1)} %get-tuple-element.24), channel_id=1, source_target_pairs={{0,96},{32,0},{64,32},{96,64},{1,97},{33,1},{65,33},{97,65},{2,98}... | collective-permute-start | bytes 196616 | tf_op jit(solution)/shard_map/ppermute | solution.py:295

commit v5 on v4

--- a/solution.py
+++ b/solution.py
@@ -86,7 +86,10 @@
                 out_ref[p, first + r] = got[start : start + slots]
 
 
-def coarse_kernel(plane_ref, grid_ref, own_ref, one_ref, two_ref, three_ref, out_ref, table_ref, cell_ref):
+def coarse_kernel(
+    plane_ref, grid_ref, own_ref, one_ref, two_ref, three_ref, out_ref,
+    table_ref, cell_ref, hot_a, hot_b, picked_a, picked_b
+):
     owners, rows, _ = grid_ref.shape
     plane = plane_ref[0]
     side = owners * 2 * WIN
@@ -94,7 +97,7 @@
     chunks = side // LANES
     halves = chunks // 2
     width = TALL * LANES
-    step = 256
+    step = picked_a.shape[1]
     count = windows * chunks
     grid = grid_ref.reshape(owners * rows, LANES)
 
@@ -134,34 +137,55 @@
     bundles = cell_ref.shape[0]
     per = cell_ref.shape[1] // step
 
-    def one(index, carry):
+    def cells_of(index):
         bundle = index // per
         start = pl.multiple_of((index % per) * step, step)
         cell = cell_ref[pl.ds(bundle, 1), pl.ds(start, step)]
-        first_x = (cell - 1) & (side - 1)
-        first_y = (cell // side - 1) & (side - 1)
+        return bundle, start, (cell - 1) & (side - 1), (cell // side - 1) & (side - 1)
+
+    def select(index, hot_ref):
+        _, _, first_x, first_y = cells_of(index)
         tall = first_y // WIN
         window = (first_x // LANES) * windows + (tall & 1) * owners + tall // 2
         ids = lax.broadcasted_iota(jnp.int32, (count, step), 0)
         onehot = (ids == window).astype(jnp.float32).astype(jnp.bfloat16)
-        onehot = jnp.concatenate([onehot, onehot], axis=0)
-        picked = lax.dot_general(
-            table_ref[...], onehot, (((0,), (0,)), ((), ())), preferred_element_type=jnp.float32
+        hot_ref[0:count] = onehot
+        hot_ref[count : 2 * count] = onehot
+
+    def pick(hot_ref, picked_ref):
+        picked_ref[...] = lax.dot_general(
+            table_ref[...], hot_ref[...], (((0,), (0,)), ((), ())), preferred_element_type=jnp.float32
         )
+
+    def narrow(index, picked_ref):
+        bundle, start, first_x, first_y = cells_of(index)
         off_y = first_y & (WIN - 1)
         off_x = first_x & (LANES - 1)
         lines = []
         for dy in range(TALL):
-            parts = [picked[dy * LANES + 8 * k : dy * LANES + 8 * k + 8] for k in range(LANES // 8)]
-            parts.append(picked[width + dy * HALO : width + (dy + 1) * HALO])
+            parts = [picked_ref[dy * LANES + 8 * k : dy * LANES + 8 * k + 8] for k in range(LANES // 8)]
+            parts.append(picked_ref[width + dy * HALO : width + (dy + 1) * HALO])
             lines.append(shift_rows(parts, off_x // 8, (8, 4, 2, 1), 2))
         low = shift_rows([line[0] for line in lines], off_y, (4, 2, 1), 4)
         high = shift_rows([line[1] for line in lines], off_y, (4, 2, 1), 4)
-        patch = [shift_within(low[i], high[i], off_x)[:4] for i in range(4)]
-        out_ref[bundle, :, pl.ds(start, step)] = jnp.concatenate(patch, axis=0)
+        patch = [shift_within(low[i], high[i], off_x)[:4].astype(jnp.int32) for i in range(4)]
+        words = [(patch[i] << 16) | (patch[i + 2] & 0xFFFF) for i in range(2)]
+        out_ref[bundle, :, pl.ds(start, step)] = jnp.concatenate(words, axis=0)
+
+    total = bundles * per
+    select(0, hot_a)
+
+    def two(j, carry):
+        select(2 * j + 1, hot_b)
+        pick(hot_a, picked_a)
+        narrow(jnp.maximum(2 * j - 1, 0), picked_b)
+        select(jnp.minimum(2 * j + 2, total - 1), hot_a)
+        pick(hot_b, picked_b)
+        narrow(2 * j, picked_a)
         return carry
 
-    lax.fori_loop(0, bundles * per, one, 0)
+    lax.fori_loop(0, total // 2, two, 0)
+    narrow(total - 1, picked_b)
 
 
 def stencil_terms(patch, frac_x, frac_y):
@@ -193,10 +217,14 @@
 ):
     planes = tile_ref.shape[0]
     for k, ref in enumerate((own_ref, one_ref, two_ref, three_ref)):
-        coarse_ref[(plane_ref[0] + k) & (planes - 1)] = ref[...]
+        words = ref[...]
+        half = words.shape[0]
+        from_plane = (plane_ref[0] + k) & (planes - 1)
+        coarse_ref[from_plane, 0:half] = (words >> 16).astype(jnp.float32)
+        coarse_ref[from_plane, half : 2 * half] = ((words << 16) >> 16).astype(jnp.float32)
     slots = tile_ref.shape[1]
     rays = slot_ref.shape[1]
-    step = 256
+    step = rays
 
     def one(index, carry):
         plane = index // (rays // step)
@@ -217,7 +245,7 @@
             patch_ref[plane, i, :, pl.ds(start, step)] = shift_within(first, high[i], off_x)
         return carry
 
-    lax.fori_loop(0, planes * (rays // step), one, 0)
+    lax.fori_loop(0, planes * (rays // step), one, 0, unroll=True)
 
     offset = [offset_ref[0:1], offset_ref[1:2]]
     disp = [jnp.zeros((1, rays), jnp.float32)] * 2
@@ -322,14 +350,20 @@
     )(asked, fine_tiles[0])
     arrived = swap(outgoing.reshape(planes * owners, slots, cells), ("plane", "ray"))
 
+    codes = 2 * side // WIN * (side // LANES)
+    step = min(512, rays)
     found = pl.pallas_call(
         coarse_kernel,
-        out_shape=jax.ShapeDtypeStruct((planes, 16, rays), jnp.float32),
+        out_shape=jax.ShapeDtypeStruct((planes, 8, rays), jnp.int32),
         in_specs=[smem] + [vmem] * 5,
         out_specs=vmem,
         scratch_shapes=[
-            pltpu.VMEM((2 * side // WIN * (side // LANES), (TALL + 1) * LANES), jnp.bfloat16),
+            pltpu.VMEM((codes, (TALL + 1) * LANES), jnp.bfloat16),
             pltpu.VMEM((planes, rays), jnp.int32),
+            pltpu.VMEM((codes, step), jnp.bfloat16),
+            pltpu.VMEM((codes, step), jnp.bfloat16),
+            pltpu.VMEM(((TALL + 1) * LANES, step), jnp.float32),
+            pltpu.VMEM(((TALL + 1) * LANES, step), jnp.float32),
         ],
         compiler_params=pltpu.CompilerParams(vmem_limit_bytes=32 << 20),
         cost_estimate=pl.CostEstimate(flops=6_000_000_000, bytes_accessed=1_500_000, transcendentals=0),

time: 67.9 us -> 63.6 us (0.937)
  Pallas kernels: 21.1 us -> 16.1 us
  waiting for transfers between devices: 12.4 us -> 13.1 us
    pallas_call x1, Pallas kernels: 5.83 us -> 2.59 us  [body(): pl.pallas_call(trace_kernel, out_shape=(jax.ShapeDtypeStruct((2, rays), j...]
    pallas_call x1, Pallas kernels: 11.1 us -> 9.26 us  [body(): pl.pallas_call(coarse_kernel, out_shape=jax.ShapeDtypeStruct((planes, 8,...]
    all_to_all x2, waiting for transfers between devices: 5.84 us -> 6.63 us  [swap(): return lax.all_to_all(array, axes, split_axis=0, concat_axis=0, tiled=True)]
  transfers between devices with their start and end apart: 11 -> 11, of which waited for: 5 -> 6; matrix products, arithmetic and copies ran while one was open for 0% -> 0% of each run, Pallas kernels for 16% -> 15%
where the time goes in v5:
time: 63.6 us; the launch traced here: 63.2 us
  starting transfers between devices  32.6 us (51%)
  Pallas kernels  16.1 us (25%)
  waiting for transfers between devices  13.1 us (21%)
  between operations  0.77 us (1%)
  local copies, waits for them, and re-layouts  0.66 us (1%)
    ppermute x9, starting transfers between devices, hop(): lax.ppermute(array, 'plane', [(i, (i + by) % planes) for i in range(plane...  16.7 us
    all_to_all x2, starting transfers between devices, swap(): return lax.all_to_all(array, axes, split_axis=0, concat_axis=0, tiled=True)  15.9 us
    pallas_call x1, Pallas kernels, body(): pl.pallas_call(coarse_kernel, out_shape=jax.ShapeDtypeStruct((planes, 8,...  9.26 us
    all_to_all x2, waiting for transfers between devices, swap(): return lax.all_to_all(array, axes, split_axis=0, concat_axis=0, tiled=True)  6.63 us
    ppermute x9, waiting for transfers between devices, hop(): lax.ppermute(array, 'plane', [(i, (i + by) % planes) for i in range(plane...  6.47 us
    pallas_call x1, Pallas kernels, body(): pl.pallas_call(trace_kernel, out_shape=(jax.ShapeDtypeStruct((2, rays), j...  2.59 us
    pallas_call x1, Pallas kernels, body(): pl.pallas_call(take_kernel, out_shape=jax.ShapeDtypeStruct((planes, owner...  2.42 us
    pallas_call x1, Pallas kernels, body(): pl.pallas_call(pack_kernel, out_shape=jax.ShapeDtypeStruct((owners, size...  1.79 us
  transfers between devices with their start and end apart: 11, of which 6 were waited for; matrix products, arithmetic and copies ran while one was open for 0% of the time, Pallas kernels for 15%

profile of v5, /device:TPU:1, one launch (start us, length us, event | category | flops | bytes accessed | tf_op | source)
XLA Modules:
  0.0 63.2 jit_solution(7543779144038916935)
XLA Ops:
  0.6 1.5 %collective-permute-start.2 = (s32[64,32]{1,0:T(8,128)}, s32[64,32]{1,0:T(8,128)S(1)}, u32[]{:S(2)}, u32[]{:S(2)}) collective-permute-start(s32[64,32]{1,0:T(8,128)} %bitcast.21), channel_id=1, source_target_pairs={{0,96},{32,0},{64,32},{96,64},{1,97},{33,1},{65,33},{97,65},{2,98}... | collective-permute-start | bytes 24584 | tf_op jit(solution)/shard_map/ppermute | solution.py:323
  2.1 2.8 %collective-permute-start.1 = (s32[64,32]{1,0:T(8,128)}, s32[64,32]{1,0:T(8,128)S(1)}, u32[]{:S(2)}, u32[]{:S(2)}) collective-permute-start(s32[64,32]{1,0:T(8,128)} %bitcast.22), channel_id=1, source_target_pairs={{0,64},{32,96},{64,0},{96,32},{1,65},{33,97},{65,1},{97,33},{2,66}... | collective-permute-start | bytes 24584 | tf_op jit(solution)/shard_map/ppermute | solution.py:323
  5.0 2.8 %collective-permute-start = (s32[64,32]{1,0:T(8,128)}, s32[64,32]{1,0:T(8,128)S(1)}, u32[]{:S(2)}, u32[]{:S(2)}) collective-permute-start(s32[64,32]{1,0:T(8,128)} %bitcast.23), channel_id=1, source_target_pairs={{0,32},{32,64},{64,96},{96,0},{1,33},{33,65},{65,97},{97,1},{2,34}... | collective-permute-start | bytes 24584 | tf_op jit(solution)/shard_map/ppermute | solution.py:323
  7.8 1.3 %collective-permute-done.one_ref = s32[64,32]{1,0:T(8,128)S(1)} collective-permute-done((s32[64,32]{1,0:T(8,128)}, s32[64,32]{1,0:T(8,128)S(1)}, u32[]{:S(2)}, u32[]{:S(2)}) %collective-permute-start) | collective-permute-done | bytes 8224 | tf_op jit(solution)/shard_map/ppermute | solution.py:323
  9.2 0.6 copy-done.8
  9.7 1.8 %pack.1 = s32[32,40,128]{2,1,0:T(8,128)} custom-call(s32[1]{0:T(128)} %bitcast.plane_ref, f32[16,512]{1,0:T(8,128)} %coarse_ref.1, s32[64,32]{1,0:T(8,128)} %bitcast.24, s32[64,32]{1,0:T(8,128)} %copy-done.8, s32[64,32]{1,0:T(8,128)} %copy-done.7, s32[64,32]{1,0:T(8,128)} %copy-done.6), custom_call_target="tpu_custom_call" | custom-call | tf_op jit(solution)/shard_map/pack/pallas_call | solution.py:329
  11.5 8.2 %all-to-all-start = ((s32[32,40,128]{2,1,0:T(8,128)}), s32[32,40,128]{2,1,0:T(8,128)S(1)}, u32[]{:S(2)}, u32[]{:S(2)}) async-start(s32[32,40,128]{2,1,0:T(8,128)} %pack.1), calls=%async_computation | async-start | bytes 1310720 | tf_op jit(solution)/shard_map/all_to_all | solution.py:299
  19.8 2.3 %collective-permute-start.5 = (s32[4,1024]{1,0:T(4,128)S(1)}, s32[4,1024]{1,0:T(4,128)S(1)}, u32[]{:S(2)}, u32[]{:S(2)}) collective-permute-start(s32[4,1024]{1,0:T(4,128)S(1)} %copy-done.1), channel_id=1, source_target_pairs={{0,96},{32,0},{64,32},{96,64},{1,97},{33,1},{65,33},{97,65},{2,98}... | collective-permute-start | bytes 49160 | tf_op jit(solution)/shard_map/ppermute | solution.py:323
  22.1 2.5 %collective-permute-start.4 = (s32[4,1024]{1,0:T(4,128)S(1)}, s32[4,1024]{1,0:T(4,128)S(1)}, u32[]{:S(2)}, u32[]{:S(2)}) collective-permute-start(s32[4,1024]{1,0:T(4,128)S(1)} %copy-done.1), channel_id=1, source_target_pairs={{0,64},{32,96},{64,0},{96,32},{1,65},{33,97},{65,1},{97,33},{2,66}... | collective-permute-start | bytes 49160 | tf_op jit(solution)/shard_map/ppermute | solution.py:323
  24.6 0.8 %collective-permute-start.3 = (s32[4,1024]{1,0:T(4,128)S(1)}, s32[4,1024]{1,0:T(4,128)S(1)}, u32[]{:S(2)}, u32[]{:S(2)}) collective-permute-start(s32[4,1024]{1,0:T(4,128)S(1)} %copy-done.1), channel_id=1, source_target_pairs={{0,32},{32,64},{64,96},{96,0},{1,33},{33,65},{65,97},{97,1},{2,34}... | collective-permute-start | bytes 49160 | tf_op jit(solution)/shard_map/ppermute | solution.py:323
  25.3 5.8 %all-to-all-done.grid_ref = s32[32,40,128]{2,1,0:T(8,128)S(1)} async-done(((s32[32,40,128]{2,1,0:T(8,128)}), s32[32,40,128]{2,1,0:T(8,128)S(1)}, u32[]{:S(2)}, u32[]{:S(2)}) %all-to-all-start) | async-done | bytes 655392 | tf_op jit(solution)/shard_map/all_to_all | solution.py:299
  31.2 2.4 %take.1 = bf16[4,32,16,256]{3,2,1,0:T(8,128)(2,1)} custom-call(s32[32,128]{1,0:T(8,128)S(1)} %bitcast.19, bf16[1024,256]{1,0:T(8,128)(2,1)S(1)} %bitcast.20), custom_call_target="tpu_custom_call" | custom-call | flops 1100000000 | bytes 1600000 | tf_op jit(solution)/shard_map/take/pallas_call | solution.py:341
  33.7 7.7 %all-to-all-start.1 = ((bf16[128,16,256]{2,1,0:T(8,128)(2,1)}), bf16[128,16,256]{2,1,0:T(8,128)(2,1)S(1)}, u32[]{:S(2)}, u32[]{:S(2)}) async-start(bf16[128,16,256]{2,1,0:T(8,128)(2,1)} %bitcast.8), calls=%async_computation.1 | async-start | bytes 2097152 | tf_op jit(solution)/shard_map/all_to_all | solution.py:299
  41.3 9.3 %coarse.1 = s32[4,8,1024]{2,1,0:T(8,128)S(1)} custom-call(s32[1]{0:T(128)} %bitcast.plane_ref, s32[32,40,128]{2,1,0:T(8,128)S(1)} %all-to-all-done.grid_ref, s32[4,1024]{1,0:T(4,128)S(1)} %copy-done.1, s32[4,1024]{1,0:T(4,128)S(1)} %collective-permute-done.3.one_ref, s32[4,1024]{1,0:T(4,128)S(1)} %collective-permute-done.4.two_ref, ...), custom_call_target="tpu_custom_call" | custom-call | flops 6000000000 | bytes 1500000 | tf_op jit(solution)/shard_map/coarse/pallas_call | solution.py:355
  50.6 0.0 copy-start.3
  50.6 0.0 copy-start.4
  50.7 0.0 copy-start.5
  50.7 3.2 %collective-permute-start.8 = (s32[8,1024]{1,0:T(8,128)S(1)}, s32[8,1024]{1,0:T(8,128)S(1)}, u32[]{:S(2)}, u32[]{:S(2)}) collective-permute-start(s32[8,1024]{1,0:T(8,128)S(1)} %get-tuple-element.22), channel_id=1, source_target_pairs={{0,32},{32,64},{64,96},{96,0},{1,33},{33,65},{65,97},{97,1},{2,34}... | collective-permute-start | bytes 98312 | tf_op jit(solution)/shard_map/ppermute | solution.py:323
  53.9 0.8 %collective-permute-start.7 = (s32[8,1024]{1,0:T(8,128)S(1)}, s32[8,1024]{1,0:T(8,128)S(1)}, u32[]{:S(2)}, u32[]{:S(2)}) collective-permute-start(s32[8,1024]{1,0:T(8,128)S(1)} %get-tuple-element.23), channel_id=1, source_target_pairs={{0,64},{32,96},{64,0},{96,32},{1,65},{33,97},{65,1},{97,33},{2,66}... | collective-permute-start | bytes 98312 | tf_op jit(solution)/shard_map/ppermute | solution.py:323
  54.7 0.2 collective-permute-done.8.three_ref
  54.9 3.5 %collective-permute-done.7.two_ref = s32[8,1024]{1,0:T(8,128)S(1)} collective-permute-done((s32[8,1024]{1,0:T(8,128)S(1)}, s32[8,1024]{1,0:T(8,128)S(1)}, u32[]{:S(2)}, u32[]{:S(2)}) %collective-permute-start.7) | collective-permute-done | bytes 32800 | tf_op jit(solution)/shard_map/ppermute | solution.py:323
  58.5 1.4 %collective-permute-done.6.one_ref = s32[8,1024]{1,0:T(8,128)S(1)} collective-permute-done((s32[8,1024]{1,0:T(8,128)S(1)}, s32[8,1024]{1,0:T(8,128)S(1)}, u32[]{:S(2)}, u32[]{:S(2)}) %collective-permute-start.6) | collective-permute-done | bytes 32800 | tf_op jit(solution)/shard_map/ppermute | solution.py:323
  59.8 0.8 %all-to-all-done.1 = bf16[128,16,256]{2,1,0:T(8,128)(2,1)S(1)} async-done(((bf16[128,16,256]{2,1,0:T(8,128)(2,1)}), bf16[128,16,256]{2,1,0:T(8,128)(2,1)S(1)}, u32[]{:S(2)}, u32[]{:S(2)}) %all-to-all-start.1) | async-done | bytes 1048608 | tf_op jit(solution)/shard_map/all_to_all | solution.py:299
  60.6 2.6 %trace.1 = (f32[2,1024]{1,0:T(2,128)}, f32[4,1024]{1,0:T(4,128)}) custom-call(s32[1]{0:T(128)} %bitcast.plane_ref, bf16[4,512,256]{2,1,0:T(8,128)(2,1)S(1)} %bitcast.18, s32[4,1024]{1,0:T(4,128)S(1)} %copy-done.2, s32[4,1024]{1,0:T(4,128)S(1)} %copy-done.3, s32[4,1024]{1,0:T(4,128)S(1)} %copy-done.4, s32[8,1024]{1,0:T(8,128)S(1)} %get-tuple-element.25.own_ref, ...), custom_call_target="tpu_custom_call" | custom-call | flops 1500000000 | bytes 1500000 | tf_op jit(solution)/shard_map/trace/pallas_call | solution.py:374
  (22 shorter events, 0.1 us)
Async XLA Ops:
  0.6 7.2 %collective-permute-start.2 = (s32[64,32]{1,0:T(8,128)}, s32[64,32]{1,0:T(8,128)S(1)}, u32[]{:S(2)}, u32[]{:S(2)}) collective-permute-start(s32[64,32]{1,0:T(8,128)} %bitcast.21), channel_id=1, source_target_pairs={{0,96},{32,0},{64,32},{96,64},{1,97},{33,1},{65,33},{97,65},{2,98}... | collective-permute-start | bytes 24584 | tf_op jit(solution)/shard_map/ppermute | solution.py:323
  2.1 5.7 %collective-permute-start.1 = (s32[64,32]{1,0:T(8,128)}, s32[64,32]{1,0:T(8,128)S(1)}, u32[]{:S(2)}, u32[]{:S(2)}) collective-permute-start(s32[64,32]{1,0:T(8,128)} %bitcast.22), channel_id=1, source_target_pairs={{0,64},{32,96},{64,0},{96,32},{1,65},{33,97},{65,1},{97,33},{2,66}... | collective-permute-start | bytes 24584 | tf_op jit(solution)/shard_map/ppermute | solution.py:323
  5.0 4.2 %collective-permute-start = (s32[64,32]{1,0:T(8,128)}, s32[64,32]{1,0:T(8,128)S(1)}, u32[]{:S(2)}, u32[]{:S(2)}) collective-permute-start(s32[64,32]{1,0:T(8,128)} %bitcast.23), channel_id=1, source_target_pairs={{0,32},{32,64},{64,96},{96,0},{1,33},{33,65},{65,97},{97,1},{2,34}... | collective-permute-start | bytes 24584 | tf_op jit(solution)/shard_map/ppermute | solution.py:323
  7.8 1.3 %copy-start.6 = (s32[64,32]{1,0:T(8,128)}, s32[64,32]{1,0:T(8,128)S(1)}, u32[]{:S(2)}) copy-start(s32[64,32]{1,0:T(8,128)S(1)} %collective-permute-done.2.three_ref) | copy-start | bytes 24580
  7.8 1.3 %copy-start.7 = (s32[64,32]{1,0:T(8,128)}, s32[64,32]{1,0:T(8,128)S(1)}, u32[]{:S(2)}) copy-start(s32[64,32]{1,0:T(8,128)S(1)} %collective-permute-done.1.two_ref) | copy-start | bytes 24580
  9.1 0.6 copy-start.8
  11.5 8.2 %copy-start.1 = (s32[4,1024]{1,0:T(4,128)S(1)}, s32[4,1024]{1,0:T(4,128)}, u32[]{:S(2)}) copy-start(s32[4,1024]{1,0:T(4,128)} %own_ref) | copy-start | bytes 49156
  11.5 19.7 %copy-start = (bf16[1,1024,256]{2,1,0:T(8,128)(2,1)S(1)}, bf16[1,1024,256]{2,1,0:T(8,128)(2,1)}, u32[]{:S(2)}) copy-start(bf16[1,1024,256]{2,1,0:T(8,128)(2,1)} %param.9) | copy-start | bytes 1572868
  11.5 19.6 %all-to-all-start = ((s32[32,40,128]{2,1,0:T(8,128)}), s32[32,40,128]{2,1,0:T(8,128)S(1)}, u32[]{:S(2)}, u32[]{:S(2)}) async-start(s32[32,40,128]{2,1,0:T(8,128)} %pack.1), calls=%async_computation | async-start | bytes 1310720 | tf_op jit(solution)/shard_map/all_to_all | solution.py:299
  19.8 11.4 %collective-permute-start.5 = (s32[4,1024]{1,0:T(4,128)S(1)}, s32[4,1024]{1,0:T(4,128)S(1)}, u32[]{:S(2)}, u32[]{:S(2)}) collective-permute-start(s32[4,1024]{1,0:T(4,128)S(1)} %copy-done.1), channel_id=1, source_target_pairs={{0,96},{32,0},{64,32},{96,64},{1,97},{33,1},{65,33},{97,65},{2,98}... | collective-permute-start | bytes 49160 | tf_op jit(solution)/shard_map/ppermute | solution.py:323
  22.1 9.1 %collective-permute-start.4 = (s32[4,1024]{1,0:T(4,128)S(1)}, s32[4,1024]{1,0:T(4,128)S(1)}, u32[]{:S(2)}, u32[]{:S(2)}) collective-permute-start(s32[4,1024]{1,0:T(4,128)S(1)} %copy-done.1), channel_id=1, source_target_pairs={{0,64},{32,96},{64,0},{96,32},{1,65},{33,97},{65,1},{97,33},{2,66}... | collective-permute-start | bytes 49160 | tf_op jit(solution)/shard_map/ppermute | solution.py:323
  24.6 6.6 %collective-permute-start.3 = (s32[4,1024]{1,0:T(4,128)S(1)}, s32[4,1024]{1,0:T(4,128)S(1)}, u32[]{:S(2)}, u32[]{:S(2)}) collective-permute-start(s32[4,1024]{1,0:T(4,128)S(1)} %copy-done.1), channel_id=1, source_target_pairs={{0,32},{32,64},{64,96},{96,0},{1,33},{33,65},{65,97},{97,1},{2,34}... | collective-permute-start | bytes 49160 | tf_op jit(solution)/shard_map/ppermute | solution.py:323
  33.7 27.0 %all-to-all-start.1 = ((bf16[128,16,256]{2,1,0:T(8,128)(2,1)}), bf16[128,16,256]{2,1,0:T(8,128)(2,1)S(1)}, u32[]{:S(2)}, u32[]{:S(2)}) async-start(bf16[128,16,256]{2,1,0:T(8,128)(2,1)} %bitcast.8), calls=%async_computation.1 | async-start | bytes 2097152 | tf_op jit(solution)/shard_map/all_to_all | solution.py:299
  50.6 10.0 %copy-start.2 = (s32[4,1024]{1,0:T(4,128)S(1)}, s32[4,1024]{1,0:T(4,128)}, u32[]{:S(2)}) copy-start(s32[4,1024]{1,0:T(4,128)} %slot_ref.1) | copy-start | bytes 49156
  50.6 10.0 %copy-start.3 = (s32[4,1024]{1,0:T(4,128)S(1)}, s32[4,1024]{1,0:T(4,128)}, u32[]{:S(2)}) copy-start(s32[4,1024]{1,0:T(4,128)} %fine_ref.1) | copy-start | bytes 49156
  50.6 10.0 %copy-start.4 = (s32[4,1024]{1,0:T(4,128)S(1)}, s32[4,1024]{1,0:T(4,128)}, u32[]{:S(2)}) copy-start(s32[4,1024]{1,0:T(4,128)} %root_ref.1) | copy-start | bytes 49156
  50.7 10.0 %copy-start.5 = (f32[2,1024]{1,0:T(2,128)S(1)}, f32[2,1024]{1,0:T(2,128)}, u32[]{:S(2)}) copy-start(f32[2,1024]{1,0:T(2,128)} %offset_ref.1) | copy-start | bytes 24580
  50.7 4.2 %collective-permute-start.8 = (s32[8,1024]{1,0:T(8,128)S(1)}, s32[8,1024]{1,0:T(8,128)S(1)}, u32[]{:S(2)}, u32[]{:S(2)}) collective-permute-start(s32[8,1024]{1,0:T(8,128)S(1)} %get-tuple-element.22), channel_id=1, source_target_pairs={{0,32},{32,64},{64,96},{96,0},{1,33},{33,65},{65,97},{97,1},{2,34}... | collective-permute-start | bytes 98312 | tf_op jit(solution)/shard_map/ppermute | solution.py:323
  53.9 4.6 %collective-permute-start.7 = (s32[8,1024]{1,0:T(8,128)S(1)}, s32[8,1024]{1,0:T(8,128)S(1)}, u32[]{:S(2)}, u32[]{:S(2)}) collective-permute-start(s32[8,1024]{1,0:T(8,128)S(1)} %get-tuple-element.23), channel_id=1, source_target_pairs={{0,64},{32,96},{64,0},{96,32},{1,65},{33,97},{65,1},{97,33},{2,66}... | collective-permute-start | bytes 98312 | tf_op jit(solution)/shard_map/ppermute | solution.py:323
  54.7 5.1 %collective-permute-start.6 = (s32[8,1024]{1,0:T(8,128)S(1)}, s32[8,1024]{1,0:T(8,128)S(1)}, u32[]{:S(2)}, u32[]{:S(2)}) collective-permute-start(s32[8,1024]{1,0:T(8,128)S(1)} %get-tuple-element.24), channel_id=1, source_target_pairs={{0,96},{32,0},{64,32},{96,64},{1,97},{33,1},{65,33},{97,65},{2,98}... | collective-permute-start | bytes 98312 | tf_op jit(solution)/shard_map/ppermute | solution.py:323

commit v6 on v5

--- a/solution.py
+++ b/solution.py
@@ -37,76 +37,87 @@
     return jnp.where((amount & 1) != 0, pltpu.roll(here, 7, 0), here)
 
 
-def pack_kernel(plane_ref, coarse_ref, own_ref, one_ref, two_ref, three_ref, out_ref, wish_ref, row_ref):
-    owners, rows, _ = out_ref.shape
-    planes = PLANES
-    slots = own_ref.shape[0] // planes
+def pack_kernel(place_ref, coarse_ref, own_ref, far_ref, out_ref, wish_ref, row_ref):
+    cores = 2
+    slots = LANES // 8
+    owners = own_ref.shape[1]
+    rows = out_ref.shape[0] // (cores * owners)
     side = coarse_ref.shape[1]
     half = side // 2
     code = jnp.floor(coarse_ref[...] * (1.0 / UNIT) + 0.5).astype(jnp.int32)
     word = (code[:, :half] << 16) | (code[:, half:] & 0xFFFF)
-    tiles = []
-    for y in range(coarse_ref.shape[0] // WIN):
-        for x in range(half // LANES):
-            tiles.append(word[y * WIN : (y + 1) * WIN, x * LANES : (x + 1) * LANES])
-    block = jnp.concatenate(tiles, axis=0)
-    plane = plane_ref[0]
+    far = place_ref[0] // cores
     wish_ref[...] = jnp.zeros_like(wish_ref)
-    for k, ref in enumerate((own_ref, one_ref, two_ref, three_ref)):
-        source = (plane + planes - k) & (planes - 1)
-        wish_ref[pl.ds(pl.multiple_of(source * slots, slots), slots), 0:owners] = ref[
-            pl.ds(pl.multiple_of(plane * slots, slots), slots), :
-        ]
+    for core in range(cores):
+        line = pl.ds(pl.multiple_of((far * cores + core) * slots, slots), slots)
+        wish_ref[pl.ds(pl.multiple_of(core * 2 * slots + far * slots, slots), slots), 0:owners] = own_ref[line, :]
+        wish_ref[pl.ds(pl.multiple_of(core * 2 * slots + (1 - far) * slots, slots), slots), 0:owners] = far_ref[line, :]
     row_ref[...] = jnp.transpose(wish_ref[...])
-    size = rows - 8
-    for owner in range(owners):
-        out_ref[owner, 0:size] = block
-        out_ref[owner, size:rows] = jnp.broadcast_to(row_ref[owner : owner + 1], (8, LANES))
-
-
-def take_kernel(asked_ref, tile_ref, out_ref, turned_ref):
-    planes, owners, slots, cells = out_ref.shape
+    for core in range(cores):
+        lines = row_ref[0:owners]
+        lines = pltpu.roll(lines, LANES - core * 2 * slots, 1) if core else lines
+        part = [word[core * WIN : (core + 1) * WIN, x * LANES : (x + 1) * LANES] for x in range(half // LANES)]
+        for owner in range(owners):
+            at = (core * owners + owner) * rows
+            for x in range(half // LANES):
+                out_ref[at + x * WIN : at + (x + 1) * WIN] = part[x]
+            out_ref[at + rows - 1 : at + rows] = lines[owner : owner + 1]
+
+
+def take_kernel(message_ref, tile_ref, out_ref, turned_ref):
+    bundles, slots, cells = out_ref.shape
+    messages = bundles // 2
+    rows = message_ref.shape[0] // messages
     count = tile_ref.shape[0]
-    lot = planes * slots
-    group = 4
-    turned_ref[...] = jnp.transpose(asked_ref[...])
-    ids = lax.broadcasted_iota(jnp.int32, (lot, count), 1)
-    for first in range(0, owners, group):
+    group = 16
+    asked = message_ref[pl.ds(rows - 1, messages, stride=rows), :]
+    turned_ref[...] = jnp.transpose(asked)
+    ids = lax.broadcasted_iota(jnp.int32, (slots, count), 1)
+    for first in range(0, bundles, group):
+        line = first // messages * slots
         onehot = jnp.concatenate(
             [
-                (ids == turned_ref[0:lot, r : r + 1]).astype(jnp.float32).astype(jnp.bfloat16)
-                for r in range(first, first + group)
+                (ids == turned_ref[line : line + slots, b % messages : b % messages + 1])
+                .astype(jnp.float32)
+                .astype(jnp.bfloat16)
+                for b in range(first, first + group)
             ],
             axis=0,
         )
         got = jnp.dot(onehot, tile_ref[...], preferred_element_type=jnp.float32).astype(jnp.bfloat16)
-        for r in range(group):
-            for p in range(planes):
-                start = r * lot + p * slots
-                out_ref[p, first + r] = got[start : start + slots]
+        out_ref[first : first + group] = got.reshape(group, slots, cells)
 
 
 def coarse_kernel(
-    plane_ref, grid_ref, own_ref, one_ref, two_ref, three_ref, out_ref,
-    table_ref, cell_ref, hot_a, hot_b, picked_a, picked_b
+    place_ref, near_ref, pair_ref, own_ref, one_ref, two_ref, three_ref, out_ref,
+    table_ref, cell_ref, hot_a, hot_b, picked_a, picked_b, grid_ref
 ):
-    owners, rows, _ = grid_ref.shape
-    plane = plane_ref[0]
-    side = owners * 2 * WIN
+    plane = place_ref[0]
+    core = plane & 1
+    size = 2 * WIN
+    owners = grid_ref.shape[0] // (2 * size)
+    rows = near_ref.shape[0] // (2 * owners)
+    side = owners * size
     windows = side // WIN
     chunks = side // LANES
     halves = chunks // 2
     width = TALL * LANES
     step = picked_a.shape[1]
     count = windows * chunks
-    grid = grid_ref.reshape(owners * rows, LANES)
+    for owner in range(owners):
+        first = owner * rows
+        second = (owners + owner) * rows
+        near = jnp.where(core == 0, near_ref[first : first + size], near_ref[second : second + size])
+        pair = jnp.where(core == 0, pair_ref[first : first + size], pair_ref[second : second + size])
+        grid_ref[owner * size : (owner + 1) * size] = jnp.where(core == 0, near, pair)
+        grid_ref[(owners + owner) * size : (owners + owner + 1) * size] = jnp.where(core == 0, pair, near)
 
     def load(chunk, dy):
         parts = []
         for parity in range(2):
             pick = (parity + dy // WIN) % 2
-            start = (pick * halves + chunk % halves) * WIN + dy % WIN
-            part = grid[pl.ds(start, owners, stride=rows), :]
+            start = pick * owners * size + chunk % halves * WIN + dy % WIN
+            part = grid_ref[pl.ds(start, owners, stride=size), :]
             if parity + dy // WIN >= 2:
                 part = pltpu.roll(part, owners - 1, 0)
             parts.append(part)
@@ -317,45 +328,52 @@
     cells = TP * TP
     vmem = pl.BlockSpec(memory_space=pltpu.VMEM)
     smem = pl.BlockSpec(memory_space=pltpu.SMEM)
-    plane = jnp.full((1,), lax.axis_index("plane"), jnp.int32)
+    place = jnp.full((1,), lax.axis_index("plane"), jnp.int32)
 
     def hop(array, by):
         return lax.ppermute(array, "plane", [(i, (i + by) % planes) for i in range(planes)])
 
     wishes = tile_requests[0].transpose(0, 2, 1).reshape(planes * slots, owners)
-    wish_parts = [wishes] + [hop(wishes, k) for k in range(1, planes)]
-    coarse_cell, *wish_parts = lax.optimization_barrier((coarse_cell, *wish_parts))
-    size = coarse_potential.shape[0] * side // 2 // LANES
+    coarse_cell, far_wishes = lax.optimization_barrier((coarse_cell, hop(wishes, 2)))
+    rows = coarse_potential.shape[0] // 2 * (side // 2) // LANES + 1
+    wide = planes // 2 * owners
     message = pl.pallas_call(
         pack_kernel,
-        out_shape=jax.ShapeDtypeStruct((owners, size + 8, LANES), jnp.int32),
-        in_specs=[smem] + [vmem] * 5,
+        out_shape=jax.ShapeDtypeStruct((wide * rows, LANES), jnp.int32),
+        in_specs=[smem] + [vmem] * 3,
         out_specs=vmem,
         scratch_shapes=[pltpu.VMEM((LANES, LANES), jnp.int32)] * 2,
         name="pack",
-    )(plane, coarse_potential, *wish_parts)
-    messages = swap(message, "ray")
+    )(place, coarse_potential, wishes, far_wishes)
+    messages = lax.all_to_all(
+        message.reshape(wide * rows, 1, LANES),
+        ("plane", "ray"),
+        split_axis=0,
+        concat_axis=0,
+        tiled=True,
+        axis_index_groups=[list(range(k * wide, (k + 1) * wide)) for k in range(2)],
+    ).reshape(wide * rows, LANES)
     cell_parts = [coarse_cell] + [hop(coarse_cell, k) for k in range(1, planes)]
-    asked, *cell_parts = lax.optimization_barrier((messages[:, size], *cell_parts))
-
+    messages, *cell_parts = lax.optimization_barrier((messages, *cell_parts))
+    pair_messages = lax.ppermute(messages, "plane", [(i, i ^ 1) for i in range(planes)])
     outgoing = pl.pallas_call(
         take_kernel,
-        out_shape=jax.ShapeDtypeStruct((planes, owners, slots, cells), jnp.bfloat16),
+        out_shape=jax.ShapeDtypeStruct((planes * owners, slots, cells), jnp.bfloat16),
         in_specs=[vmem] * 2,
         out_specs=vmem,
-        scratch_shapes=[pltpu.VMEM((LANES, owners), jnp.int32)],
+        scratch_shapes=[pltpu.VMEM((LANES, wide), jnp.int32)],
         compiler_params=pltpu.CompilerParams(vmem_limit_bytes=32 << 20),
         cost_estimate=pl.CostEstimate(flops=1_100_000_000, bytes_accessed=1_600_000, transcendentals=0),
         name="take",
-    )(asked, fine_tiles[0])
-    arrived = swap(outgoing.reshape(planes * owners, slots, cells), ("plane", "ray"))
+    )(messages, fine_tiles[0])
+    arrived = swap(outgoing, ("plane", "ray"))
 
     codes = 2 * side // WIN * (side // LANES)
     step = min(512, rays)
     found = pl.pallas_call(
         coarse_kernel,
         out_shape=jax.ShapeDtypeStruct((planes, 8, rays), jnp.int32),
-        in_specs=[smem] + [vmem] * 5,
+        in_specs=[smem] + [vmem] * 6,
         out_specs=vmem,
         scratch_shapes=[
             pltpu.VMEM((codes, (TALL + 1) * LANES), jnp.bfloat16),
@@ -364,11 +382,12 @@
             pltpu.VMEM((codes, step), jnp.bfloat16),
             pltpu.VMEM(((TALL + 1) * LANES, step), jnp.float32),
             pltpu.VMEM(((TALL + 1) * LANES, step), jnp.float32),
+            pltpu.VMEM((wide * (rows - 1), LANES), jnp.int32),
         ],
         compiler_params=pltpu.CompilerParams(vmem_limit_bytes=32 << 20),
         cost_estimate=pl.CostEstimate(flops=6_000_000_000, bytes_accessed=1_500_000, transcendentals=0),
         name="coarse",
-    )(plane, messages, *cell_parts)
+    )(place, messages, pair_messages, *cell_parts)
     found_parts = [found[0]] + [hop(found[k], planes - k) for k in range(1, planes)]
 
     return pl.pallas_call(
@@ -387,7 +406,7 @@
         cost_estimate=pl.CostEstimate(flops=1_500_000_000, bytes_accessed=1_500_000, transcendentals=0),
         name="trace",
     )(
-        plane,
+        place,
         arrived.reshape(planes, owners * slots, cells),
         ray_slot,
         fine_cell,

time: 63.6 us -> 63.2 us (level)
  starting transfers between devices: 32.6 us -> 31.9 us
    all_to_all x0 -> x1, starting transfers between devices: none -> 11.7 us  [body(): lax.all_to_all(message.reshape(wide * rows, 1, LANES), ('plane', 'ray'),...]
    all_to_all x2 -> x1, starting transfers between devices: 15.9 us -> 5.28 us  [swap(): return lax.all_to_all(array, axes, split_axis=0, concat_axis=0, tiled=True)]
    all_to_all x2 -> x1, waiting for transfers between devices: 6.63 us -> 0.29 us  [swap(): return lax.all_to_all(array, axes, split_axis=0, concat_axis=0, tiled=True)]
    ppermute x9 -> x7, waiting for transfers between devices: 6.47 us -> 10.6 us  [hop(): lax.ppermute(array, 'plane', [(i, (i + by) % planes) for i in range(plane...]
    ppermute x9 -> x7, starting transfers between devices: 16.7 us -> 13.7 us  [hop(): lax.ppermute(array, 'plane', [(i, (i + by) % planes) for i in range(plane...]
    all_to_all x0 -> x1, waiting for transfers between devices: none -> 2.2 us  [body(): lax.all_to_all(message.reshape(wide * rows, 1, LANES), ('plane', 'ray'),...]
    ppermute x0 -> x1, starting transfers between devices: none -> 1.21 us  [body(): lax.ppermute(messages, 'plane', [(i, i ^ 1) for i in range(planes)])]
  transfers between devices with their start and end apart: 11 -> 10, of which waited for: 6 -> 7; matrix products, arithmetic and copies ran while one was open for 0% -> 0% of each run, Pallas kernels for 15% -> 19%
where the time goes in v6:
time: 63.2 us; the launch traced here: 62.9 us
  starting transfers between devices  31.9 us (50%)
  Pallas kernels  16.5 us (26%)
  waiting for transfers between devices  13.1 us (21%)
  between operations  0.73 us (1%)
  local copies, waits for them, and re-layouts  0.65 us (1%)
    ppermute x7, starting transfers between devices, hop(): lax.ppermute(array, 'plane', [(i, (i + by) % planes) for i in range(plane...  13.7 us
    all_to_all x1, starting transfers between devices, body(): lax.all_to_all(message.reshape(wide * rows, 1, LANES), ('plane', 'ray'),...  11.7 us
    ppermute x7, waiting for transfers between devices, hop(): lax.ppermute(array, 'plane', [(i, (i + by) % planes) for i in range(plane...  10.6 us
    pallas_call x1, Pallas kernels, body(): pl.pallas_call(coarse_kernel, out_shape=jax.ShapeDtypeStruct((planes, 8,...  9.78 us
    all_to_all x1, starting transfers between devices, swap(): return lax.all_to_all(array, axes, split_axis=0, concat_axis=0, tiled=True)  5.28 us
    pallas_call x1, Pallas kernels, body(): pl.pallas_call(trace_kernel, out_shape=(jax.ShapeDtypeStruct((2, rays), j...  2.59 us
    pallas_call x1, Pallas kernels, body(): pl.pallas_call(take_kernel, out_shape=jax.ShapeDtypeStruct((planes * owne...  2.4 us
    all_to_all x1, waiting for transfers between devices, body(): lax.all_to_all(message.reshape(wide * rows, 1, LANES), ('plane', 'ray'),...  2.2 us
  transfers between devices with their start and end apart: 10, of which 7 were waited for; matrix products, arithmetic and copies ran while one was open for 0% of the time, Pallas kernels for 19%

profile of v6, /device:TPU:1, one launch (start us, length us, event | category | flops | bytes accessed | tf_op | source)
XLA Modules:
  0.0 62.9 jit_solution(14451994882032936308)
XLA Ops:
  0.6 3.7 %collective-permute-start = (s32[64,32]{1,0:T(8,128)}, s32[64,32]{1,0:T(8,128)S(1)}, u32[]{:S(2)}, u32[]{:S(2)}) collective-permute-start(s32[64,32]{1,0:T(8,128)} %bitcast.26), channel_id=1, source_target_pairs={{0,64},{32,96},{64,0},{96,32},{1,65},{33,97},{65,1},{97,33},{2,66}... | collective-permute-start | bytes 24584 | tf_op jit(solution)/shard_map/ppermute | solution.py:334
  4.3 1.5 %collective-permute-done.far_ref = s32[64,32]{1,0:T(8,128)S(1)} collective-permute-done((s32[64,32]{1,0:T(8,128)}, s32[64,32]{1,0:T(8,128)S(1)}, u32[]{:S(2)}, u32[]{:S(2)}) %collective-permute-start) | collective-permute-done | bytes 8224 | tf_op jit(solution)/shard_map/ppermute | solution.py:334
  5.8 0.6 copy-done.6
  6.4 1.8 %pack.1 = s32[1088,128]{1,0:T(8,128)} custom-call(s32[1]{0:T(128)} %bitcast.place_ref.plane_ref, f32[16,512]{1,0:T(8,128)} %coarse_ref.1, s32[64,32]{1,0:T(8,128)} %bitcast.27, s32[64,32]{1,0:T(8,128)} %copy-done.6), custom_call_target="tpu_custom_call" | custom-call | tf_op jit(solution)/shard_map/pack/pallas_call | solution.py:340
  8.2 11.7 %all-to-all-start = ((s32[1088,1,128]{2,1,0:T(1,128)}), s32[1088,1,128]{2,1,0:T(1,128)S(1)}, u32[]{:S(2)}, u32[]{:S(2)}) async-start(s32[1088,1,128]{2,1,0:T(1,128)} %bitcast.25), calls=%async_computation | async-start | bytes 1114112 | tf_op jit(solution)/shard_map/all_to_all | solution.py:348
  19.9 0.4 collective-permute-start.3
  20.3 2.5 %collective-permute-start.2 = (s32[4,1024]{1,0:T(4,128)S(1)}, s32[4,1024]{1,0:T(4,128)S(1)}, u32[]{:S(2)}, u32[]{:S(2)}) collective-permute-start(s32[4,1024]{1,0:T(4,128)S(1)} %copy-done.1), channel_id=1, source_target_pairs={{0,64},{32,96},{64,0},{96,32},{1,65},{33,97},{65,1},{97,33},{2,66}... | collective-permute-start | bytes 49160 | tf_op jit(solution)/shard_map/ppermute | solution.py:334
  22.8 3.2 %collective-permute-start.1 = (s32[4,1024]{1,0:T(4,128)S(1)}, s32[4,1024]{1,0:T(4,128)S(1)}, u32[]{:S(2)}, u32[]{:S(2)}) collective-permute-start(s32[4,1024]{1,0:T(4,128)S(1)} %copy-done.1), channel_id=1, source_target_pairs={{0,32},{32,64},{64,96},{96,0},{1,33},{33,65},{65,97},{97,1},{2,34}... | collective-permute-start | bytes 49160 | tf_op jit(solution)/shard_map/ppermute | solution.py:334
  25.9 4.0 %collective-permute-done.3.three_ref = s32[4,1024]{1,0:T(4,128)S(1)} collective-permute-done((s32[4,1024]{1,0:T(4,128)S(1)}, s32[4,1024]{1,0:T(4,128)S(1)}, u32[]{:S(2)}, u32[]{:S(2)}) %collective-permute-start.3) | collective-permute-done | bytes 16416 | tf_op jit(solution)/shard_map/ppermute | solution.py:334
  29.9 2.2 %all-to-all-done = s32[1088,1,128]{2,1,0:T(1,128)S(1)} async-done(((s32[1088,1,128]{2,1,0:T(1,128)}), s32[1088,1,128]{2,1,0:T(1,128)S(1)}, u32[]{:S(2)}, u32[]{:S(2)}) %all-to-all-start) | async-done | bytes 557088 | tf_op jit(solution)/shard_map/all_to_all | solution.py:348
  32.1 1.2 %collective-permute-start.4 = (s32[1088,128]{1,0:T(8,128)S(1)}, s32[1088,128]{1,0:T(8,128)S(1)}, u32[]{:S(2)}, u32[]{:S(2)}) collective-permute-start(s32[1088,128]{1,0:T(8,128)S(1)} %bitcast.21), channel_id=1, source_target_pairs={{0,32},{32,0},{64,96},{96,64},{1,33},{33,1},{65,97},{97,65},{2,34}... | collective-permute-start | bytes 1671176 | tf_op jit(solution)/shard_map/ppermute | solution.py:358
  33.3 2.4 %take.1 = bf16[128,16,256]{2,1,0:T(8,128)(2,1)} custom-call(s32[1088,128]{1,0:T(8,128)S(1)} %bitcast.22, bf16[1024,256]{1,0:T(8,128)(2,1)S(1)} %bitcast.24), custom_call_target="tpu_custom_call" | custom-call | flops 1100000000 | bytes 1600000 | tf_op jit(solution)/shard_map/take/pallas_call | solution.py:359
  35.7 5.3 %all-to-all-start.1 = ((bf16[128,16,256]{2,1,0:T(8,128)(2,1)}), bf16[128,16,256]{2,1,0:T(8,128)(2,1)S(1)}, u32[]{:S(2)}, u32[]{:S(2)}) async-start(bf16[128,16,256]{2,1,0:T(8,128)(2,1)} %take.1), calls=%async_computation.1 | async-start | bytes 2097152 | tf_op jit(solution)/shard_map/all_to_all | solution.py:310
  41.0 9.8 %coarse.1 = s32[4,8,1024]{2,1,0:T(8,128)S(1)} custom-call(s32[1]{0:T(128)} %bitcast.place_ref.plane_ref, s32[1088,128]{1,0:T(8,128)S(1)} %bitcast.23, s32[1088,128]{1,0:T(8,128)S(1)} %collective-permute-done.4.pair_ref, s32[4,1024]{1,0:T(4,128)S(1)} %copy-done.1, s32[4,1024]{1,0:T(4,128)S(1)} %collective-permute-done.1.one_ref, ...), custom_call_target="tpu_custom_call" | custom-call | flops 6000000000 | bytes 1500000 | tf_op jit(solution)/shard_map/coarse/pallas_call | solution.py:373
  50.8 0.0 copy-start.3
  50.8 0.0 copy-start.4
  50.9 0.0 copy-start.5
  50.9 3.2 %collective-permute-start.7 = (s32[8,1024]{1,0:T(8,128)S(1)}, s32[8,1024]{1,0:T(8,128)S(1)}, u32[]{:S(2)}, u32[]{:S(2)}) collective-permute-start(s32[8,1024]{1,0:T(8,128)S(1)} %get-tuple-element.16), channel_id=1, source_target_pairs={{0,32},{32,64},{64,96},{96,0},{1,33},{33,65},{65,97},{97,1},{2,34}... | collective-permute-start | bytes 98312 | tf_op jit(solution)/shard_map/ppermute | solution.py:334
  54.1 0.8 %collective-permute-start.6 = (s32[8,1024]{1,0:T(8,128)S(1)}, s32[8,1024]{1,0:T(8,128)S(1)}, u32[]{:S(2)}, u32[]{:S(2)}) collective-permute-start(s32[8,1024]{1,0:T(8,128)S(1)} %get-tuple-element.17), channel_id=1, source_target_pairs={{0,64},{32,96},{64,0},{96,32},{1,65},{33,97},{65,1},{97,33},{2,66}... | collective-permute-start | bytes 98312 | tf_op jit(solution)/shard_map/ppermute | solution.py:334
  54.9 0.2 collective-permute-done.7.three_ref
  55.1 3.5 %collective-permute-done.6.two_ref = s32[8,1024]{1,0:T(8,128)S(1)} collective-permute-done((s32[8,1024]{1,0:T(8,128)S(1)}, s32[8,1024]{1,0:T(8,128)S(1)}, u32[]{:S(2)}, u32[]{:S(2)}) %collective-permute-start.6) | collective-permute-done | bytes 32800 | tf_op jit(solution)/shard_map/ppermute | solution.py:334
  58.6 1.4 %collective-permute-done.5.one_ref = s32[8,1024]{1,0:T(8,128)S(1)} collective-permute-done((s32[8,1024]{1,0:T(8,128)S(1)}, s32[8,1024]{1,0:T(8,128)S(1)}, u32[]{:S(2)}, u32[]{:S(2)}) %collective-permute-start.5) | collective-permute-done | bytes 32800 | tf_op jit(solution)/shard_map/ppermute | solution.py:334
  60.0 0.3 all-to-all-done.1
  60.3 2.6 %trace.1 = (f32[2,1024]{1,0:T(2,128)}, f32[4,1024]{1,0:T(4,128)}) custom-call(s32[1]{0:T(128)} %bitcast.place_ref.plane_ref, bf16[4,512,256]{2,1,0:T(8,128)(2,1)S(1)} %bitcast.20, s32[4,1024]{1,0:T(4,128)S(1)} %copy-done.2, s32[4,1024]{1,0:T(4,128)S(1)} %copy-done.3, s32[4,1024]{1,0:T(4,128)S(1)} %copy-done.4, s32[8,1024]{1,0:T(8,128)S(1)} %get-tuple-element.19.own_ref, ...), custom_call_target="tpu_custom_call" | custom-call | flops 1500000000 | bytes 1500000 | tf_op jit(solution)/shard_map/trace/pallas_call | solution.py:393
  (15 shorter events, 0.0 us)
Async XLA Ops:
  0.6 5.2 %collective-permute-start = (s32[64,32]{1,0:T(8,128)}, s32[64,32]{1,0:T(8,128)S(1)}, u32[]{:S(2)}, u32[]{:S(2)}) collective-permute-start(s32[64,32]{1,0:T(8,128)} %bitcast.26), channel_id=1, source_target_pairs={{0,64},{32,96},{64,0},{96,32},{1,65},{33,97},{65,1},{97,33},{2,66}... | collective-permute-start | bytes 24584 | tf_op jit(solution)/shard_map/ppermute | solution.py:334
  5.8 0.6 copy-start.6
  8.2 11.7 %copy-start.1 = (s32[4,1024]{1,0:T(4,128)S(1)}, s32[4,1024]{1,0:T(4,128)}, u32[]{:S(2)}) copy-start(s32[4,1024]{1,0:T(4,128)} %own_ref) | copy-start | bytes 49156
  8.2 25.2 %copy-start = (bf16[1,1024,256]{2,1,0:T(8,128)(2,1)S(1)}, bf16[1,1024,256]{2,1,0:T(8,128)(2,1)}, u32[]{:S(2)}) copy-start(bf16[1,1024,256]{2,1,0:T(8,128)(2,1)} %param.9) | copy-start | bytes 1572868
  8.2 23.9 %all-to-all-start = ((s32[1088,1,128]{2,1,0:T(1,128)}), s32[1088,1,128]{2,1,0:T(1,128)S(1)}, u32[]{:S(2)}, u32[]{:S(2)}) async-start(s32[1088,1,128]{2,1,0:T(1,128)} %bitcast.25), calls=%async_computation | async-start | bytes 1114112 | tf_op jit(solution)/shard_map/all_to_all | solution.py:348
  19.9 10.0 %collective-permute-start.3 = (s32[4,1024]{1,0:T(4,128)S(1)}, s32[4,1024]{1,0:T(4,128)S(1)}, u32[]{:S(2)}, u32[]{:S(2)}) collective-permute-start(s32[4,1024]{1,0:T(4,128)S(1)} %copy-done.1), channel_id=1, source_target_pairs={{0,96},{32,0},{64,32},{96,64},{1,97},{33,1},{65,33},{97,65},{2,98}... | collective-permute-start | bytes 49160 | tf_op jit(solution)/shard_map/ppermute | solution.py:334
  20.3 9.6 %collective-permute-start.2 = (s32[4,1024]{1,0:T(4,128)S(1)}, s32[4,1024]{1,0:T(4,128)S(1)}, u32[]{:S(2)}, u32[]{:S(2)}) collective-permute-start(s32[4,1024]{1,0:T(4,128)S(1)} %copy-done.1), channel_id=1, source_target_pairs={{0,64},{32,96},{64,0},{96,32},{1,65},{33,97},{65,1},{97,33},{2,66}... | collective-permute-start | bytes 49160 | tf_op jit(solution)/shard_map/ppermute | solution.py:334
  22.8 7.2 %collective-permute-start.1 = (s32[4,1024]{1,0:T(4,128)S(1)}, s32[4,1024]{1,0:T(4,128)S(1)}, u32[]{:S(2)}, u32[]{:S(2)}) collective-permute-start(s32[4,1024]{1,0:T(4,128)S(1)} %copy-done.1), channel_id=1, source_target_pairs={{0,32},{32,64},{64,96},{96,0},{1,33},{33,65},{65,97},{97,1},{2,34}... | collective-permute-start | bytes 49160 | tf_op jit(solution)/shard_map/ppermute | solution.py:334
  32.1 8.9 %collective-permute-start.4 = (s32[1088,128]{1,0:T(8,128)S(1)}, s32[1088,128]{1,0:T(8,128)S(1)}, u32[]{:S(2)}, u32[]{:S(2)}) collective-permute-start(s32[1088,128]{1,0:T(8,128)S(1)} %bitcast.21), channel_id=1, source_target_pairs={{0,32},{32,0},{64,96},{96,64},{1,33},{33,1},{65,97},{97,65},{2,34}... | collective-permute-start | bytes 1671176 | tf_op jit(solution)/shard_map/ppermute | solution.py:358
  35.7 24.5 %all-to-all-start.1 = ((bf16[128,16,256]{2,1,0:T(8,128)(2,1)}), bf16[128,16,256]{2,1,0:T(8,128)(2,1)S(1)}, u32[]{:S(2)}, u32[]{:S(2)}) async-start(bf16[128,16,256]{2,1,0:T(8,128)(2,1)} %take.1), calls=%async_computation.1 | async-start | bytes 2097152 | tf_op jit(solution)/shard_map/all_to_all | solution.py:310
  50.8 9.5 %copy-start.2 = (s32[4,1024]{1,0:T(4,128)S(1)}, s32[4,1024]{1,0:T(4,128)}, u32[]{:S(2)}) copy-start(s32[4,1024]{1,0:T(4,128)} %slot_ref.1) | copy-start | bytes 49156
  50.8 9.5 %copy-start.3 = (s32[4,1024]{1,0:T(4,128)S(1)}, s32[4,1024]{1,0:T(4,128)}, u32[]{:S(2)}) copy-start(s32[4,1024]{1,0:T(4,128)} %fine_ref.1) | copy-start | bytes 49156
  50.8 9.4 %copy-start.4 = (s32[4,1024]{1,0:T(4,128)S(1)}, s32[4,1024]{1,0:T(4,128)}, u32[]{:S(2)}) copy-start(s32[4,1024]{1,0:T(4,128)} %root_ref.1) | copy-start | bytes 49156
  50.9 9.4 %copy-start.5 = (f32[2,1024]{1,0:T(2,128)S(1)}, f32[2,1024]{1,0:T(2,128)}, u32[]{:S(2)}) copy-start(f32[2,1024]{1,0:T(2,128)} %offset_ref.1) | copy-start | bytes 24580
  50.9 4.2 %collective-permute-start.7 = (s32[8,1024]{1,0:T(8,128)S(1)}, s32[8,1024]{1,0:T(8,128)S(1)}, u32[]{:S(2)}, u32[]{:S(2)}) collective-permute-start(s32[8,1024]{1,0:T(8,128)S(1)} %get-tuple-element.16), channel_id=1, source_target_pairs={{0,32},{32,64},{64,96},{96,0},{1,33},{33,65},{65,97},{97,1},{2,34}... | collective-permute-start | bytes 98312 | tf_op jit(solution)/shard_map/ppermute | solution.py:334
  54.1 4.6 %collective-permute-start.6 = (s32[8,1024]{1,0:T(8,128)S(1)}, s32[8,1024]{1,0:T(8,128)S(1)}, u32[]{:S(2)}, u32[]{:S(2)}) collective-permute-start(s32[8,1024]{1,0:T(8,128)S(1)} %get-tuple-element.17), channel_id=1, source_target_pairs={{0,64},{32,96},{64,0},{96,32},{1,65},{33,97},{65,1},{97,33},{2,66}... | collective-permute-start | bytes 98312 | tf_op jit(solution)/shard_map/ppermute | solution.py:334
  54.9 5.1 %collective-permute-start.5 = (s32[8,1024]{1,0:T(8,128)S(1)}, s32[8,1024]{1,0:T(8,128)S(1)}, u32[]{:S(2)}, u32[]{:S(2)}) collective-permute-start(s32[8,1024]{1,0:T(8,128)S(1)} %get-tuple-element.18), channel_id=1, source_target_pairs={{0,96},{32,0},{64,32},{96,64},{1,97},{33,1},{65,33},{97,65},{2,98}... | collective-permute-start | bytes 98312 | tf_op jit(solution)/shard_map/ppermute | solution.py:334

commit v7 on v5

--- a/solution.py
+++ b/solution.py
@@ -1,3 +1,5 @@
+import math
+
 import jax
 import jax.numpy as jnp
 from jax import lax
@@ -38,7 +40,8 @@
 
 
 def pack_kernel(plane_ref, coarse_ref, own_ref, one_ref, two_ref, three_ref, out_ref, wish_ref, row_ref):
-    owners, rows, _ = out_ref.shape
+    owners = own_ref.shape[1]
+    rows = out_ref.shape[0] // owners
     planes = PLANES
     slots = own_ref.shape[0] // planes
     side = coarse_ref.shape[1]
@@ -58,18 +61,20 @@
             pl.ds(pl.multiple_of(plane * slots, slots), slots), :
         ]
     row_ref[...] = jnp.transpose(wish_ref[...])
-    size = rows - 8
     for owner in range(owners):
-        out_ref[owner, 0:size] = block
-        out_ref[owner, size:rows] = jnp.broadcast_to(row_ref[owner : owner + 1], (8, LANES))
-
-
-def take_kernel(asked_ref, tile_ref, out_ref, turned_ref):
+        at = owner * rows
+        out_ref[at : at + rows - 1] = block
+        out_ref[at + rows - 1 : at + rows] = row_ref[owner : owner + 1]
+
+
+def take_kernel(asked_ref, tile_ref, out_ref, turned_ref, held_ref, sems):
     planes, owners, slots, cells = out_ref.shape
     count = tile_ref.shape[0]
     lot = planes * slots
     group = 4
-    turned_ref[...] = jnp.transpose(asked_ref[...])
+    copies = []
+    rows = asked_ref.shape[0] // owners
+    turned_ref[...] = jnp.transpose(asked_ref[pl.ds(rows - 1, owners, stride=rows), :])
     ids = lax.broadcasted_iota(jnp.int32, (lot, count), 1)
     for first in range(0, owners, group):
         onehot = jnp.concatenate(
@@ -83,23 +88,33 @@
         for r in range(group):
             for p in range(planes):
                 start = r * lot + p * slots
-                out_ref[p, first + r] = got[start : start + slots]
+                held_ref[p, first + r] = got[start : start + slots]
+        for p in range(planes):
+            copies.append(
+                pltpu.make_async_copy(
+                    held_ref.at[p, first : first + group], out_ref.at[p, first : first + group], sems.at[p, first // group]
+                )
+            )
+            copies[-1].start()
+    for copy in copies:
+        copy.wait()
 
 
 def coarse_kernel(
     plane_ref, grid_ref, own_ref, one_ref, two_ref, three_ref, out_ref,
     table_ref, cell_ref, hot_a, hot_b, picked_a, picked_b
 ):
-    owners, rows, _ = grid_ref.shape
     plane = plane_ref[0]
-    side = owners * 2 * WIN
+    side = math.isqrt(table_ref.shape[0] // 2 * WIN * LANES)
+    owners = side // (2 * WIN)
+    rows = grid_ref.shape[0] // owners
     windows = side // WIN
     chunks = side // LANES
     halves = chunks // 2
     width = TALL * LANES
     step = picked_a.shape[1]
     count = windows * chunks
-    grid = grid_ref.reshape(owners * rows, LANES)
+    grid = grid_ref
 
     def load(chunk, dy):
         parts = []
@@ -132,7 +147,7 @@
         put(halo, base, width)
 
     for k, ref in enumerate((own_ref, one_ref, two_ref, three_ref)):
-        cell_ref[k : k + 1] = ref[pl.ds(plane, 1), :]
+        cell_ref[k : k + 1] = ref[...]
 
     bundles = cell_ref.shape[0]
     per = cell_ref.shape[1] // step
@@ -328,26 +343,32 @@
     size = coarse_potential.shape[0] * side // 2 // LANES
     message = pl.pallas_call(
         pack_kernel,
-        out_shape=jax.ShapeDtypeStruct((owners, size + 8, LANES), jnp.int32),
+        out_shape=jax.ShapeDtypeStruct((owners * (size + 1), LANES), jnp.int32),
         in_specs=[smem] + [vmem] * 5,
         out_specs=vmem,
         scratch_shapes=[pltpu.VMEM((LANES, LANES), jnp.int32)] * 2,
         name="pack",
     )(plane, coarse_potential, *wish_parts)
-    messages = swap(message, "ray")
-    cell_parts = [coarse_cell] + [hop(coarse_cell, k) for k in range(1, planes)]
-    asked, *cell_parts = lax.optimization_barrier((messages[:, size], *cell_parts))
+    messages = swap(message.reshape(-1, 1, LANES), "ray").reshape(-1, LANES)
+    at = lax.axis_index("plane")
+    cell_rows = [lax.dynamic_slice(coarse_cell, ((at + k) % planes, 0), (1, rays)) for k in range(planes)]
+    cell_parts = [cell_rows[0]] + [hop(cell_rows[k], k) for k in range(1, planes)]
+    messages, *cell_parts = lax.optimization_barrier((messages, *cell_parts))
 
     outgoing = pl.pallas_call(
         take_kernel,
         out_shape=jax.ShapeDtypeStruct((planes, owners, slots, cells), jnp.bfloat16),
         in_specs=[vmem] * 2,
-        out_specs=vmem,
-        scratch_shapes=[pltpu.VMEM((LANES, owners), jnp.int32)],
+        out_specs=pl.BlockSpec(memory_space=pl.ANY),
+        scratch_shapes=[
+            pltpu.VMEM((LANES, owners), jnp.int32),
+            pltpu.VMEM((planes, owners, slots, cells), jnp.bfloat16),
+            pltpu.SemaphoreType.DMA((planes, owners // 4)),
+        ],
         compiler_params=pltpu.CompilerParams(vmem_limit_bytes=32 << 20),
         cost_estimate=pl.CostEstimate(flops=1_100_000_000, bytes_accessed=1_600_000, transcendentals=0),
         name="take",
-    )(asked, fine_tiles[0])
+    )(messages, fine_tiles[0])
     arrived = swap(outgoing.reshape(planes * owners, slots, cells), ("plane", "ray"))
 
     codes = 2 * side // WIN * (side // LANES)

time: 63.6 us -> 62.6 us (0.984)
  waiting for transfers between devices: 13.1 us -> 11.3 us
  local copies, waits for them, and re-layouts: 0.66 us -> 1.37 us
    all_to_all x2, waiting for transfers between devices: 6.63 us -> 2.05 us  [swap(): return lax.all_to_all(array, axes, split_axis=0, concat_axis=0, tiled=True)]
    ppermute x9, waiting for transfers between devices: 6.47 us -> 9.21 us  [hop(): lax.ppermute(array, 'plane', [(i, (i + by) % planes) for i in range(plane...]
    unnamed x18, local copies, waits for them, and re-layouts: 0.64 us -> 1.34 us
  transfers between devices with their start and end apart: 11 -> 11, of which waited for: 6 -> 7; matrix products, arithmetic and copies ran while one was open for 0% -> 0% of each run, Pallas kernels for 15% -> 15%
where the time goes in v7:
time: 62.6 us; the launch traced here: 62.2 us
  starting transfers between devices  32.8 us (52%)
  Pallas kernels  15.9 us (25%)
  waiting for transfers between devices  11.3 us (18%)
  local copies, waits for them, and re-layouts  1.37 us (2%)
  between operations  0.8 us (1%)
    ppermute x9, starting transfers between devices, hop(): lax.ppermute(array, 'plane', [(i, (i + by) % planes) for i in range(plane...  16.7 us
    all_to_all x2, starting transfers between devices, swap(): return lax.all_to_all(array, axes, split_axis=0, concat_axis=0, tiled=True)  16.1 us
    ppermute x9, waiting for transfers between devices, hop(): lax.ppermute(array, 'plane', [(i, (i + by) % planes) for i in range(plane...  9.21 us
    pallas_call x1, Pallas kernels, body(): pl.pallas_call(coarse_kernel, out_shape=jax.ShapeDtypeStruct((planes, 8,...  9.18 us
    pallas_call x1, Pallas kernels, body(): pl.pallas_call(trace_kernel, out_shape=(jax.ShapeDtypeStruct((2, rays), j...  2.61 us
    pallas_call x1, Pallas kernels, body(): pl.pallas_call(take_kernel, out_shape=jax.ShapeDtypeStruct((planes, owner...  2.43 us
    all_to_all x2, waiting for transfers between devices, swap(): return lax.all_to_all(array, axes, split_axis=0, concat_axis=0, tiled=True)  2.05 us
    pallas_call x1, Pallas kernels, body(): pl.pallas_call(pack_kernel, out_shape=jax.ShapeDtypeStruct((owners * (siz...  1.74 us
  transfers between devices with their start and end apart: 11, of which 7 were waited for; matrix products, arithmetic and copies ran while one was open for 0% of the time, Pallas kernels for 15%

profile of v7, /device:TPU:1, one launch (start us, length us, event | category | flops | bytes accessed | tf_op | source)
XLA Modules:
  0.0 62.2 jit_solution(17841432576480062147)
XLA Ops:
  0.6 1.5 %collective-permute-start.2 = (s32[64,32]{1,0:T(8,128)}, s32[64,32]{1,0:T(8,128)S(1)}, u32[]{:S(2)}, u32[]{:S(2)}) collective-permute-start(s32[64,32]{1,0:T(8,128)} %bitcast.26), channel_id=1, source_target_pairs={{0,96},{32,0},{64,32},{96,64},{1,97},{33,1},{65,33},{97,65},{2,98}... | collective-permute-start | bytes 24584 | tf_op jit(solution)/shard_map/ppermute | solution.py:338
  2.1 2.8 %collective-permute-start.1 = (s32[64,32]{1,0:T(8,128)}, s32[64,32]{1,0:T(8,128)S(1)}, u32[]{:S(2)}, u32[]{:S(2)}) collective-permute-start(s32[64,32]{1,0:T(8,128)} %bitcast.27), channel_id=1, source_target_pairs={{0,64},{32,96},{64,0},{96,32},{1,65},{33,97},{65,1},{97,33},{2,66}... | collective-permute-start | bytes 24584 | tf_op jit(solution)/shard_map/ppermute | solution.py:338
  5.0 2.8 %collective-permute-start = (s32[64,32]{1,0:T(8,128)}, s32[64,32]{1,0:T(8,128)S(1)}, u32[]{:S(2)}, u32[]{:S(2)}) collective-permute-start(s32[64,32]{1,0:T(8,128)} %bitcast.28), channel_id=1, source_target_pairs={{0,32},{32,64},{64,96},{96,0},{1,33},{33,65},{65,97},{97,1},{2,34}... | collective-permute-start | bytes 24584 | tf_op jit(solution)/shard_map/ppermute | solution.py:338
  7.8 1.3 %collective-permute-done.one_ref = s32[64,32]{1,0:T(8,128)S(1)} collective-permute-done((s32[64,32]{1,0:T(8,128)}, s32[64,32]{1,0:T(8,128)S(1)}, u32[]{:S(2)}, u32[]{:S(2)}) %collective-permute-start) | collective-permute-done | bytes 8224 | tf_op jit(solution)/shard_map/ppermute | solution.py:338
  9.2 0.6 copy-done.7
  9.8 1.7 %pack.1 = s32[1056,128]{1,0:T(8,128)} custom-call(s32[1]{0:T(128)} %bitcast.plane_ref, f32[16,512]{1,0:T(8,128)} %coarse_ref.1, s32[64,32]{1,0:T(8,128)} %bitcast.29, s32[64,32]{1,0:T(8,128)} %copy-done.7, s32[64,32]{1,0:T(8,128)} %copy-done.6, s32[64,32]{1,0:T(8,128)} %copy-done.5), custom_call_target="tpu_custom_call" | custom-call | tf_op jit(solution)/shard_map/pack/pallas_call | solution.py:344
  11.5 8.2 %all-to-all-start = ((s32[1056,1,128]{2,1,0:T(1,128)}), s32[1056,1,128]{2,1,0:T(1,128)S(1)}, u32[]{:S(2)}, u32[]{:S(2)}) async-start(s32[1056,1,128]{2,1,0:T(1,128)} %bitcast.25), calls=%async_computation | async-start | bytes 1081344 | tf_op jit(solution)/shard_map/all_to_all | solution.py:314
  19.8 0.7 %copy-done.8 = s32[4,1024]{1,0:T(4,128)S(1)} copy-done((s32[4,1024]{1,0:T(4,128)S(1)}, s32[4,1024]{1,0:T(4,128)}, u32[]{:S(2)}) %copy-start.8) | copy-done | bytes 16408
  20.5 2.3 %collective-permute-start.5 = (s32[1,1024]{1,0:T(1,128)S(1)}, s32[1,1024]{1,0:T(1,128)S(1)}, u32[]{:S(2)}, u32[]{:S(2)}) collective-permute-start(s32[1,1024]{1,0:T(1,128)S(1)} %get-tuple-element.26), channel_id=1, source_target_pairs={{0,96},{32,0},{64,32},{96,64},{1,97},{33,1},{65,33},{97,65},{2,98}... | collective-permute-start | bytes 12296 | tf_op jit(solution)/shard_map/ppermute | solution.py:338
  22.8 2.5 %collective-permute-start.4 = (s32[1,1024]{1,0:T(1,128)S(1)}, s32[1,1024]{1,0:T(1,128)S(1)}, u32[]{:S(2)}, u32[]{:S(2)}) collective-permute-start(s32[1,1024]{1,0:T(1,128)S(1)} %get-tuple-element.27), channel_id=1, source_target_pairs={{0,64},{32,96},{64,0},{96,32},{1,65},{33,97},{65,1},{97,33},{2,66}... | collective-permute-start | bytes 12296 | tf_op jit(solution)/shard_map/ppermute | solution.py:338
  25.3 0.8 %collective-permute-start.3 = (s32[1,1024]{1,0:T(1,128)S(1)}, s32[1,1024]{1,0:T(1,128)S(1)}, u32[]{:S(2)}, u32[]{:S(2)}) collective-permute-start(s32[1,1024]{1,0:T(1,128)S(1)} %get-tuple-element.28), channel_id=1, source_target_pairs={{0,32},{32,64},{64,96},{96,0},{1,33},{33,65},{65,97},{97,1},{2,34}... | collective-permute-start | bytes 12296 | tf_op jit(solution)/shard_map/ppermute | solution.py:338
  26.1 2.7 %collective-permute-done.5.three_ref = s32[1,1024]{1,0:T(1,128)S(1)} collective-permute-done((s32[1,1024]{1,0:T(1,128)S(1)}, s32[1,1024]{1,0:T(1,128)S(1)}, u32[]{:S(2)}, u32[]{:S(2)}) %collective-permute-start.5) | collective-permute-done | bytes 4128 | tf_op jit(solution)/shard_map/ppermute | solution.py:338
  28.8 1.2 %all-to-all-done = s32[1056,1,128]{2,1,0:T(1,128)S(1)} async-done(((s32[1056,1,128]{2,1,0:T(1,128)}), s32[1056,1,128]{2,1,0:T(1,128)S(1)}, u32[]{:S(2)}, u32[]{:S(2)}) %all-to-all-start) | async-done | bytes 540704 | tf_op jit(solution)/shard_map/all_to_all | solution.py:314
  30.0 2.4 %take.1 = bf16[4,32,16,256]{3,2,1,0:T(8,128)(2,1)} custom-call(s32[1056,128]{1,0:T(8,128)S(1)} %bitcast.22, bf16[1024,256]{1,0:T(8,128)(2,1)S(1)} %bitcast.24), custom_call_target="tpu_custom_call" | custom-call | flops 1100000000 | bytes 1600000 | tf_op jit(solution)/shard_map/take/pallas_call | solution.py:358
  32.4 7.9 %all-to-all-start.1 = ((bf16[128,16,256]{2,1,0:T(8,128)(2,1)}), bf16[128,16,256]{2,1,0:T(8,128)(2,1)S(1)}, u32[]{:S(2)}, u32[]{:S(2)}) async-start(bf16[128,16,256]{2,1,0:T(8,128)(2,1)} %bitcast.10), calls=%async_computation.1 | async-start | bytes 2097152 | tf_op jit(solution)/shard_map/all_to_all | solution.py:314
  40.3 9.2 %coarse.1 = s32[4,8,1024]{2,1,0:T(8,128)S(1)} custom-call(s32[1]{0:T(128)} %bitcast.plane_ref, s32[1056,128]{1,0:T(8,128)S(1)} %bitcast.23, s32[1,1024]{1,0:T(1,128)S(1)} %get-tuple-element.18.own_ref, s32[1,1024]{1,0:T(1,128)S(1)} %collective-permute-done.3.one_ref, s32[1,1024]{1,0:T(1,128)S(1)} %collective-permute-done.4.two_ref, ...), custom_call_target="tpu_custom_call" | custom-call | flops 6000000000 | bytes 1500000 | tf_op jit(solution)/shard_map/coarse/pallas_call | solution.py:376
  49.5 0.0 copy-start.3
  49.6 3.2 %collective-permute-start.8 = (s32[8,1024]{1,0:T(8,128)S(1)}, s32[8,1024]{1,0:T(8,128)S(1)}, u32[]{:S(2)}, u32[]{:S(2)}) collective-permute-start(s32[8,1024]{1,0:T(8,128)S(1)} %get-tuple-element.22), channel_id=1, source_target_pairs={{0,32},{32,64},{64,96},{96,0},{1,33},{33,65},{65,97},{97,1},{2,34}... | collective-permute-start | bytes 98312 | tf_op jit(solution)/shard_map/ppermute | solution.py:338
  52.8 0.8 %collective-permute-start.7 = (s32[8,1024]{1,0:T(8,128)S(1)}, s32[8,1024]{1,0:T(8,128)S(1)}, u32[]{:S(2)}, u32[]{:S(2)}) collective-permute-start(s32[8,1024]{1,0:T(8,128)S(1)} %get-tuple-element.23), channel_id=1, source_target_pairs={{0,64},{32,96},{64,0},{96,32},{1,65},{33,97},{65,1},{97,33},{2,66}... | collective-permute-start | bytes 98312 | tf_op jit(solution)/shard_map/ppermute | solution.py:338
  53.6 0.2 collective-permute-done.8.three_ref
  53.8 3.5 %collective-permute-done.7.two_ref = s32[8,1024]{1,0:T(8,128)S(1)} collective-permute-done((s32[8,1024]{1,0:T(8,128)S(1)}, s32[8,1024]{1,0:T(8,128)S(1)}, u32[]{:S(2)}, u32[]{:S(2)}) %collective-permute-start.7) | collective-permute-done | bytes 32800 | tf_op jit(solution)/shard_map/ppermute | solution.py:338
  57.3 1.4 %collective-permute-done.6.one_ref = s32[8,1024]{1,0:T(8,128)S(1)} collective-permute-done((s32[8,1024]{1,0:T(8,128)S(1)}, s32[8,1024]{1,0:T(8,128)S(1)}, u32[]{:S(2)}, u32[]{:S(2)}) %collective-permute-start.6) | collective-permute-done | bytes 32800 | tf_op jit(solution)/shard_map/ppermute | solution.py:338
  58.7 0.9 %all-to-all-done.1 = bf16[128,16,256]{2,1,0:T(8,128)(2,1)S(1)} async-done(((bf16[128,16,256]{2,1,0:T(8,128)(2,1)}), bf16[128,16,256]{2,1,0:T(8,128)(2,1)S(1)}, u32[]{:S(2)}, u32[]{:S(2)}) %all-to-all-start.1) | async-done | bytes 1048608 | tf_op jit(solution)/shard_map/all_to_all | solution.py:314
  59.6 2.6 %trace.1 = (f32[2,1024]{1,0:T(2,128)}, f32[4,1024]{1,0:T(4,128)}) custom-call(s32[1]{0:T(128)} %bitcast.plane_ref, bf16[4,512,256]{2,1,0:T(8,128)(2,1)S(1)} %bitcast.21, s32[4,1024]{1,0:T(4,128)S(1)} %copy-done.1, s32[4,1024]{1,0:T(4,128)S(1)} %copy-done.2, s32[4,1024]{1,0:T(4,128)S(1)} %copy-done.3, s32[8,1024]{1,0:T(8,128)S(1)} %get-tuple-element.25.own_ref, ...), custom_call_target="tpu_custom_call" | custom-call | flops 1500000000 | bytes 1500000 | tf_op jit(solution)/shard_map/trace/pallas_call | solution.py:395
  (22 shorter events, 0.1 us)
Async XLA Ops:
  0.6 7.2 %collective-permute-start.2 = (s32[64,32]{1,0:T(8,128)}, s32[64,32]{1,0:T(8,128)S(1)}, u32[]{:S(2)}, u32[]{:S(2)}) collective-permute-start(s32[64,32]{1,0:T(8,128)} %bitcast.26), channel_id=1, source_target_pairs={{0,96},{32,0},{64,32},{96,64},{1,97},{33,1},{65,33},{97,65},{2,98}... | collective-permute-start | bytes 24584 | tf_op jit(solution)/shard_map/ppermute | solution.py:338
  2.1 5.7 %collective-permute-start.1 = (s32[64,32]{1,0:T(8,128)}, s32[64,32]{1,0:T(8,128)S(1)}, u32[]{:S(2)}, u32[]{:S(2)}) collective-permute-start(s32[64,32]{1,0:T(8,128)} %bitcast.27), channel_id=1, source_target_pairs={{0,64},{32,96},{64,0},{96,32},{1,65},{33,97},{65,1},{97,33},{2,66}... | collective-permute-start | bytes 24584 | tf_op jit(solution)/shard_map/ppermute | solution.py:338
  5.0 4.2 %collective-permute-start = (s32[64,32]{1,0:T(8,128)}, s32[64,32]{1,0:T(8,128)S(1)}, u32[]{:S(2)}, u32[]{:S(2)}) collective-permute-start(s32[64,32]{1,0:T(8,128)} %bitcast.28), channel_id=1, source_target_pairs={{0,32},{32,64},{64,96},{96,0},{1,33},{33,65},{65,97},{97,1},{2,34}... | collective-permute-start | bytes 24584 | tf_op jit(solution)/shard_map/ppermute | solution.py:338
  7.8 1.3 %copy-start.5 = (s32[64,32]{1,0:T(8,128)}, s32[64,32]{1,0:T(8,128)S(1)}, u32[]{:S(2)}) copy-start(s32[64,32]{1,0:T(8,128)S(1)} %collective-permute-done.2.three_ref) | copy-start | bytes 24580
  7.8 1.3 %copy-start.6 = (s32[64,32]{1,0:T(8,128)}, s32[64,32]{1,0:T(8,128)S(1)}, u32[]{:S(2)}) copy-start(s32[64,32]{1,0:T(8,128)S(1)} %collective-permute-done.1.two_ref) | copy-start | bytes 24580
  9.1 0.6 copy-start.7
  11.5 18.5 %copy-start = (bf16[1,1024,256]{2,1,0:T(8,128)(2,1)S(1)}, bf16[1,1024,256]{2,1,0:T(8,128)(2,1)}, u32[]{:S(2)}) copy-start(bf16[1,1024,256]{2,1,0:T(8,128)(2,1)} %param.9) | copy-start | bytes 1572868
  11.5 18.5 %all-to-all-start = ((s32[1056,1,128]{2,1,0:T(1,128)}), s32[1056,1,128]{2,1,0:T(1,128)S(1)}, u32[]{:S(2)}, u32[]{:S(2)}) async-start(s32[1056,1,128]{2,1,0:T(1,128)} %bitcast.25), calls=%async_computation | async-start | bytes 1081344 | tf_op jit(solution)/shard_map/all_to_all | solution.py:314
  19.8 0.7 %copy-start.8 = (s32[4,1024]{1,0:T(4,128)S(1)}, s32[4,1024]{1,0:T(4,128)}, u32[]{:S(2)}) copy-start(s32[4,1024]{1,0:T(4,128)} %param.13) | copy-start | bytes 49156
  20.5 8.3 %collective-permute-start.5 = (s32[1,1024]{1,0:T(1,128)S(1)}, s32[1,1024]{1,0:T(1,128)S(1)}, u32[]{:S(2)}, u32[]{:S(2)}) collective-permute-start(s32[1,1024]{1,0:T(1,128)S(1)} %get-tuple-element.26), channel_id=1, source_target_pairs={{0,96},{32,0},{64,32},{96,64},{1,97},{33,1},{65,33},{97,65},{2,98}... | collective-permute-start | bytes 12296 | tf_op jit(solution)/shard_map/ppermute | solution.py:338
  22.8 6.0 %collective-permute-start.4 = (s32[1,1024]{1,0:T(1,128)S(1)}, s32[1,1024]{1,0:T(1,128)S(1)}, u32[]{:S(2)}, u32[]{:S(2)}) collective-permute-start(s32[1,1024]{1,0:T(1,128)S(1)} %get-tuple-element.27), channel_id=1, source_target_pairs={{0,64},{32,96},{64,0},{96,32},{1,65},{33,97},{65,1},{97,33},{2,66}... | collective-permute-start | bytes 12296 | tf_op jit(solution)/shard_map/ppermute | solution.py:338
  25.3 3.5 %collective-permute-start.3 = (s32[1,1024]{1,0:T(1,128)S(1)}, s32[1,1024]{1,0:T(1,128)S(1)}, u32[]{:S(2)}, u32[]{:S(2)}) collective-permute-start(s32[1,1024]{1,0:T(1,128)S(1)} %get-tuple-element.28), channel_id=1, source_target_pairs={{0,32},{32,64},{64,96},{96,0},{1,33},{33,65},{65,97},{97,1},{2,34}... | collective-permute-start | bytes 12296 | tf_op jit(solution)/shard_map/ppermute | solution.py:338
  32.4 27.2 %all-to-all-start.1 = ((bf16[128,16,256]{2,1,0:T(8,128)(2,1)}), bf16[128,16,256]{2,1,0:T(8,128)(2,1)S(1)}, u32[]{:S(2)}, u32[]{:S(2)}) async-start(bf16[128,16,256]{2,1,0:T(8,128)(2,1)} %bitcast.10), calls=%async_computation.1 | async-start | bytes 2097152 | tf_op jit(solution)/shard_map/all_to_all | solution.py:314
  49.5 10.1 %copy-start.1 = (s32[4,1024]{1,0:T(4,128)S(1)}, s32[4,1024]{1,0:T(4,128)}, u32[]{:S(2)}) copy-start(s32[4,1024]{1,0:T(4,128)} %slot_ref.1) | copy-start | bytes 49156
  49.5 10.1 %copy-start.2 = (s32[4,1024]{1,0:T(4,128)S(1)}, s32[4,1024]{1,0:T(4,128)}, u32[]{:S(2)}) copy-start(s32[4,1024]{1,0:T(4,128)} %fine_ref.1) | copy-start | bytes 49156
  49.5 10.1 %copy-start.3 = (s32[4,1024]{1,0:T(4,128)S(1)}, s32[4,1024]{1,0:T(4,128)}, u32[]{:S(2)}) copy-start(s32[4,1024]{1,0:T(4,128)} %root_ref.1) | copy-start | bytes 49156
  49.6 10.0 %copy-start.4 = (f32[2,1024]{1,0:T(2,128)S(1)}, f32[2,1024]{1,0:T(2,128)}, u32[]{:S(2)}) copy-start(f32[2,1024]{1,0:T(2,128)} %offset_ref.1) | copy-start | bytes 24580
  49.6 4.2 %collective-permute-start.8 = (s32[8,1024]{1,0:T(8,128)S(1)}, s32[8,1024]{1,0:T(8,128)S(1)}, u32[]{:S(2)}, u32[]{:S(2)}) collective-permute-start(s32[8,1024]{1,0:T(8,128)S(1)} %get-tuple-element.22), channel_id=1, source_target_pairs={{0,32},{32,64},{64,96},{96,0},{1,33},{33,65},{65,97},{97,1},{2,34}... | collective-permute-start | bytes 98312 | tf_op jit(solution)/shard_map/ppermute | solution.py:338
  52.8 4.6 %collective-permute-start.7 = (s32[8,1024]{1,0:T(8,128)S(1)}, s32[8,1024]{1,0:T(8,128)S(1)}, u32[]{:S(2)}, u32[]{:S(2)}) collective-permute-start(s32[8,1024]{1,0:T(8,128)S(1)} %get-tuple-element.23), channel_id=1, source_target_pairs={{0,64},{32,96},{64,0},{96,32},{1,65},{33,97},{65,1},{97,33},{2,66}... | collective-permute-start | bytes 98312 | tf_op jit(solution)/shard_map/ppermute | solution.py:338
  53.6 5.1 %collective-permute-start.6 = (s32[8,1024]{1,0:T(8,128)S(1)}, s32[8,1024]{1,0:T(8,128)S(1)}, u32[]{:S(2)}, u32[]{:S(2)}) collective-permute-start(s32[8,1024]{1,0:T(8,128)S(1)} %get-tuple-element.24), channel_id=1, source_target_pairs={{0,96},{32,0},{64,32},{96,64},{1,97},{33,1},{65,33},{97,65},{2,98}... | collective-permute-start | bytes 98312 | tf_op jit(solution)/shard_map/ppermute | solution.py:338

commit v8 on v7

--- a/solution.py
+++ b/solution.py
@@ -39,7 +39,7 @@
     return jnp.where((amount & 1) != 0, pltpu.roll(here, 7, 0), here)
 
 
-def pack_kernel(plane_ref, coarse_ref, own_ref, one_ref, two_ref, three_ref, out_ref, wish_ref, row_ref):
+def pack_kernel(coarse_ref, own_ref, one_ref, two_ref, three_ref, out_ref, wish_ref, row_ref):
     owners = own_ref.shape[1]
     rows = out_ref.shape[0] // owners
     planes = PLANES
@@ -53,7 +53,7 @@
         for x in range(half // LANES):
             tiles.append(word[y * WIN : (y + 1) * WIN, x * LANES : (x + 1) * LANES])
     block = jnp.concatenate(tiles, axis=0)
-    plane = plane_ref[0]
+    plane = lax.axis_index("plane")
     wish_ref[...] = jnp.zeros_like(wish_ref)
     for k, ref in enumerate((own_ref, one_ref, two_ref, three_ref)):
         source = (plane + planes - k) & (planes - 1)
@@ -101,10 +101,10 @@
 
 
 def coarse_kernel(
-    plane_ref, grid_ref, own_ref, one_ref, two_ref, three_ref, out_ref,
+    grid_ref, own_ref, one_ref, two_ref, three_ref, out_ref,
     table_ref, cell_ref, hot_a, hot_b, picked_a, picked_b
 ):
-    plane = plane_ref[0]
+    plane = lax.axis_index("plane")
     side = math.isqrt(table_ref.shape[0] // 2 * WIN * LANES)
     owners = side // (2 * WIN)
     rows = grid_ref.shape[0] // owners
@@ -227,14 +227,14 @@
 
 
 def trace_kernel(
-    plane_ref, tile_ref, slot_ref, fine_ref, root_ref, own_ref, one_ref, two_ref, three_ref, offset_ref,
+    tile_ref, slot_ref, fine_ref, root_ref, own_ref, one_ref, two_ref, three_ref, offset_ref,
     disp_ref, dist_ref, patch_ref, coarse_ref
 ):
     planes = tile_ref.shape[0]
     for k, ref in enumerate((own_ref, one_ref, two_ref, three_ref)):
         words = ref[...]
         half = words.shape[0]
-        from_plane = (plane_ref[0] + k) & (planes - 1)
+        from_plane = (lax.axis_index("plane") + k) & (planes - 1)
         coarse_ref[from_plane, 0:half] = (words >> 16).astype(jnp.float32)
         coarse_ref[from_plane, half : 2 * half] = ((words << 16) >> 16).astype(jnp.float32)
     slots = tile_ref.shape[1]
@@ -246,8 +246,8 @@
         start = pl.multiple_of((index % (rays // step)) * step, step)
         slot = slot_ref[pl.ds(plane, 1), pl.ds(start, step)]
         cell = fine_ref[pl.ds(plane, 1), pl.ds(start, step)]
-        ids = lax.broadcasted_iota(jnp.int32, (slots, step), 0)
-        onehot = (ids == slot).astype(jnp.float32).astype(jnp.bfloat16)
+        ids = lax.broadcasted_iota(jnp.int16, (slots, step), 0)
+        onehot = jnp.where(ids == slot.astype(jnp.int16), jnp.bfloat16(1), jnp.bfloat16(0))
         picked = lax.dot_general(
             tile_ref[plane], onehot, (((0,), (0,)), ((), ())), preferred_element_type=jnp.float32
         )
@@ -331,8 +331,6 @@
     rays = ray_offset.shape[1]
     cells = TP * TP
     vmem = pl.BlockSpec(memory_space=pltpu.VMEM)
-    smem = pl.BlockSpec(memory_space=pltpu.SMEM)
-    plane = jnp.full((1,), lax.axis_index("plane"), jnp.int32)
 
     def hop(array, by):
         return lax.ppermute(array, "plane", [(i, (i + by) % planes) for i in range(planes)])
@@ -344,11 +342,11 @@
     message = pl.pallas_call(
         pack_kernel,
         out_shape=jax.ShapeDtypeStruct((owners * (size + 1), LANES), jnp.int32),
-        in_specs=[smem] + [vmem] * 5,
+        in_specs=[vmem] * 5,
         out_specs=vmem,
         scratch_shapes=[pltpu.VMEM((LANES, LANES), jnp.int32)] * 2,
         name="pack",
-    )(plane, coarse_potential, *wish_parts)
+    )(coarse_potential, *wish_parts)
     messages = swap(message.reshape(-1, 1, LANES), "ray").reshape(-1, LANES)
     at = lax.axis_index("plane")
     cell_rows = [lax.dynamic_slice(coarse_cell, ((at + k) % planes, 0), (1, rays)) for k in range(planes)]
@@ -376,7 +374,7 @@
     found = pl.pallas_call(
         coarse_kernel,
         out_shape=jax.ShapeDtypeStruct((planes, 8, rays), jnp.int32),
-        in_specs=[smem] + [vmem] * 5,
+        in_specs=[vmem] * 5,
         out_specs=vmem,
         scratch_shapes=[
             pltpu.VMEM((codes, (TALL + 1) * LANES), jnp.bfloat16),
@@ -389,7 +387,7 @@
         compiler_params=pltpu.CompilerParams(vmem_limit_bytes=32 << 20),
         cost_estimate=pl.CostEstimate(flops=6_000_000_000, bytes_accessed=1_500_000, transcendentals=0),
         name="coarse",
-    )(plane, messages, *cell_parts)
+    )(messages, *cell_parts)
     found_parts = [found[0]] + [hop(found[k], planes - k) for k in range(1, planes)]
 
     return pl.pallas_call(
@@ -398,7 +396,7 @@
             jax.ShapeDtypeStruct((2, rays), jnp.float32),
             jax.ShapeDtypeStruct((4, rays), jnp.float32),
         ),
-        in_specs=[smem] + [vmem] * 9,
+        in_specs=[vmem] * 9,
         out_specs=(vmem,) * 2,
         scratch_shapes=[
             pltpu.VMEM((planes, 4, 8, rays), jnp.float32),
@@ -408,7 +406,6 @@
         cost_estimate=pl.CostEstimate(flops=1_500_000_000, bytes_accessed=1_500_000, transcendentals=0),
         name="trace",
     )(
-        plane,
         arrived.reshape(planes, owners * slots, cells),
         ray_slot,
         fine_cell,

time: 62.6 us -> 62.3 us (level)
  no operation moved by 1% of the time
where the time goes in v8:
time: 62.3 us; the launch traced here: 61.9 us
  starting transfers between devices  33.2 us (53%)
  Pallas kernels  15.6 us (25%)
  waiting for transfers between devices  10.9 us (17%)
  local copies, waits for them, and re-layouts  1.37 us (2%)
  between operations  0.8 us (1%)
    ppermute x9, starting transfers between devices, hop(): lax.ppermute(array, 'plane', [(i, (i + by) % planes) for i in range(plane...  16.7 us
    all_to_all x2, starting transfers between devices, swap(): return lax.all_to_all(array, axes, split_axis=0, concat_axis=0, tiled=True)  16.4 us
    ppermute x9, waiting for transfers between devices, hop(): lax.ppermute(array, 'plane', [(i, (i + by) % planes) for i in range(plane...  9.2 us
    pallas_call x1, Pallas kernels, body(): pl.pallas_call(coarse_kernel, out_shape=jax.ShapeDtypeStruct((planes, 8,...  9.17 us
    pallas_call x1, Pallas kernels, body(): pl.pallas_call(take_kernel, out_shape=jax.ShapeDtypeStruct((planes, owner...  2.43 us
    pallas_call x1, Pallas kernels, body(): pl.pallas_call(trace_kernel, out_shape=(jax.ShapeDtypeStruct((2, rays), j...  2.27 us
    pallas_call x1, Pallas kernels, body(): pl.pallas_call(pack_kernel, out_shape=jax.ShapeDtypeStruct((owners * (siz...  1.74 us
    all_to_all x2, waiting for transfers between devices, swap(): return lax.all_to_all(array, axes, split_axis=0, concat_axis=0, tiled=True)  1.74 us
  transfers between devices with their start and end apart: 11, of which 7 were waited for; matrix products, arithmetic and copies ran while one was open for 0% of the time, Pallas kernels for 15%

profile of v8, /device:TPU:1, one launch (start us, length us, event | category | flops | bytes accessed | tf_op | source)
XLA Modules:
  0.0 61.9 jit_solution(12730511444484614195)
XLA Ops:
  0.6 1.5 %collective-permute-start.2 = (s32[64,32]{1,0:T(8,128)}, s32[64,32]{1,0:T(8,128)S(1)}, u32[]{:S(2)}, u32[]{:S(2)}) collective-permute-start(s32[64,32]{1,0:T(8,128)} %bitcast.25), channel_id=1, source_target_pairs={{0,96},{32,0},{64,32},{96,64},{1,97},{33,1},{65,33},{97,65},{2,98}... | collective-permute-start | bytes 24584 | tf_op jit(solution)/shard_map/ppermute | solution.py:336
  2.1 2.8 %collective-permute-start.1 = (s32[64,32]{1,0:T(8,128)}, s32[64,32]{1,0:T(8,128)S(1)}, u32[]{:S(2)}, u32[]{:S(2)}) collective-permute-start(s32[64,32]{1,0:T(8,128)} %bitcast.26), channel_id=1, source_target_pairs={{0,64},{32,96},{64,0},{96,32},{1,65},{33,97},{65,1},{97,33},{2,66}... | collective-permute-start | bytes 24584 | tf_op jit(solution)/shard_map/ppermute | solution.py:336
  5.0 2.8 %collective-permute-start = (s32[64,32]{1,0:T(8,128)}, s32[64,32]{1,0:T(8,128)S(1)}, u32[]{:S(2)}, u32[]{:S(2)}) collective-permute-start(s32[64,32]{1,0:T(8,128)} %bitcast.27), channel_id=1, source_target_pairs={{0,32},{32,64},{64,96},{96,0},{1,33},{33,65},{65,97},{97,1},{2,34}... | collective-permute-start | bytes 24584 | tf_op jit(solution)/shard_map/ppermute | solution.py:336
  7.8 1.3 %collective-permute-done.one_ref = s32[64,32]{1,0:T(8,128)S(1)} collective-permute-done((s32[64,32]{1,0:T(8,128)}, s32[64,32]{1,0:T(8,128)S(1)}, u32[]{:S(2)}, u32[]{:S(2)}) %collective-permute-start) | collective-permute-done | bytes 8224 | tf_op jit(solution)/shard_map/ppermute | solution.py:336
  9.2 0.6 copy-done.7
  9.8 1.7 %pack.1 = s32[1056,128]{1,0:T(8,128)} custom-call(f32[16,512]{1,0:T(8,128)} %coarse_ref.1, s32[64,32]{1,0:T(8,128)} %bitcast.28, s32[64,32]{1,0:T(8,128)} %copy-done.7, s32[64,32]{1,0:T(8,128)} %copy-done.6, s32[64,32]{1,0:T(8,128)} %copy-done.5), custom_call_target="tpu_custom_call" | custom-call | tf_op jit(solution)/shard_map/pack/pallas_call | solution.py:342
  11.5 8.2 %all-to-all-start = ((s32[1056,1,128]{2,1,0:T(1,128)}), s32[1056,1,128]{2,1,0:T(1,128)S(1)}, u32[]{:S(2)}, u32[]{:S(2)}) async-start(s32[1056,1,128]{2,1,0:T(1,128)} %bitcast.24), calls=%async_computation | async-start | bytes 1081344 | tf_op jit(solution)/shard_map/all_to_all | solution.py:314
  19.8 0.0 copy-start.8
  19.8 0.7 %copy-done.8 = s32[4,1024]{1,0:T(4,128)S(1)} copy-done((s32[4,1024]{1,0:T(4,128)S(1)}, s32[4,1024]{1,0:T(4,128)}, u32[]{:S(2)}) %copy-start.8) | copy-done | bytes 16408
  20.5 2.3 %collective-permute-start.5 = (s32[1,1024]{1,0:T(1,128)S(1)}, s32[1,1024]{1,0:T(1,128)S(1)}, u32[]{:S(2)}, u32[]{:S(2)}) collective-permute-start(s32[1,1024]{1,0:T(1,128)S(1)} %get-tuple-element.26), channel_id=1, source_target_pairs={{0,96},{32,0},{64,32},{96,64},{1,97},{33,1},{65,33},{97,65},{2,98}... | collective-permute-start | bytes 12296 | tf_op jit(solution)/shard_map/ppermute | solution.py:336
  22.9 2.5 %collective-permute-start.4 = (s32[1,1024]{1,0:T(1,128)S(1)}, s32[1,1024]{1,0:T(1,128)S(1)}, u32[]{:S(2)}, u32[]{:S(2)}) collective-permute-start(s32[1,1024]{1,0:T(1,128)S(1)} %get-tuple-element.27), channel_id=1, source_target_pairs={{0,64},{32,96},{64,0},{96,32},{1,65},{33,97},{65,1},{97,33},{2,66}... | collective-permute-start | bytes 12296 | tf_op jit(solution)/shard_map/ppermute | solution.py:336
  25.3 0.8 %collective-permute-start.3 = (s32[1,1024]{1,0:T(1,128)S(1)}, s32[1,1024]{1,0:T(1,128)S(1)}, u32[]{:S(2)}, u32[]{:S(2)}) collective-permute-start(s32[1,1024]{1,0:T(1,128)S(1)} %get-tuple-element.28), channel_id=1, source_target_pairs={{0,32},{32,64},{64,96},{96,0},{1,33},{33,65},{65,97},{97,1},{2,34}... | collective-permute-start | bytes 12296 | tf_op jit(solution)/shard_map/ppermute | solution.py:336
  26.1 2.7 %collective-permute-done.5.three_ref = s32[1,1024]{1,0:T(1,128)S(1)} collective-permute-done((s32[1,1024]{1,0:T(1,128)S(1)}, s32[1,1024]{1,0:T(1,128)S(1)}, u32[]{:S(2)}, u32[]{:S(2)}) %collective-permute-start.5) | collective-permute-done | bytes 4128 | tf_op jit(solution)/shard_map/ppermute | solution.py:336
  28.8 0.9 %all-to-all-done = s32[1056,1,128]{2,1,0:T(1,128)S(1)} async-done(((s32[1056,1,128]{2,1,0:T(1,128)}), s32[1056,1,128]{2,1,0:T(1,128)S(1)}, u32[]{:S(2)}, u32[]{:S(2)}) %all-to-all-start) | async-done | bytes 540704 | tf_op jit(solution)/shard_map/all_to_all | solution.py:314
  29.7 2.4 %take.1 = bf16[4,32,16,256]{3,2,1,0:T(8,128)(2,1)} custom-call(s32[1056,128]{1,0:T(8,128)S(1)} %bitcast.21, bf16[1024,256]{1,0:T(8,128)(2,1)S(1)} %bitcast.23), custom_call_target="tpu_custom_call" | custom-call | flops 1100000000 | bytes 1600000 | tf_op jit(solution)/shard_map/take/pallas_call | solution.py:356
  32.1 8.2 %all-to-all-start.1 = ((bf16[128,16,256]{2,1,0:T(8,128)(2,1)}), bf16[128,16,256]{2,1,0:T(8,128)(2,1)S(1)}, u32[]{:S(2)}, u32[]{:S(2)}) async-start(bf16[128,16,256]{2,1,0:T(8,128)(2,1)} %bitcast.9), calls=%async_computation.1 | async-start | bytes 2097152 | tf_op jit(solution)/shard_map/all_to_all | solution.py:314
  40.3 9.2 %coarse.1 = s32[4,8,1024]{2,1,0:T(8,128)S(1)} custom-call(s32[1056,128]{1,0:T(8,128)S(1)} %bitcast.22, s32[1,1024]{1,0:T(1,128)S(1)} %get-tuple-element.18.own_ref, s32[1,1024]{1,0:T(1,128)S(1)} %collective-permute-done.3.one_ref, s32[1,1024]{1,0:T(1,128)S(1)} %collective-permute-done.4.two_ref, s32[1,1024]{1,0:T(1,128)S(1)} %collective-permute-done.5.three_ref), custom_call_target="tpu_custom_call" | custom-call | flops 6000000000 | bytes 1500000 | tf_op jit(solution)/shard_map/coarse/pallas_call | solution.py:374
  49.6 3.2 %collective-permute-start.8 = (s32[8,1024]{1,0:T(8,128)S(1)}, s32[8,1024]{1,0:T(8,128)S(1)}, u32[]{:S(2)}, u32[]{:S(2)}) collective-permute-start(s32[8,1024]{1,0:T(8,128)S(1)} %get-tuple-element.22), channel_id=1, source_target_pairs={{0,32},{32,64},{64,96},{96,0},{1,33},{33,65},{65,97},{97,1},{2,34}... | collective-permute-start | bytes 98312 | tf_op jit(solution)/shard_map/ppermute | solution.py:336
  52.8 0.8 %collective-permute-start.7 = (s32[8,1024]{1,0:T(8,128)S(1)}, s32[8,1024]{1,0:T(8,128)S(1)}, u32[]{:S(2)}, u32[]{:S(2)}) collective-permute-start(s32[8,1024]{1,0:T(8,128)S(1)} %get-tuple-element.23), channel_id=1, source_target_pairs={{0,64},{32,96},{64,0},{96,32},{1,65},{33,97},{65,1},{97,33},{2,66}... | collective-permute-start | bytes 98312 | tf_op jit(solution)/shard_map/ppermute | solution.py:336
  53.6 0.2 collective-permute-done.8.three_ref
  53.8 3.5 %collective-permute-done.7.two_ref = s32[8,1024]{1,0:T(8,128)S(1)} collective-permute-done((s32[8,1024]{1,0:T(8,128)S(1)}, s32[8,1024]{1,0:T(8,128)S(1)}, u32[]{:S(2)}, u32[]{:S(2)}) %collective-permute-start.7) | collective-permute-done | bytes 32800 | tf_op jit(solution)/shard_map/ppermute | solution.py:336
  57.4 1.4 %collective-permute-done.6.one_ref = s32[8,1024]{1,0:T(8,128)S(1)} collective-permute-done((s32[8,1024]{1,0:T(8,128)S(1)}, s32[8,1024]{1,0:T(8,128)S(1)}, u32[]{:S(2)}, u32[]{:S(2)}) %collective-permute-start.6) | collective-permute-done | bytes 32800 | tf_op jit(solution)/shard_map/ppermute | solution.py:336
  58.7 0.9 %all-to-all-done.1 = bf16[128,16,256]{2,1,0:T(8,128)(2,1)S(1)} async-done(((bf16[128,16,256]{2,1,0:T(8,128)(2,1)}), bf16[128,16,256]{2,1,0:T(8,128)(2,1)S(1)}, u32[]{:S(2)}, u32[]{:S(2)}) %all-to-all-start.1) | async-done | bytes 1048608 | tf_op jit(solution)/shard_map/all_to_all | solution.py:314
  59.6 2.3 %trace.1 = (f32[2,1024]{1,0:T(2,128)}, f32[4,1024]{1,0:T(4,128)}) custom-call(bf16[4,512,256]{2,1,0:T(8,128)(2,1)S(1)} %bitcast.20, s32[4,1024]{1,0:T(4,128)S(1)} %copy-done.1, s32[4,1024]{1,0:T(4,128)S(1)} %copy-done.2, s32[4,1024]{1,0:T(4,128)S(1)} %copy-done.3, s32[8,1024]{1,0:T(8,128)S(1)} %get-tuple-element.25.own_ref, ...), custom_call_target="tpu_custom_call" | custom-call | flops 1500000000 | bytes 1500000 | tf_op jit(solution)/shard_map/trace/pallas_call | solution.py:393
  (22 shorter events, 0.1 us)
Async XLA Ops:
  0.6 7.2 %collective-permute-start.2 = (s32[64,32]{1,0:T(8,128)}, s32[64,32]{1,0:T(8,128)S(1)}, u32[]{:S(2)}, u32[]{:S(2)}) collective-permute-start(s32[64,32]{1,0:T(8,128)} %bitcast.25), channel_id=1, source_target_pairs={{0,96},{32,0},{64,32},{96,64},{1,97},{33,1},{65,33},{97,65},{2,98}... | collective-permute-start | bytes 24584 | tf_op jit(solution)/shard_map/ppermute | solution.py:336
  2.1 5.7 %collective-permute-start.1 = (s32[64,32]{1,0:T(8,128)}, s32[64,32]{1,0:T(8,128)S(1)}, u32[]{:S(2)}, u32[]{:S(2)}) collective-permute-start(s32[64,32]{1,0:T(8,128)} %bitcast.26), channel_id=1, source_target_pairs={{0,64},{32,96},{64,0},{96,32},{1,65},{33,97},{65,1},{97,33},{2,66}... | collective-permute-start | bytes 24584 | tf_op jit(solution)/shard_map/ppermute | solution.py:336
  5.0 4.2 %collective-permute-start = (s32[64,32]{1,0:T(8,128)}, s32[64,32]{1,0:T(8,128)S(1)}, u32[]{:S(2)}, u32[]{:S(2)}) collective-permute-start(s32[64,32]{1,0:T(8,128)} %bitcast.27), channel_id=1, source_target_pairs={{0,32},{32,64},{64,96},{96,0},{1,33},{33,65},{65,97},{97,1},{2,34}... | collective-permute-start | bytes 24584 | tf_op jit(solution)/shard_map/ppermute | solution.py:336
  7.8 1.3 %copy-start.5 = (s32[64,32]{1,0:T(8,128)}, s32[64,32]{1,0:T(8,128)S(1)}, u32[]{:S(2)}) copy-start(s32[64,32]{1,0:T(8,128)S(1)} %collective-permute-done.2.three_ref) | copy-start | bytes 24580
  7.8 1.3 %copy-start.6 = (s32[64,32]{1,0:T(8,128)}, s32[64,32]{1,0:T(8,128)S(1)}, u32[]{:S(2)}) copy-start(s32[64,32]{1,0:T(8,128)S(1)} %collective-permute-done.1.two_ref) | copy-start | bytes 24580
  9.1 0.6 copy-start.7
  11.5 18.2 %copy-start = (bf16[1,1024,256]{2,1,0:T(8,128)(2,1)S(1)}, bf16[1,1024,256]{2,1,0:T(8,128)(2,1)}, u32[]{:S(2)}) copy-start(bf16[1,1024,256]{2,1,0:T(8,128)(2,1)} %param.9) | copy-start | bytes 1572868
  11.5 18.2 %all-to-all-start = ((s32[1056,1,128]{2,1,0:T(1,128)}), s32[1056,1,128]{2,1,0:T(1,128)S(1)}, u32[]{:S(2)}, u32[]{:S(2)}) async-start(s32[1056,1,128]{2,1,0:T(1,128)} %bitcast.24), calls=%async_computation | async-start | bytes 1081344 | tf_op jit(solution)/shard_map/all_to_all | solution.py:314
  19.8 0.7 %copy-start.8 = (s32[4,1024]{1,0:T(4,128)S(1)}, s32[4,1024]{1,0:T(4,128)}, u32[]{:S(2)}) copy-start(s32[4,1024]{1,0:T(4,128)} %param.13) | copy-start | bytes 49156
  20.5 8.3 %collective-permute-start.5 = (s32[1,1024]{1,0:T(1,128)S(1)}, s32[1,1024]{1,0:T(1,128)S(1)}, u32[]{:S(2)}, u32[]{:S(2)}) collective-permute-start(s32[1,1024]{1,0:T(1,128)S(1)} %get-tuple-element.26), channel_id=1, source_target_pairs={{0,96},{32,0},{64,32},{96,64},{1,97},{33,1},{65,33},{97,65},{2,98}... | collective-permute-start | bytes 12296 | tf_op jit(solution)/shard_map/ppermute | solution.py:336
  22.9 6.0 %collective-permute-start.4 = (s32[1,1024]{1,0:T(1,128)S(1)}, s32[1,1024]{1,0:T(1,128)S(1)}, u32[]{:S(2)}, u32[]{:S(2)}) collective-permute-start(s32[1,1024]{1,0:T(1,128)S(1)} %get-tuple-element.27), channel_id=1, source_target_pairs={{0,64},{32,96},{64,0},{96,32},{1,65},{33,97},{65,1},{97,33},{2,66}... | collective-permute-start | bytes 12296 | tf_op jit(solution)/shard_map/ppermute | solution.py:336
  25.3 3.5 %collective-permute-start.3 = (s32[1,1024]{1,0:T(1,128)S(1)}, s32[1,1024]{1,0:T(1,128)S(1)}, u32[]{:S(2)}, u32[]{:S(2)}) collective-permute-start(s32[1,1024]{1,0:T(1,128)S(1)} %get-tuple-element.28), channel_id=1, source_target_pairs={{0,32},{32,64},{64,96},{96,0},{1,33},{33,65},{65,97},{97,1},{2,34}... | collective-permute-start | bytes 12296 | tf_op jit(solution)/shard_map/ppermute | solution.py:336
  32.1 27.5 %all-to-all-start.1 = ((bf16[128,16,256]{2,1,0:T(8,128)(2,1)}), bf16[128,16,256]{2,1,0:T(8,128)(2,1)S(1)}, u32[]{:S(2)}, u32[]{:S(2)}) async-start(bf16[128,16,256]{2,1,0:T(8,128)(2,1)} %bitcast.9), calls=%async_computation.1 | async-start | bytes 2097152 | tf_op jit(solution)/shard_map/all_to_all | solution.py:314
  49.5 10.1 %copy-start.1 = (s32[4,1024]{1,0:T(4,128)S(1)}, s32[4,1024]{1,0:T(4,128)}, u32[]{:S(2)}) copy-start(s32[4,1024]{1,0:T(4,128)} %slot_ref.1) | copy-start | bytes 49156
  49.5 10.1 %copy-start.2 = (s32[4,1024]{1,0:T(4,128)S(1)}, s32[4,1024]{1,0:T(4,128)}, u32[]{:S(2)}) copy-start(s32[4,1024]{1,0:T(4,128)} %fine_ref.1) | copy-start | bytes 49156
  49.5 10.1 %copy-start.3 = (s32[4,1024]{1,0:T(4,128)S(1)}, s32[4,1024]{1,0:T(4,128)}, u32[]{:S(2)}) copy-start(s32[4,1024]{1,0:T(4,128)} %root_ref.1) | copy-start | bytes 49156
  49.6 10.0 %copy-start.4 = (f32[2,1024]{1,0:T(2,128)S(1)}, f32[2,1024]{1,0:T(2,128)}, u32[]{:S(2)}) copy-start(f32[2,1024]{1,0:T(2,128)} %offset_ref.1) | copy-start | bytes 24580
  49.6 4.2 %collective-permute-start.8 = (s32[8,1024]{1,0:T(8,128)S(1)}, s32[8,1024]{1,0:T(8,128)S(1)}, u32[]{:S(2)}, u32[]{:S(2)}) collective-permute-start(s32[8,1024]{1,0:T(8,128)S(1)} %get-tuple-element.22), channel_id=1, source_target_pairs={{0,32},{32,64},{64,96},{96,0},{1,33},{33,65},{65,97},{97,1},{2,34}... | collective-permute-start | bytes 98312 | tf_op jit(solution)/shard_map/ppermute | solution.py:336
  52.8 4.6 %collective-permute-start.7 = (s32[8,1024]{1,0:T(8,128)S(1)}, s32[8,1024]{1,0:T(8,128)S(1)}, u32[]{:S(2)}, u32[]{:S(2)}) collective-permute-start(s32[8,1024]{1,0:T(8,128)S(1)} %get-tuple-element.23), channel_id=1, source_target_pairs={{0,64},{32,96},{64,0},{96,32},{1,65},{33,97},{65,1},{97,33},{2,66}... | collective-permute-start | bytes 98312 | tf_op jit(solution)/shard_map/ppermute | solution.py:336
  53.6 5.1 %collective-permute-start.6 = (s32[8,1024]{1,0:T(8,128)S(1)}, s32[8,1024]{1,0:T(8,128)S(1)}, u32[]{:S(2)}, u32[]{:S(2)}) collective-permute-start(s32[8,1024]{1,0:T(8,128)S(1)} %get-tuple-element.24), channel_id=1, source_target_pairs={{0,96},{32,0},{64,32},{96,64},{1,97},{33,1},{65,33},{97,65},{2,98}... | collective-permute-start | bytes 98312 | tf_op jit(solution)/shard_map/ppermute | solution.py:336
